TPU v7x, 32 devices: a whole 2x2x4 slice. The times are simulated.
32 devices in a mesh: fsdp: 4 (over z), ctx: 2 (over x), tp: 4 (over y, core).
Axes of the slice: x: 2, y: 2, z: 4, core: 2. Of those that a mesh axis runs over, the one named last changes fastest.
Arguments:
- layer_in: bfloat16 [8, 1024, 1024], P('fsdp', ('ctx', 'tp')), may hold values from -6 to 6
- attn_gain: bfloat16 [1024], replicated, may hold values from 0.5 to 1.5
- ffn_gain: bfloat16 [1024], replicated, may hold values from 0.5 to 1.5
- query_weight: bfloat16 [1024, 1024], P(('fsdp', 'ctx'), 'tp'), may hold values from -0.1875 to 0.1875
- key_weight: bfloat16 [1024, 1024], P(('fsdp', 'ctx'), 'tp'), may hold values from -0.1875 to 0.1875
- value_weight: bfloat16 [1024, 1024], P(('fsdp', 'ctx'), 'tp'), may hold values from -0.1875 to 0.1875
- out_weight: bfloat16 [1024, 1024], P(('fsdp', 'ctx'), 'tp'), may hold values from -0.75 to 0.75
- variate_bias: float32 [2, 16], P(None, 'tp'), may hold values from -4 to 4
- gate_weight: bfloat16 [1024, 4096], P(('fsdp', 'ctx'), 'tp'), may hold values from -0.1875 to 0.1875
- up_weight: bfloat16 [1024, 4096], P(('fsdp', 'ctx'), 'tp'), may hold values from -0.1875 to 0.1875
- down_weight: bfloat16 [1024, 4096], P(('fsdp', 'ctx'), 'tp'), may hold values from -0.09375 to 0.09375
- segment_ids: int32 [8, 1024], P('fsdp'), may hold values from 0 to 15, never falling along the last dimension, each value on 1 to 512 neighbouring positions
- variate_ids: int32 [8, 1024], P('fsdp'), may hold values from 0 to 3
- time_ids: int32 [8, 1024], P('fsdp'), may hold values from 0 to 1023
- out_grad: bfloat16 [8, 1024, 1024], P('fsdp', ('ctx', 'tp')), may hold values from -6 to 6
Outputs:
- layer_out: bfloat16 [8, 1024, 1024], P('fsdp', ('ctx', 'tp'))
- in_grad: bfloat16 [8, 1024, 1024], P('fsdp', ('ctx', 'tp'))
- attn_gain_grad: float32 [1024], replicated
- ffn_gain_grad: float32 [1024], replicated
- query_grad: float32 [1024, 1024], P(('fsdp', 'ctx'), 'tp')
- key_grad: float32 [1024, 1024], P(('fsdp', 'ctx'), 'tp')
- value_grad: float32 [1024, 1024], P(('fsdp', 'ctx'), 'tp')
- out_weight_grad: float32 [1024, 1024], P(('fsdp', 'ctx'), 'tp')
- bias_grad: float32 [2, 16], P(None, 'tp')
- gate_grad: float32 [1024, 4096], P(('fsdp', 'ctx'), 'tp')
- up_grad: float32 [1024, 4096], P(('fsdp', 'ctx'), 'tp')
- down_grad: float32 [1024, 4096], P(('fsdp', 'ctx'), 'tp')
All inputs are finite; a program needn't handle non-finite values.
Results may differ from a plain program's by a relative error of at most 0.019.
Values may be sent and summed in bfloat16 or wider, within the bound.
No kernel may reach another device: no remote copies, remote signals or barrier semaphores. Data moves between devices by JAX's collectives and lax.ppermute only.
A program may use at most 128 MiB of HBM per device.

v0:
```python
import jax
import jax.numpy as jnp
from jax import lax
from jax.sharding import PartitionSpec as P

HEADS = 16
HEAD = 64


EPS = 1e-05
NEG = -1e30


def rms_norm(values, gain):
    return values * lax.rsqrt(jnp.mean(values * values, axis=-1, keepdims=True) + EPS) * gain


def rotate(values, time_rows):
    half_dim = values.shape[-1] // 2
    frequency = 10000.0 ** (-2.0 * jnp.arange(half_dim, dtype=jnp.float32) / values.shape[-1])
    angles = time_rows.astype(jnp.float32)[..., None, None] * frequency
    cosine = jnp.cos(angles)
    sine_part = jnp.sin(angles)
    first_half = values[..., :half_dim]
    second = values[..., half_dim:]
    return jnp.concatenate(
        [first_half * cosine - second * sine_part, second * cosine + first_half * sine_part],
        axis=-1,
    )


def swiglu(gate_vals, up_vals):
    return jax.nn.silu(gate_vals) * up_vals


def gather_rows(values):
    return lax.all_gather(values, "tp", axis=1, tiled=True)


def scatter_rows(values):
    return lax.psum_scatter(values, "tp", scatter_dimension=1, tiled=True)


def shards(
    layer_in,
    attn_gain,
    ffn_gain,
    query_weight,
    key_weight,
    value_weight,
    out_weight,
    variate_bias,
    gate_weight,
    up_weight,
    down_weight,
    segment_ids,
    variate_ids,
    time_ids,
    out_grad,
):
    seq_count, share, width = layer_in.shape
    span = share * lax.axis_size("tp")
    seq_length = segment_ids.shape[1]
    offset = lax.axis_index("ctx") * span
    local_heads = variate_bias.shape[1]
    proj_width = local_heads * HEAD
    row_count = seq_count * span
    block = 512
    block_starts = jnp.arange(span // block, dtype=jnp.int32) * block
    scale = HEAD ** (-0.5)
    my_times = lax.dynamic_slice_in_dim(time_ids, offset, span, 1)
    my_variates = lax.dynamic_slice_in_dim(variate_ids, offset, span, 1)
    my_segments = lax.dynamic_slice_in_dim(segment_ids, offset, span, 1)
    bias_same = variate_bias[0]
    bias_diff = variate_bias[1]
    gain_one = attn_gain.astype(jnp.float32)
    gain_two = ffn_gain.astype(jnp.float32)
    inputs = layer_in.astype(jnp.float32)
    rows_one = gather_rows(rms_norm(inputs, gain_one).astype(jnp.bfloat16)).reshape(
        row_count, width
    )
    query_full, key_full, value_full, out_full = (
        lax.all_gather(query_weight, ("fsdp", "ctx"), axis=0, tiled=True),
        lax.all_gather(key_weight, ("fsdp", "ctx"), axis=0, tiled=True),
        lax.all_gather(value_weight, ("fsdp", "ctx"), axis=0, tiled=True),
        lax.all_gather(out_weight, ("fsdp", "ctx"), axis=0, tiled=True),
    )
    queries_raw = jnp.dot(rows_one, query_full, preferred_element_type=jnp.float32).reshape(
        seq_count, span, local_heads, HEAD
    )
    keys_raw = jnp.dot(rows_one, key_full, preferred_element_type=jnp.float32).reshape(
        seq_count, span, local_heads, HEAD
    )
    queries = rotate(queries_raw, my_times).astype(jnp.bfloat16)
    keys_mine = rotate(keys_raw, my_times).astype(jnp.bfloat16).reshape(seq_count, span, proj_width)
    values_mine = (
        jnp.dot(rows_one, value_full, preferred_element_type=jnp.float32)
        .astype(jnp.bfloat16)
        .reshape(seq_count, span, proj_width)
    )
    keys_all, values_all = (
        lax.all_gather(keys_mine, "ctx", axis=1, tiled=True),
        lax.all_gather(values_mine, "ctx", axis=1, tiled=True),
    )

    def scores_of(query_block, key_rows, query_var, key_var, query_seg, key_seg):
        raw = (
            jnp.einsum("qhd,khd->hqk", query_block, key_rows, preferred_element_type=jnp.float32)
            * scale
        )
        same = (query_var[:, None] == key_var[None, :])[None]
        raw = raw + jnp.where(same, bias_same[:, None, None], bias_diff[:, None, None])
        return (jnp.where((query_seg[:, None] == key_seg[None, :])[None], raw, NEG), same)

    mixed_parts = []
    lse_parts = []
    for seq in range(seq_count):
        key_rows = keys_all[seq].reshape(seq_length, local_heads, HEAD)
        value_rows = values_all[seq].reshape(seq_length, local_heads, HEAD)

        def forward_block(first, seq=seq, key_rows=key_rows, value_rows=value_rows):
            query_block = queries[seq]
            query_var = my_variates[seq]
            query_seg = my_segments[seq]
            scores, same = scores_of(
                query_block, key_rows, query_var, variate_ids[seq], query_seg, segment_ids[seq]
            )
            top = jnp.max(scores, axis=-1, keepdims=True)
            expo = jnp.exp(scores - top)
            total = jnp.sum(expo, axis=-1, keepdims=True)
            probs = (expo / total).astype(jnp.bfloat16)
            mixed_block = jnp.einsum(
                "hqk,khd->qhd", probs, value_rows, preferred_element_type=jnp.float32
            )
            return (
                mixed_block.astype(jnp.bfloat16).reshape(block, proj_width),
                top[..., 0] + jnp.log(total[..., 0]),
            )

        mixed_seq, lse_seq = lax.map(forward_block, block_starts)
        mixed_parts.append(mixed_seq.reshape(span, proj_width))
        lse_parts.append(lse_seq)
    mixed = jnp.stack(mixed_parts).reshape(row_count, proj_width)
    attn_part = jnp.einsum("rp,dp->rd", mixed, out_full, preferred_element_type=jnp.float32)
    hidden = inputs + scatter_rows(attn_part.reshape(seq_count, span, width))
    rows_two = gather_rows(rms_norm(hidden, gain_two).astype(jnp.bfloat16)).reshape(
        row_count, width
    )
    gate_full, up_full, down_full = (
        lax.all_gather(gate_weight, ("fsdp", "ctx"), axis=0, tiled=True),
        lax.all_gather(up_weight, ("fsdp", "ctx"), axis=0, tiled=True),
        lax.all_gather(down_weight, ("fsdp", "ctx"), axis=0, tiled=True),
    )
    gate = jnp.dot(rows_two, gate_full, preferred_element_type=jnp.float32)
    up_vals = jnp.dot(rows_two, up_full, preferred_element_type=jnp.float32)
    act = swiglu(gate, up_vals).astype(jnp.bfloat16)
    ffn_part = jnp.einsum("rf,df->rd", act, down_full, preferred_element_type=jnp.float32)
    layer_out = (hidden + scatter_rows(ffn_part.reshape(seq_count, span, width))).astype(
        jnp.bfloat16
    )
    query_back, key_back, value_back, out_back = (
        lax.all_gather(query_weight, ("fsdp", "ctx"), axis=0, tiled=True),
        lax.all_gather(key_weight, ("fsdp", "ctx"), axis=0, tiled=True),
        lax.all_gather(value_weight, ("fsdp", "ctx"), axis=0, tiled=True),
        lax.all_gather(out_weight, ("fsdp", "ctx"), axis=0, tiled=True),
    )
    gate_back, up_back, down_back = (
        lax.all_gather(gate_weight, ("fsdp", "ctx"), axis=0, tiled=True),
        lax.all_gather(up_weight, ("fsdp", "ctx"), axis=0, tiled=True),
        lax.all_gather(down_weight, ("fsdp", "ctx"), axis=0, tiled=True),
    )
    grad_rows = gather_rows(out_grad).reshape(row_count, width)
    d_act = jnp.dot(grad_rows, down_back, preferred_element_type=jnp.float32)
    down_local = jnp.einsum("rd,rf->df", grad_rows, act, preferred_element_type=jnp.float32)
    swiglu_pull = jax.vjp(swiglu, gate, up_vals)[1]
    d_gate, d_up = swiglu_pull(d_act)
    d_gate = d_gate.astype(jnp.bfloat16)
    d_up = d_up.astype(jnp.bfloat16)
    gate_local = jnp.einsum("rd,rf->df", rows_two, d_gate, preferred_element_type=jnp.float32)
    up_local = jnp.einsum("rd,rf->df", rows_two, d_up, preferred_element_type=jnp.float32)
    d_normed_two = jnp.einsum("rf,df->rd", d_gate, gate_back, preferred_element_type=jnp.float32)
    d_normed_two = d_normed_two + jnp.einsum(
        "rf,df->rd", d_up, up_back, preferred_element_type=jnp.float32
    )
    norm_two_pull = jax.vjp(rms_norm, hidden, gain_two)[1]
    d_hidden_norm, d_gain_two = norm_two_pull(
        scatter_rows(d_normed_two.reshape(seq_count, span, width))
    )
    d_hidden = out_grad.astype(jnp.float32) + d_hidden_norm
    branch_rows = gather_rows(d_hidden.astype(jnp.bfloat16)).reshape(row_count, width)
    out_local = jnp.einsum("rd,rp->dp", branch_rows, mixed, preferred_element_type=jnp.float32)
    d_mixed = jnp.dot(branch_rows, out_back, preferred_element_type=jnp.float32).astype(
        jnp.bfloat16
    )
    d_mixed = d_mixed.reshape(seq_count, span, local_heads, HEAD)
    d_query_parts = []
    d_key_parts = []
    d_value_parts = []
    d_bias = jnp.zeros((2, local_heads), jnp.float32)
    for seq in range(seq_count):
        key_rows = keys_all[seq].reshape(seq_length, local_heads, HEAD)
        value_rows = values_all[seq].reshape(seq_length, local_heads, HEAD)

        def back_block(carry, item, seq=seq, key_rows=key_rows, value_rows=value_rows):
            d_keys, d_values, bias_sum = carry
            first, lse_block = item
            query_block = queries[seq]
            query_var = my_variates[seq]
            query_seg = my_segments[seq]
            scores, same = scores_of(
                query_block, key_rows, query_var, variate_ids[seq], query_seg, segment_ids[seq]
            )
            probs = jnp.exp(scores - lse_block[:, :, None])
            probs_low = probs.astype(jnp.bfloat16)
            d_out = d_mixed[seq]
            d_probs = jnp.einsum(
                "qhd,khd->hqk", d_out, value_rows, preferred_element_type=jnp.float32
            )
            delta = jnp.sum(probs * d_probs, axis=-1, keepdims=True)
            d_scores = (probs * (d_probs - delta)).astype(jnp.bfloat16)
            d_query = (
                jnp.einsum("hqk,khd->qhd", d_scores, key_rows, preferred_element_type=jnp.float32)
                * scale
            )
            d_keys = (
                d_keys
                + jnp.einsum(
                    "hqk,qhd->khd", d_scores, query_block, preferred_element_type=jnp.float32
                )
                * scale
            )
            d_values = d_values + jnp.einsum(
                "hqk,qhd->khd", probs_low, d_out, preferred_element_type=jnp.float32
            )
            wide_scores = d_scores.astype(jnp.float32)
            same_sum = jnp.sum(jnp.where(same, wide_scores, 0.0), axis=(1, 2))
            diff_sum = jnp.sum(jnp.where(same, 0.0, wide_scores), axis=(1, 2))
            return ((d_keys, d_values, bias_sum + jnp.stack([same_sum, diff_sum])), d_query)

        zero_rows = jnp.zeros((seq_length, local_heads, HEAD), jnp.float32)
        (d_keys, d_values, bias_sum), d_query_blocks = lax.scan(
            back_block,
            (zero_rows, zero_rows, jnp.zeros((2, local_heads), jnp.float32)),
            (block_starts, lse_parts[seq]),
        )
        d_query_parts.append(d_query_blocks.reshape(span, local_heads, HEAD))
        d_key_parts.append(d_keys.reshape(seq_length, proj_width))
        d_value_parts.append(d_values.reshape(seq_length, proj_width))
        d_bias = d_bias + bias_sum
    d_keys_mine, d_values_mine = (
        lax.psum_scatter(
            jnp.stack(d_key_parts).astype(jnp.bfloat16), "ctx", scatter_dimension=1, tiled=True
        ).astype(jnp.float32),
        lax.psum_scatter(
            jnp.stack(d_value_parts).astype(jnp.bfloat16), "ctx", scatter_dimension=1, tiled=True
        ).astype(jnp.float32),
    )

    def rope_local(values):
        return rotate(values, my_times)

    rope_pull = jax.vjp(rope_local, queries_raw)[1]
    d_query_raw = (
        rope_pull(jnp.stack(d_query_parts))[0].astype(jnp.bfloat16).reshape(row_count, proj_width)
    )
    d_key_raw = (
        rope_pull(d_keys_mine.reshape(seq_count, span, local_heads, HEAD))[0]
        .astype(jnp.bfloat16)
        .reshape(row_count, proj_width)
    )
    d_value_low = d_values_mine.astype(jnp.bfloat16).reshape(row_count, proj_width)
    query_local = jnp.einsum("rd,rp->dp", rows_one, d_query_raw, preferred_element_type=jnp.float32)
    key_local = jnp.einsum("rd,rp->dp", rows_one, d_key_raw, preferred_element_type=jnp.float32)
    value_local = jnp.einsum("rd,rp->dp", rows_one, d_value_low, preferred_element_type=jnp.float32)
    d_normed_one = jnp.einsum(
        "rp,dp->rd", d_query_raw, query_back, preferred_element_type=jnp.float32
    )
    d_normed_one = d_normed_one + jnp.einsum(
        "rp,dp->rd", d_key_raw, key_back, preferred_element_type=jnp.float32
    )
    d_normed_one = d_normed_one + jnp.einsum(
        "rp,dp->rd", d_value_low, value_back, preferred_element_type=jnp.float32
    )
    norm_one_pull = jax.vjp(rms_norm, inputs, gain_one)[1]
    d_input_norm, d_gain_one = norm_one_pull(
        scatter_rows(d_normed_one.reshape(seq_count, span, width))
    )
    in_grad = (d_hidden + d_input_norm).astype(jnp.bfloat16)
    query_grad, key_grad, value_grad, out_weight_grad = (
        lax.psum_scatter(
            query_local.astype(jnp.bfloat16), ("fsdp", "ctx"), scatter_dimension=0, tiled=True
        ).astype(jnp.float32),
        lax.psum_scatter(
            key_local.astype(jnp.bfloat16), ("fsdp", "ctx"), scatter_dimension=0, tiled=True
        ).astype(jnp.float32),
        lax.psum_scatter(
            value_local.astype(jnp.bfloat16), ("fsdp", "ctx"), scatter_dimension=0, tiled=True
        ).astype(jnp.float32),
        lax.psum_scatter(
            out_local.astype(jnp.bfloat16), ("fsdp", "ctx"), scatter_dimension=0, tiled=True
        ).astype(jnp.float32),
    )
    gate_grad, up_grad, down_grad = (
        lax.psum_scatter(
            gate_local.astype(jnp.bfloat16), ("fsdp", "ctx"), scatter_dimension=0, tiled=True
        ).astype(jnp.float32),
        lax.psum_scatter(
            up_local.astype(jnp.bfloat16), ("fsdp", "ctx"), scatter_dimension=0, tiled=True
        ).astype(jnp.float32),
        lax.psum_scatter(
            down_local.astype(jnp.bfloat16), ("fsdp", "ctx"), scatter_dimension=0, tiled=True
        ).astype(jnp.float32),
    )
    head_offset = lax.axis_index("tp") * local_heads
    bias_full = lax.dynamic_update_slice_in_dim(
        jnp.zeros((2, HEADS), jnp.float32), d_bias, head_offset, 1
    )
    attn_gain_grad, ffn_gain_grad, bias_total = lax.psum(
        (d_gain_one, d_gain_two, bias_full), ("fsdp", "ctx", "tp")
    )
    bias_grad = lax.dynamic_slice_in_dim(bias_total, head_offset, local_heads, 1)
    return (
        layer_out,
        in_grad,
        attn_gain_grad,
        ffn_gain_grad,
        query_grad,
        key_grad,
        value_grad,
        out_weight_grad,
        bias_grad,
        gate_grad,
        up_grad,
        down_grad,
    )


def solution(mesh):
    in_specs = (
        P("fsdp", ("ctx", "tp"), None),
        P(),
        P(),
        P(("fsdp", "ctx"), "tp"),
        P(("fsdp", "ctx"), "tp"),
        P(("fsdp", "ctx"), "tp"),
        P(("fsdp", "ctx"), "tp"),
        P(None, "tp"),
        P(("fsdp", "ctx"), "tp"),
        P(("fsdp", "ctx"), "tp"),
        P(("fsdp", "ctx"), "tp"),
        P("fsdp", None),
        P("fsdp", None),
        P("fsdp", None),
        P("fsdp", ("ctx", "tp"), None),
    )
    out_specs = (
        P("fsdp", ("ctx", "tp"), None),
        P("fsdp", ("ctx", "tp"), None),
        P(),
        P(),
        P(("fsdp", "ctx"), "tp"),
        P(("fsdp", "ctx"), "tp"),
        P(("fsdp", "ctx"), "tp"),
        P(("fsdp", "ctx"), "tp"),
        P(None, "tp"),
        P(("fsdp", "ctx"), "tp"),
        P(("fsdp", "ctx"), "tp"),
        P(("fsdp", "ctx"), "tp"),
    )
    return jax.shard_map(shards, mesh=mesh, in_specs=in_specs, out_specs=out_specs, check_vma=False)
```

profile of v0, /device:TPU:0, one launch (start us, length us, event | category | flops | bytes accessed | tf_op | source)
XLA Modules:
  0.0 1151.3 jit_solution(9747962312075755871)
XLA Ops:
  15.6 33.3 %all_gather.49 = bf16[1024,256]{1,0:T(8,128)(2,1)S(1)} all-gather(bf16[128,256]{1,0:T(8,128)(2,1)} %param.18), channel_id=1, replica_groups=mesh['fsdp'=4,'ctx'=2,'tp'=4] {'fsdp','ctx'}, dimensions={0}, use_global_device_ids=true | all-gather | bytes 589824 | tf_op jit(solution)/shard_map/all_gather | solution.py:83
  48.9 31.6 %all_gather.50 = bf16[1024,256]{1,0:T(8,128)(2,1)S(1)} all-gather(bf16[128,256]{1,0:T(8,128)(2,1)} %param.19), channel_id=1, replica_groups=mesh['fsdp'=4,'ctx'=2,'tp'=4] {'fsdp','ctx'}, dimensions={0}, use_global_device_ids=true | all-gather | bytes 589824 | tf_op jit(solution)/shard_map/all_gather | solution.py:84
  80.5 31.9 %all_gather.47 = bf16[1024,256]{1,0:T(8,128)(2,1)S(1)} all-gather(bf16[128,256]{1,0:T(8,128)(2,1)} %param.20), channel_id=1, replica_groups=mesh['fsdp'=4,'ctx'=2,'tp'=4] {'fsdp','ctx'}, dimensions={0}, use_global_device_ids=true | all-gather | bytes 589824 | tf_op jit(solution)/shard_map/all_gather | solution.py:85
  112.3 31.6 %all_gather.52 = bf16[1024,256]{1,0:T(8,128)(2,1)S(1)} all-gather(bf16[128,256]{1,0:T(8,128)(2,1)} %param.21), channel_id=1, replica_groups=mesh['fsdp'=4,'ctx'=2,'tp'=4] {'fsdp','ctx'}, dimensions={0}, use_global_device_ids=true | all-gather | bytes 589824 | tf_op jit(solution)/shard_map/all_gather | solution.py:86
  144.9 3.3 convolution_convert_fusion.5
  156.3 14.2 %all-gather.12.cloned.1.call-done = bf16[2,1024,256]{2,1,0:T(8,128)(2,1)} async-done(((bf16[2,512,256]{2,1,0:T(8,128)(2,1)}), bf16[2,1024,256]{2,1,0:T(8,128)(2,1)}) %all-gather.12.cloned.1.call-update) | async-done | bytes 1048592 | tf_op jit(solution)/shard_map/all_gather | solution.py:103
  176.9 17.1 %all-gather.14.cloned.1.call-done = bf16[2,1024,256]{1,2,0:T(8,128)(2,1)} async-done(((bf16[2,512,256]{1,2,0:T(8,128)(2,1)}), bf16[2,1024,256]{1,2,0:T(8,128)(2,1)}) %all-gather.14.cloned.1.call-update) | async-done | bytes 1048592 | tf_op jit(solution)/shard_map/all_gather | solution.py:102
  196.1 4.1 fusion.69
  203.5 2.8 fusion.38
  207.4 4.2 fusion.70
  221.1 43.6 %reduce-scatter.16.cloned.1.call-done = f32[2,128,1024]{2,1,0:T(8,128)} async-done(((f32[2,512,1024]{2,1,0:T(8,128)}), f32[2,128,1024]{2,1,0:T(8,128)}) %reduce-scatter.16.cloned.1.call-update) | async-done | bytes 1048592 | tf_op jit(solution)/shard_map/reduce_scatter | solution.py:41
  269.3 2.9 all-gather.20.cloned.1.call-done
  272.2 23.0 %all-gather.16.cloned.1.call-done = bf16[2,512,1024]{2,1,0:T(8,128)(2,1)} async-done(((bf16[2,128,1024]{2,1,0:T(8,128)(2,1)}), bf16[2,512,1024]{2,1,0:T(8,128)(2,1)}) %all-gather.16.cloned.1.call-update) | async-done | bytes 2097168 | tf_op jit(solution)/shard_map/all_gather | solution.py:37
  295.3 6.6 fusion.72
  301.8 45.0 %all-gather.18.cloned.1.call-done = bf16[1024,1024]{1,0:T(8,128)(2,1)} async-done(((bf16[128,1024]{1,0:T(8,128)(2,1)}), bf16[1024,1024]{1,0:T(8,128)(2,1)}) %all-gather.18.cloned.1.call-update) | async-done | bytes 2097168 | tf_op jit(solution)/shard_map/all_gather | solution.py:150
  346.9 6.5 fusion.71
  353.4 16.1 %all-gather.24.cloned.1.call-done = bf16[2,512,1024]{2,1,0:T(8,128)(2,1)} async-done(((bf16[2,128,1024]{2,1,0:T(8,128)(2,1)}), bf16[2,512,1024]{2,1,0:T(8,128)(2,1)}) %all-gather.24.cloned.1.call-update) | async-done | bytes 2097168 | tf_op jit(solution)/shard_map/all_gather | solution.py:37
  369.5 51.7 %all-gather.22.cloned.1.call-done = bf16[1024,1024]{1,0:T(8,128)(2,1)} async-done(((bf16[128,1024]{1,0:T(8,128)(2,1)}), bf16[1024,1024]{1,0:T(8,128)(2,1)}) %all-gather.22.cloned.1.call-update) | async-done | bytes 2097168 | tf_op jit(solution)/shard_map/all_gather | solution.py:152
  421.2 9.9 multiply_convert_fusion.2
  434.2 4.4 convolution_add_fusion
  438.7 43.1 %reduce-scatter.20.cloned.1.call-done = f32[2,128,1024]{2,1,0:T(8,128)} async-done(((f32[2,512,1024]{2,1,0:T(8,128)}), f32[2,128,1024]{2,1,0:T(8,128)}) %reduce-scatter.20.cloned.1.call-update) | async-done | bytes 1048592 | tf_op jit(solution)/shard_map/reduce_scatter | solution.py:41
  486.5 22.2 %all-gather.26.cloned.1.call-done = bf16[2,512,1024]{2,1,0:T(8,128)(2,1)} async-done(((bf16[2,128,1024]{2,1,0:T(8,128)(2,1)}), bf16[2,512,1024]{2,1,0:T(8,128)(2,1)}) %all-gather.26.cloned.1.call-update) | async-done | bytes 2097168 | tf_op jit(solution)/shard_map/all_gather | solution.py:37
  511.2 5.8 fusion.24
  517.1 7.2 multiply_reduce_fusion.1
  533.1 8.7 fusion
  545.9 4.8 fusion.2
  554.9 6.0 convert_bitcast_fusion
  560.8 4.1 copy.67
  565.0 5.9 convolution_convert_fusion
  571.0 5.9 convolution_convert_fusion.1
  577.0 3.1 fusion.33
  580.2 4.5 fusion.36
  584.8 3.2 fusion.32
  588.3 4.5 fusion.37
  594.1 2.8 multiply_add_fusion.1
  602.8 3.2 convolution_convert_fusion.3
  611.5 6.7 fusion.73
  618.3 29.3 %reduce-scatter.40.cloned.1.call-done = bf16[128,1024]{1,0:T(8,128)(2,1)} async-done(((bf16[1024,1024]{1,0:T(8,128)(2,1)}), bf16[128,1024]{1,0:T(8,128)(2,1)}) %reduce-scatter.40.cloned.1.call-update) | async-done | bytes 262160
  649.6 68.4 %reduce-scatter.38.cloned.1.call-done = bf16[128,1024]{1,0:T(8,128)(2,1)} async-done(((bf16[1024,1024]{1,0:T(8,128)(2,1)}), bf16[128,1024]{1,0:T(8,128)(2,1)}) %reduce-scatter.38.cloned.1.call-update) | async-done | bytes 262160 | tf_op jit(solution)/shard_map/reduce_scatter | solution.py:307
  719.8 68.3 %reduce-scatter.36.cloned.1.call-done = bf16[128,1024]{1,0:T(8,128)(2,1)} async-done(((bf16[1024,1024]{1,0:T(8,128)(2,1)}), bf16[128,1024]{1,0:T(8,128)(2,1)}) %reduce-scatter.36.cloned.1.call-update) | async-done | bytes 262160 | tf_op jit(solution)/shard_map/reduce_scatter | solution.py:304
  790.1 62.4 %reduce-scatter.34.cloned.1.call-done = bf16[128,256]{1,0:T(8,128)(2,1)} async-done(((bf16[1024,256]{1,0:T(8,128)(2,1)}), bf16[128,256]{1,0:T(8,128)(2,1)}) %reduce-scatter.34.cloned.1.call-update) | async-done | bytes 65552 | tf_op jit(solution)/shard_map/reduce_scatter | solution.py:299
  854.0 63.0 %reduce-scatter.32.cloned.1.call-done = bf16[128,256]{1,0:T(8,128)(2,1)} async-done(((bf16[1024,256]{1,0:T(8,128)(2,1)}), bf16[128,256]{1,0:T(8,128)(2,1)}) %reduce-scatter.32.cloned.1.call-update) | async-done | bytes 65552 | tf_op jit(solution)/shard_map/reduce_scatter | solution.py:296
  918.5 63.3 %reduce-scatter.30.cloned.1.call-done = bf16[128,256]{1,0:T(8,128)(2,1)} async-done(((bf16[1024,256]{1,0:T(8,128)(2,1)}), bf16[128,256]{1,0:T(8,128)(2,1)}) %reduce-scatter.30.cloned.1.call-update) | async-done | bytes 65552 | tf_op jit(solution)/shard_map/reduce_scatter | solution.py:293
  983.4 63.6 %reduce-scatter.28.cloned.1.call-done = bf16[128,256]{1,0:T(8,128)(2,1)} async-done(((bf16[1024,256]{1,0:T(8,128)(2,1)}), bf16[128,256]{1,0:T(8,128)(2,1)}) %reduce-scatter.28.cloned.1.call-update) | async-done | bytes 65552 | tf_op jit(solution)/shard_map/reduce_scatter | solution.py:290
  1048.4 44.4 %reduce-scatter.26.cloned.1.call-done = f32[2,128,1024]{2,1,0:T(8,128)} async-done(((f32[2,512,1024]{2,1,0:T(8,128)}), f32[2,128,1024]{2,1,0:T(8,128)}) %reduce-scatter.26.cloned.1.call-update) | async-done | bytes 1048592 | tf_op jit(solution)/shard_map/reduce_scatter | solution.py:41
  1094.4 39.8 %all-reduce.4 = (f32[1024]{0:T(1024)}, f32[1024]{0:T(1024)}, f32[2,16]{1,0:T(2,128)S(1)}) all-reduce(f32[1024]{0:T(1024)S(1)} %get-tuple-element.206, f32[1024]{0:T(1024)S(1)} %copy-done.44, f32[2,16]{1,0:T(2,128)S(1)} %dynamic_update_slice.18), channel_id=1, replica_groups=mesh['fsdp'=4,'ctx'=2,'tp'=4] {'fsdp','ctx','tp'}, use_global_device_ids=true, to_apply=%region_17.18 | all-reduce | flops 2080 | bytes 16640 | tf_op jit(solution)/shard_map/psum | solution.py:318
  1134.9 5.8 reduce-scatter.18.cloned.1.call-done
  1140.7 3.0 fusion.44
  (259 shorter events, 97.3 us)
Async XLA Ops:
  8.0 136.9 %all-gather.10.cloned.1.call-start = ((), (), s32[]{:S(2)}) async-start(), calls=%async_computation.13 | async-start | bytes 2621440 | tf_op jit(solution)/shard_map/all_gather | solution.py:37
  13.2 157.4 %all-gather.12.cloned.1.call-start = ((), (), s32[]{:S(2)}) async-start(), calls=%async_computation.14 | async-start | bytes 1572864 | tf_op jit(solution)/shard_map/all_gather | solution.py:103
  80.5 67.8 %copy-start.43 = (s32[2,1024]{1,0:T(2,128)S(1)}, s32[2,1024]{1,0:T(2,128)}, u32[]{:S(2)}) copy-start(s32[2,1024]{1,0:T(2,128)} %param.26) | copy-start | bytes 24580
  112.3 36.2 %copy-start.23 = (bf16[1024,256]{1,0:T(8,128)(2,1)}, bf16[1024,256]{1,0:T(8,128)(2,1)S(1)}, u32[]{:S(2)}) copy-start(bf16[1024,256]{1,0:T(8,128)(2,1)S(1)} %all_gather.47) | copy-start | bytes 1572868
  144.0 73.3 %copy-start.13 = (bf16[1024,256]{1,0:T(8,128)(2,1)}, bf16[1024,256]{1,0:T(8,128)(2,1)S(1)}, u32[]{:S(2)}) copy-start(bf16[1024,256]{1,0:T(8,128)(2,1)S(1)} %all_gather.52) | copy-start | bytes 1572868
  144.9 51.2 %copy-start.11 = (pred[512,1024]{1,0:T(8,128)(4,1)}, pred[512,1024]{1,0:T(8,128)(4,1)S(1)}, u32[]{:S(2)}) copy-start(pred[512,1024]{1,0:T(8,128)(4,1)S(1)} %broadcast_compare_fusion) | copy-start | bytes 1572868
  148.2 45.8 %all-gather.14.cloned.1.call-start = ((), (), s32[]{:S(2)}) async-start(), calls=%async_computation.15 | async-start | bytes 1572864 | tf_op jit(solution)/shard_map/all_gather | solution.py:102
  152.4 55.0 %copy-start.7 = (bf16[2,512,4,32]{1,3,2,0:T(8,128)(2,1)}, bf16[2,512,4,32]{1,3,2,0:T(8,128)(2,1)S(1)}, u32[]{:S(2)}) copy-start(bf16[2,512,4,32]{1,3,2,0:T(8,128)(2,1)S(1)} %get-tuple-element.238) | copy-start | bytes 786436
  152.4 55.0 %copy-start.9 = (bf16[2,512,4,32]{1,3,2,0:T(8,128)(2,1)}, bf16[2,512,4,32]{1,3,2,0:T(8,128)(2,1)S(1)}, u32[]{:S(2)}) copy-start(bf16[2,512,4,32]{1,3,2,0:T(8,128)(2,1)S(1)} %get-tuple-element.239) | copy-start | bytes 786436
  153.4 111.4 %reduce-scatter.16.cloned.1.call-start = ((), (), s32[]{:S(2)}) async-start(), calls=%async_computation.16 | async-start | bytes 5242880 | tf_op jit(solution)/shard_map/reduce_scatter | solution.py:41
  153.6 46.5 %copy-start.55 = (f32[4]{0:T(128)}, f32[4]{0:T(128)S(1)}, u32[]{:S(2)}) copy-start(f32[4]{0:T(128)S(1)} %get-tuple-element.264) | copy-start | bytes 52
  153.6 46.5 %copy-start.56 = (f32[4]{0:T(128)}, f32[4]{0:T(128)S(1)}, u32[]{:S(2)}) copy-start(f32[4]{0:T(128)S(1)} %get-tuple-element.265) | copy-start | bytes 52
  154.0 53.4 %copy-start.14 = (pred[512,1024]{1,0:T(8,128)(4,1)}, pred[512,1024]{1,0:T(8,128)(4,1)S(1)}, u32[]{:S(2)}) copy-start(pred[512,1024]{1,0:T(8,128)(4,1)S(1)} %broadcast_compare_fusion.2) | copy-start | bytes 1572868
  217.3 47.5 %copy-start.4 = (bf16[2,128,1024]{2,1,0:T(8,128)(2,1)S(1)}, bf16[2,128,1024]{2,1,0:T(8,128)(2,1)}, u32[]{:S(2)}) copy-start(bf16[2,128,1024]{2,1,0:T(8,128)(2,1)} %param.15) | copy-start | bytes 1572868
  220.0 52.2 %all-gather.20.cloned.1.call-start = ((), (), s32[]{:S(2)}) async-start(), calls=%async_computation.19 | async-start | bytes 2359296 | tf_op jit(solution)/shard_map/all_gather | solution.py:151
  220.6 74.7 %all-gather.16.cloned.1.call-start = ((), (), s32[]{:S(2)}) async-start(), calls=%async_computation.17 | async-start | bytes 2621440 | tf_op jit(solution)/shard_map/all_gather | solution.py:37
  221.1 262.7 %copy-start.31 = (f32[1024]{0:T(1024)}, f32[1024]{0:T(1024)S(1)}, u32[]{:S(2)}) copy-start(f32[1024]{0:T(1024)S(1)} %convert_element_type.167) | copy-start | bytes 12292
  266.2 217.6 %copy-start.41 = (f32[2,128]{1,0:T(2,128)}, f32[2,128]{1,0:T(2,128)S(1)}, u32[]{:S(2)}) copy-start(f32[2,128]{1,0:T(2,128)S(1)} %fusion.57) | copy-start | bytes 3076
  267.2 79.7 %all-gather.18.cloned.1.call-start = ((), (), s32[]{:S(2)}) async-start(), calls=%async_computation.18 | async-start | bytes 2359296 | tf_op jit(solution)/shard_map/all_gather | solution.py:150
  267.8 101.7 %all-gather.24.cloned.1.call-start = ((), (), s32[]{:S(2)}) async-start(), calls=%async_computation.22 | async-start | bytes 2621440 | tf_op jit(solution)/shard_map/all_gather | solution.py:37
  268.5 152.7 %all-gather.22.cloned.1.call-start = ((), (), s32[]{:S(2)}) async-start(), calls=%async_computation.20 | async-start | bytes 2359296 | tf_op jit(solution)/shard_map/all_gather | solution.py:152
  269.3 212.5 %reduce-scatter.20.cloned.1.call-start = ((), (), s32[]{:S(2)}) async-start(), calls=%async_computation.23 | async-start | bytes 5242880 | tf_op jit(solution)/shard_map/reduce_scatter | solution.py:41
  438.6 45.3 %copy-start.6 = (bf16[2,128,1024]{2,1,0:T(8,128)(2,1)S(1)}, bf16[2,128,1024]{2,1,0:T(8,128)(2,1)}, u32[]{:S(2)}) copy-start(bf16[2,128,1024]{2,1,0:T(8,128)(2,1)} %param.29) | copy-start | bytes 1572868
  438.6 47.9 %copy-start.36 = (f32[4,512]{1,0:T(4,128)S(1)}, f32[4,512]{1,0:T(4,128)}, u32[]{:S(2)}) copy-start(f32[4,512]{1,0:T(4,128)} %copy-done.35) | copy-start | bytes 24580
  438.6 47.9 %copy-start.38 = (f32[4,512]{1,0:T(4,128)S(1)}, f32[4,512]{1,0:T(4,128)}, u32[]{:S(2)}) copy-start(f32[4,512]{1,0:T(4,128)} %copy-done.37) | copy-start | bytes 24580
  438.6 47.9 %copy-start.40 = (f32[4,512]{1,0:T(4,128)S(1)}, f32[4,512]{1,0:T(4,128)}, u32[]{:S(2)}) copy-start(f32[4,512]{1,0:T(4,128)} %copy-done.39) | copy-start | bytes 24580
  438.6 70.1 %all-gather.26.cloned.1.call-start = ((), (), s32[]{:S(2)}) async-start(), calls=%async_computation.24 | async-start | bytes 2621440 | tf_op jit(solution)/shard_map/all_gather | solution.py:37
  486.2 98.6 %reduce-scatter.24.cloned.1.call-start = ((), (), s32[]{:S(2)}) async-start(), calls=%async_computation.26 | async-start | bytes 1572864 | tf_op jit(solution)/shard_map/reduce_scatter | solution.py:254
  533.0 59.9 %reduce-scatter.22.cloned.1.call-start = ((), (), s32[]{:S(2)}) async-start(), calls=%async_computation.25 | async-start | bytes 1572864 | tf_op jit(solution)/shard_map/reduce_scatter | solution.py:251
  554.6 93.0 %reduce-scatter.40.cloned.1.call-start = ((), (), s32[]{:S(2)}) async-start(), calls=%async_computation.34 | async-start | bytes 2359296
  564.9 153.1 %reduce-scatter.38.cloned.1.call-start = ((), (), s32[]{:S(2)}) async-start(), calls=%async_computation.33 | async-start | bytes 2359296 | tf_op jit(solution)/shard_map/reduce_scatter | solution.py:307
  570.9 217.2 %reduce-scatter.36.cloned.1.call-start = ((), (), s32[]{:S(2)}) async-start(), calls=%async_computation.32 | async-start | bytes 2359296 | tf_op jit(solution)/shard_map/reduce_scatter | solution.py:304
  576.9 275.5 %reduce-scatter.34.cloned.1.call-start = ((), (), s32[]{:S(2)}) async-start(), calls=%async_computation.31 | async-start | bytes 589824 | tf_op jit(solution)/shard_map/reduce_scatter | solution.py:299
  580.2 336.8 %reduce-scatter.32.cloned.1.call-start = ((), (), s32[]{:S(2)}) async-start(), calls=%async_computation.30 | async-start | bytes 589824 | tf_op jit(solution)/shard_map/reduce_scatter | solution.py:296
  588.0 393.8 %reduce-scatter.30.cloned.1.call-start = ((), (), s32[]{:S(2)}) async-start(), calls=%async_computation.29 | async-start | bytes 589824 | tf_op jit(solution)/shard_map/reduce_scatter | solution.py:293
  600.0 447.0 %reduce-scatter.28.cloned.1.call-start = ((), (), s32[]{:S(2)}) async-start(), calls=%async_computation.28 | async-start | bytes 589824 | tf_op jit(solution)/shard_map/reduce_scatter | solution.py:290
  605.9 486.9 %reduce-scatter.26.cloned.1.call-start = ((), (), s32[]{:S(2)}) async-start(), calls=%async_computation.27 | async-start | bytes 5242880 | tf_op jit(solution)/shard_map/reduce_scatter | solution.py:41
  611.5 529.1 %reduce-scatter.18.cloned.1.call-start = ((), (), s32[]{:S(2)}) async-start(), calls=%async_computation.21 | async-start | bytes 5242880 | tf_op jit(solution)/shard_map/reduce_scatter | solution.py:41
  618.2 171.7 %copy-start.51 = (f32[4]{0:T(128)S(1)}, f32[4]{0:T(128)}, u32[]{:S(2)}) copy-start(f32[4]{0:T(128)} %get-tuple-element.202) | copy-start | bytes 52
  618.2 171.7 %copy-start.52 = (f32[4]{0:T(128)S(1)}, f32[4]{0:T(128)}, u32[]{:S(2)}) copy-start(f32[4]{0:T(128)} %get-tuple-element.203) | copy-start | bytes 52
  618.2 474.6 %copy-start.34 = (f32[1024]{0:T(1024)S(1)}, f32[1024]{0:T(1024)}, u32[]{:S(2)}) copy-start(f32[1024]{0:T(1024)} %copy-done.33) | copy-start | bytes 12292
  618.2 474.6 %copy-start.46 = (f32[2,128]{1,0:T(2,128)S(1)}, f32[2,128]{1,0:T(2,128)}, u32[]{:S(2)}) copy-start(f32[2,128]{1,0:T(2,128)} %copy-done.45) | copy-start | bytes 3076
  618.2 476.2 %copy-start.44 = (f32[1024]{0:T(1024)S(1)}, f32[1024]{0:T(1024)}, u32[]{:S(2)}) copy-start(f32[1024]{0:T(1024)} %get-tuple-element.204) | copy-start | bytes 12292
  618.2 516.6 %copy-start.48 = (f32[2,128]{1,0:T(2,128)S(1)}, f32[2,128]{1,0:T(2,128)}, u32[]{:S(2)}) copy-start(f32[2,128]{1,0:T(2,128)} %copy-done.47) | copy-start | bytes 3076
  618.2 522.4 %copy-start.5 = (f32[2,128,1024]{2,1,0:T(8,128)S(1)}, f32[2,128,1024]{2,1,0:T(8,128)}, u32[]{:S(2)}) copy-start(f32[2,128,1024]{2,1,0:T(8,128)} %reduce-scatter.20.cloned.1.call-done) | copy-start | bytes 3145732
  618.3 522.4 %copy-start.32 = (f32[1024]{0:T(1024)S(1)}, f32[1024]{0:T(1024)}, u32[]{:S(2)}) copy-start(f32[1024]{0:T(1024)} %copy-done.31) | copy-start | bytes 12292
  618.3 522.4 %copy-start.42 = (f32[2,128]{1,0:T(2,128)S(1)}, f32[2,128]{1,0:T(2,128)}, u32[]{:S(2)}) copy-start(f32[2,128]{1,0:T(2,128)} %copy-done.41) | copy-start | bytes 3076
  618.3 522.4 %copy-start.50 = (f32[2,128]{1,0:T(2,128)S(1)}, f32[2,128]{1,0:T(2,128)}, u32[]{:S(2)}) copy-start(f32[2,128]{1,0:T(2,128)} %copy-done.49) | copy-start | bytes 3076
  (41 other events, 200.3 us)
Sparse Core Ops, SparseCore 0:
  13.3 25.2 all-gather.9
  148.3 22.1 all-gather.11
  172.7 21.2 all-gather.13
  220.1 44.5 reduce-scatter.15
  438.7 42.9 reduce-scatter.19
  533.1 20.3 reduce-scatter.23
  555.8 20.3 reduce-scatter.21
  579.7 67.8 reduce-scatter.39
  651.1 66.8 reduce-scatter.37
  721.4 66.6 reduce-scatter.35
  791.5 60.9 reduce-scatter.33
  856.0 60.9 reduce-scatter.31
  920.9 60.8 reduce-scatter.29
  986.0 60.9 reduce-scatter.27
  1049.3 43.4 reduce-scatter.25
  1095.4 45.2 reduce-scatter.17
Sparse Core Ops, SparseCore 1:
  222.9 49.3 all-gather.19
  274.3 20.9 all-gather.15
  297.5 49.3 all-gather.17
  348.5 20.9 all-gather.23
  371.8 49.3 all-gather.21
  486.3 22.4 all-gather.25
where the time goes:
time: 1160 us; the launch traced here: 1150 us
  waiting for transfers between devices  750 us (65%)
  blocking collectives  168 us (14%)
  matrix products  124 us (11%)
  other arithmetic  56.5 us (5%)
  local copies, waits for them, and re-layouts  33 us (3%)
  between operations  16.9 us (1%)
    reduce_scatter x4, waiting for transfers between devices, scatter_rows(): return lax.psum_scatter(values, 'tp', scatter_dimension=1, tiled=True)  137 us
    reduce_scatter x1, waiting for transfers between devices, shards(): lax.psum_scatter(up_local.astype(jnp.bfloat16), ('fsdp', 'ctx'), scatter_...  68.4 us
    reduce_scatter x1, waiting for transfers between devices, shards(): lax.psum_scatter(gate_local.astype(jnp.bfloat16), ('fsdp', 'ctx'), scatte...  68.3 us
    reduce_scatter x1, waiting for transfers between devices, shards(): lax.psum_scatter(query_local.astype(jnp.bfloat16), ('fsdp', 'ctx'), scatt...  63.6 us
    reduce_scatter x1, waiting for transfers between devices, shards(): lax.psum_scatter(key_local.astype(jnp.bfloat16), ('fsdp', 'ctx'), scatter...  63.3 us
    reduce_scatter x1, waiting for transfers between devices, shards(): lax.psum_scatter(value_local.astype(jnp.bfloat16), ('fsdp', 'ctx'), scatt...  63 us
    reduce_scatter x1, waiting for transfers between devices, shards(): lax.psum_scatter(out_local.astype(jnp.bfloat16), ('fsdp', 'ctx'), scatter...  62.4 us
    all_gather x4, waiting for transfers between devices, gather_rows(): return lax.all_gather(values, 'tp', axis=1, tiled=True)  61.4 us
  transfers between devices with their start and end apart: 22, of which 19 were waited for; matrix products, arithmetic and copies ran while one was open for 11% of the time, Pallas kernels for 0%

commit v1 on v0

v1 whole, which is shorter than its diff:
```python
import jax
import jax.numpy as jnp
from jax import lax
from jax.sharding import PartitionSpec as P

HEADS = 16
HEAD = 64
EPS = 1e-05
NEG = -1e30
F32 = jnp.float32
BF16 = jnp.bfloat16


def hop(values, axis, flip):
    size = lax.axis_size(axis)
    return lax.ppermute(values, axis, [(i, i ^ flip) for i in range(size)])


def swap_blocks(values, axis, index, size):
    shape = values.shape
    bit = 1
    while bit < size:
        split = shape[:axis] + (size // (2 * bit), 2, bit) + shape[axis + 1 :]
        cut = values.reshape(split)
        cut = jnp.where((index & bit) != 0, jnp.flip(cut, axis + 1), cut)
        values = cut.reshape(shape)
        bit *= 2
    return values


def gather_weight(block):
    nz = lax.axis_size("fsdp")
    across = hop(block, "ctx", 1)
    mine = [block] + [hop(block, "fsdp", k) for k in range(1, nz)]
    rest = [hop(piece, "ctx", 1) for piece in mine[1:]]
    return jnp.concatenate(mine + [across] + rest, axis=0)


def scatter_weight(partial):
    nz = lax.axis_size("fsdp")
    half = partial.shape[0] // 2
    rows = half // nz
    other = hop(partial[half:], "ctx", 1)
    total = partial[:half].astype(F32) + other.astype(F32)
    low = total.astype(BF16)
    out = total[:rows]
    for k in range(1, nz):
        out = out + hop(low[k * rows : (k + 1) * rows], "fsdp", k).astype(F32)
    return out


def gather_rows(block):
    nt = lax.axis_size("tp")
    mine = [block] + [hop(block, "tp", 2 * k) for k in range(1, nt // 2)]
    twin = [hop(piece, "tp", 1) for piece in mine]
    return jnp.concatenate(mine + twin, axis=0)


def scatter_rows(partial):
    nt = lax.axis_size("tp")
    half = partial.shape[0] // 2
    rows = 2 * half // nt
    total = partial[:half].astype(F32) + hop(partial[half:].astype(BF16), "tp", 1).astype(F32)
    low = total.astype(BF16)
    out = total[:rows]
    for k in range(1, nt // 2):
        out = out + hop(low[k * rows : (k + 1) * rows], "tp", 2 * k).astype(F32)
    return out


def heads_to_rows(values):
    nt = lax.axis_size("tp")
    rows = values.shape[0] // nt
    parts = []
    for flip in range(nt):
        slot = (flip & 1) * (nt // 2) + (flip >> 1)
        piece = values[slot * rows : (slot + 1) * rows]
        parts.append(piece if flip == 0 else hop(piece, "tp", flip))
    return jnp.concatenate(parts, axis=1)


def gather_heads(block):
    nt = lax.axis_size("tp")
    mine = [block] + [hop(block, "tp", 2 * k) for k in range(1, nt // 2)]
    twin = [hop(piece, "tp", 1) for piece in mine]
    parts = [None] * nt
    for k in range(nt // 2):
        parts[2 * k] = mine[k]
        parts[2 * k + 1] = twin[k]
    return jnp.concatenate(parts, axis=1)


def psum_all(values):
    nz = lax.axis_size("fsdp")
    nt = lax.axis_size("tp")
    for axis, size in (("tp", nt), ("ctx", 2), ("fsdp", nz)):
        bit = 1
        while bit < size:
            values = values + hop(values, axis, bit)
            bit *= 2
    return values


def psum_rows(values):
    nz = lax.axis_size("fsdp")
    for axis, size in (("ctx", 2), ("fsdp", nz)):
        bit = 1
        while bit < size:
            values = values + hop(values, axis, bit)
            bit *= 2
    return values


def inverse_rms(values):
    return lax.rsqrt(jnp.mean(values * values, axis=-1, keepdims=True) + EPS)


def norm_back(values, inv, gain, grad):
    scaled = grad * gain
    normed = values * inv
    d_gain = jnp.sum(grad * normed, axis=0)
    d_values = inv * (scaled - normed * jnp.mean(scaled * normed, axis=-1, keepdims=True))
    return d_values, d_gain


def angles_of(times):
    half = HEAD // 2
    frequency = 10000.0 ** (-2.0 * jnp.arange(half, dtype=F32) / HEAD)
    angles = times.astype(F32)[:, None, None] * frequency
    return jnp.cos(angles), jnp.sin(angles)


def rotate(values, cosine, sine):
    half = HEAD // 2
    first, second = values[..., :half], values[..., half:]
    return jnp.concatenate([first * cosine - second * sine, second * cosine + first * sine], axis=-1)


def dot(left, right, left_dim, right_dim):
    return lax.dot_general(
        left, right, (((left_dim,), (right_dim,)), ((), ())), preferred_element_type=F32
    )


def shards(
    layer_in,
    attn_gain,
    ffn_gain,
    query_weight,
    key_weight,
    value_weight,
    out_weight,
    variate_bias,
    gate_weight,
    up_weight,
    down_weight,
    segment_ids,
    variate_ids,
    time_ids,
    out_grad,
):
    seq_count, share, width = layer_in.shape
    nz, nx, nt = lax.axis_size("fsdp"), lax.axis_size("ctx"), lax.axis_size("tp")
    iz, ix, it = lax.axis_index("fsdp"), lax.axis_index("ctx"), lax.axis_index("tp")
    assert nx == 2 and seq_count == nx
    length = segment_ids.shape[1]
    local_heads = variate_bias.shape[1]
    proj = local_heads * HEAD
    scale = HEAD ** (-0.5)

    def to_slots(values):
        cut = values.reshape(values.shape[0], nz, nx, width // (nz * nx))
        cut = swap_blocks(swap_blocks(cut, 1, iz, nz), 2, ix, nx)
        return cut.transpose(0, 2, 1, 3).reshape(values.shape)

    def from_slots(values):
        cut = values.reshape(values.shape[0], nx, nz, width // (nz * nx)).transpose(0, 2, 1, 3)
        return swap_blocks(swap_blocks(cut, 1, iz, nz), 2, ix, nx).reshape(values.shape)

    def own_sequence(values):
        mine = lax.dynamic_index_in_dim(values, ix, 0, keepdims=False)
        other = lax.dynamic_index_in_dim(values, 1 - ix, 0, keepdims=False)
        return jnp.concatenate([mine, hop(other, "ctx", 1)], axis=0)

    def both_sequences(values):
        mine, other = values[:share], hop(values[share:], "ctx", 1)
        first = jnp.where(ix == 0, mine, other)
        second = jnp.where(ix == 0, other, mine)
        return jnp.stack([first, second])

    def ids_of(table):
        ids = lax.dynamic_index_in_dim(table, ix, 0, keepdims=False)
        cut = ids.reshape(nx, nt // 2, 2, share)
        cut = swap_blocks(cut, 0, ix, nx)
        cut = swap_blocks(cut, 1, it // 2, nt // 2)
        cut = swap_blocks(cut, 2, it % 2, 2)
        return cut.transpose(2, 1, 0, 3).reshape(length)

    gain_one = attn_gain.astype(F32)
    gain_two = ffn_gain.astype(F32)
    inputs = own_sequence(layer_in).astype(F32)
    grads = own_sequence(out_grad)
    inv_one = inverse_rms(inputs)
    rows_one = gather_rows(to_slots((inputs * inv_one * gain_one).astype(BF16)))
    qkv_full = gather_weight(jnp.concatenate([query_weight, key_weight, value_weight], axis=1))
    out_full = gather_weight(out_weight)
    gate_full = gather_weight(gate_weight)
    up_full = gather_weight(up_weight)
    down_full = gather_weight(down_weight)
    out_all = gather_heads(out_full)
    grad_rows = gather_rows(to_slots(grads))

    times, variates, segments = ids_of(time_ids), ids_of(variate_ids), ids_of(segment_ids)
    cosine, sine = angles_of(times)
    qkv = dot(rows_one, qkv_full, 1, 0)
    queries_raw = qkv[:, :proj].reshape(length, local_heads, HEAD)
    keys_raw = qkv[:, proj : 2 * proj].reshape(length, local_heads, HEAD)
    values = qkv[:, 2 * proj :].astype(BF16).reshape(length, local_heads, HEAD)
    queries = rotate(queries_raw, cosine, sine).astype(BF16)
    keys = rotate(keys_raw, cosine, sine).astype(BF16)

    def scores_of():
        raw = jnp.einsum("qhd,khd->hqk", queries, keys, preferred_element_type=F32) * scale
        same = (variates[:, None] == variates[None, :])[None]
        raw = raw + jnp.where(same, variate_bias[0][:, None, None], variate_bias[1][:, None, None])
        return jnp.where((segments[:, None] == segments[None, :])[None], raw, NEG), same

    scores, same = scores_of()
    top = jnp.max(scores, axis=-1, keepdims=True)
    expo = jnp.exp(scores - top)
    total = jnp.sum(expo, axis=-1, keepdims=True)
    probs = (expo / total).astype(BF16)
    mixed = jnp.einsum("hqk,khd->qhd", probs, values, preferred_element_type=F32)
    mixed = mixed.astype(BF16).reshape(length, proj)
    lse = top + jnp.log(total)

    attn = dot(heads_to_rows(mixed), out_all, 1, 1)
    hidden = inputs + from_slots(attn)
    inv_two = inverse_rms(hidden)
    rows_two = gather_rows(to_slots((hidden * inv_two * gain_two).astype(BF16)))
    gate = dot(rows_two, gate_full, 1, 0)
    up_vals = dot(rows_two, up_full, 1, 0)
    sig = jax.nn.sigmoid(gate)
    silu = gate * sig
    act = (silu * up_vals).astype(BF16)
    d_act = dot(grad_rows, down_full, 1, 0)
    d_gate = (d_act * up_vals * (sig + silu * (1.0 - sig))).astype(BF16)
    d_up = (d_act * silu).astype(BF16)
    d_normed_two = dot(d_gate, gate_full, 1, 1) + dot(d_up, up_full, 1, 1)
    d_normed_two = from_slots(scatter_rows(d_normed_two))

    ffn = scatter_rows(dot(act, down_full, 1, 1))
    layer_out = both_sequences((hidden + from_slots(ffn)).astype(BF16))

    down_grad = scatter_weight(dot(grad_rows, act, 0, 0).astype(BF16))
    gate_grad = scatter_weight(dot(rows_two, d_gate, 0, 0).astype(BF16))
    up_grad = scatter_weight(dot(rows_two, d_up, 0, 0).astype(BF16))

    d_hidden_norm, d_gain_two = norm_back(hidden, inv_two, gain_two, d_normed_two)
    d_hidden = grads.astype(F32) + d_hidden_norm
    branch_rows = gather_rows(to_slots(d_hidden.astype(BF16)))
    d_mixed = dot(branch_rows, out_full, 1, 0).astype(BF16).reshape(length, local_heads, HEAD)
    out_weight_grad = scatter_weight(dot(branch_rows, mixed, 0, 0).astype(BF16))

    scores, same = scores_of()
    probs = jnp.exp(scores - lse)
    probs_low = probs.astype(BF16)
    d_probs = jnp.einsum("qhd,khd->hqk", d_mixed, values, preferred_element_type=F32)
    delta = jnp.sum(probs * d_probs, axis=-1, keepdims=True)
    d_scores = (probs * (d_probs - delta)).astype(BF16)
    d_queries = jnp.einsum("hqk,khd->qhd", d_scores, keys, preferred_element_type=F32) * scale
    d_keys = jnp.einsum("hqk,qhd->khd", d_scores, queries, preferred_element_type=F32) * scale
    d_values = jnp.einsum("hqk,qhd->khd", probs_low, d_mixed, preferred_element_type=F32)
    wide = d_scores.astype(F32)
    same_sum = jnp.sum(jnp.where(same, wide, 0.0), axis=(1, 2))
    diff_sum = jnp.sum(jnp.where(same, 0.0, wide), axis=(1, 2))
    bias_grad = psum_rows(jnp.stack([same_sum, diff_sum]))

    d_query_raw = rotate(d_queries, cosine, -sine).astype(BF16).reshape(length, proj)
    d_key_raw = rotate(d_keys, cosine, -sine).astype(BF16).reshape(length, proj)
    d_qkv = jnp.concatenate([d_query_raw, d_key_raw, d_values.astype(BF16).reshape(length, proj)], axis=1)
    d_normed_one = from_slots(scatter_rows(dot(d_qkv, qkv_full, 1, 1)))
    qkv_grad = scatter_weight(dot(rows_one, d_qkv, 0, 0).astype(BF16))
    d_input_norm, d_gain_one = norm_back(inputs, inv_one, gain_one, d_normed_one)
    in_grad = both_sequences((d_hidden + d_input_norm).astype(BF16))
    gain_grads = psum_all(jnp.stack([d_gain_one, d_gain_two]))
    return (
        layer_out,
        in_grad,
        gain_grads[0],
        gain_grads[1],
        qkv_grad[:, :proj],
        qkv_grad[:, proj : 2 * proj],
        qkv_grad[:, 2 * proj :],
        out_weight_grad,
        bias_grad,
        gate_grad,
        up_grad,
        down_grad,
    )


def solution(mesh):
    rows = P("fsdp", ("ctx", "tp"), None)
    weight = P(("fsdp", "ctx"), "tp")
    ids = P("fsdp", None)
    bias = P(None, "tp")
    in_specs = (rows, P(), P()) + (weight,) * 4 + (bias,) + (weight,) * 3 + (ids,) * 3 + (rows,)
    out_specs = (rows, rows, P(), P()) + (weight,) * 4 + (bias,) + (weight,) * 3
    return jax.shard_map(shards, mesh=mesh, in_specs=in_specs, out_specs=out_specs, check_vma=False)
```

time: 1160 us -> 498 us (0.43)
  waiting for transfers between devices: 750 us -> 215 us
  blocking collectives: 168 us -> 0 us
  starting transfers between devices: 2.17 us -> 105 us
  matrix products: 124 us -> 79.4 us
  other arithmetic: 56.5 us -> 38.8 us
  local copies, waits for them, and re-layouts: 33 us -> 48.3 us
  between operations: 16.9 us -> 2.91 us
    reduce_scatter x12 -> x0, waiting for transfers between devices: 526 us -> none  [the longest x4 137 us: scatter_rows(): return lax.psum_scatter(values, 'tp', scatter_dimension=1, tiled=True)]
    ppermute x0 -> x91, waiting for transfers between devices: none -> 215 us  [hop(): return lax.ppermute(values, axis, [(i, i ^ flip) for i in range(size)])]
    all_gather x9 -> x0, waiting for transfers between devices: 192 us -> none  [the longest x4 61.4 us: gather_rows(): return lax.all_gather(values, 'tp', axis=1, tiled=True)]
    all_gather x4 -> x0, blocking collectives: 128 us -> none  [the longest x1 33.3 us: shards(): lax.all_gather(query_weight, ('fsdp', 'ctx'), axis=0, tiled=True)]
    ppermute x0 -> x91, starting transfers between devices: none -> 105 us  [hop(): return lax.ppermute(values, axis, [(i, i ^ flip) for i in range(size)])]
    dot_general x33 -> x21, matrix products: 124 us -> 79.4 us  [the longest x15 42.1 us: dot(): lax.dot_general(left, right, (((left_dim,), (right_dim,)), ((), ())), pre...]
    psum x1 -> x0, blocking collectives: 39.8 us -> none  [shards(): lax.psum((d_gain_one, d_gain_two, bias_full), ('fsdp', 'ctx', 'tp'))]
    unnamed x23 -> x0, waiting for transfers between devices: 32 us -> none
  transfers between devices with their start and end apart: 22 -> 91, of which waited for: 19 -> 40; matrix products, arithmetic and copies ran while one was open for 11% -> 22% of each run, Pallas kernels for 0% -> 0%
where the time goes in v1:
time: 498 us; the launch traced here: 490 us
  waiting for transfers between devices  215 us (43%)
  starting transfers between devices  105 us (21%)
  matrix products  79.4 us (16%)
  local copies, waits for them, and re-layouts  48.3 us (10%)
  other arithmetic  38.8 us (8%)
    ppermute x91, waiting for transfers between devices, hop(): return lax.ppermute(values, axis, [(i, i ^ flip) for i in range(size)])  215 us
    ppermute x91, starting transfers between devices, hop(): return lax.ppermute(values, axis, [(i, i ^ flip) for i in range(size)])  105 us
    dot_general x15, matrix products, dot(): lax.dot_general(left, right, (((left_dim,), (right_dim,)), ((), ())), pre...  42.1 us
    unnamed x196, local copies, waits for them, and re-layouts  33.7 us
    reduce_sum x1, other arithmetic, shards(): same_sum = jnp.sum(jnp.where(same, wide, 0.0), axis=(1, 2))  12.2 us
    dot_general x1, matrix products, shards(): jnp.einsum('qhd,khd->hqk', d_mixed, values, preferred_element_type=F32)  10.7 us
  transfers between devices with their start and end apart: 91, of which 40 were waited for; matrix products, arithmetic and copies ran while one was open for 22% of the time, Pallas kernels for 0%

profile of v1, /device:TPU:0, one launch (start us, length us, event | category | flops | bytes accessed | tf_op | source)
XLA Modules:
  0.0 489.5 jit_solution(6136159477715342757)
XLA Ops:
  0.7 5.1 %collective-permute-start.16 = (bf16[128,256]{1,0:T(8,128)(2,1)}, bf16[128,256]{1,0:T(8,128)(2,1)}, u32[]{:S(2)}, u32[]{:S(2)}) collective-permute-start(bf16[128,256]{1,0:T(8,128)(2,1)} %param.21), channel_id=1, source_target_pairs={{0,24},{8,16},{16,8},{24,0},{1,25},{9,17},{17,9},{25,1},{2,26},{10... | collective-permute-start | bytes 196616 | tf_op jit(solution)/shard_map/ppermute | solution.py:16
  8.1 3.6 collective-permute-start.29
  49.4 2.6 collective-permute-start.5
  54.1 9.0 %collective-permute-done.5 = bf16[128,768]{1,0:T(8,128)(2,1)S(1)} collective-permute-done((bf16[128,768]{1,0:T(8,128)(2,1)S(1)}, bf16[128,768]{1,0:T(8,128)(2,1)S(1)}, u32[]{:S(2)}, u32[]{:S(2)}) %collective-permute-start.5) | collective-permute-done | bytes 196640 | tf_op jit(solution)/shard_map/ppermute | solution.py:16
  67.8 4.4 collective-permute-done
  73.5 4.2 collective-permute-done.51
  89.3 3.1 collective-permute-start.43
  93.1 3.1 collective-permute-done.34
  98.7 7.0 %collective-permute-done.35 = bf16[128,1024]{1,0:T(8,128)(2,1)} collective-permute-done((bf16[128,1024]{1,0:T(8,128)(2,1)S(1)}, bf16[128,1024]{1,0:T(8,128)(2,1)}, u32[]{:S(2)}, u32[]{:S(2)}) %collective-permute-start.35) | collective-permute-done | bytes 262176 | tf_op jit(solution)/shard_map/ppermute | solution.py:16
  107.0 3.6 collective-permute-start.42
  114.9 5.3 %collective-permute-done.42 = bf16[128,1024]{1,0:T(8,128)(2,1)S(1)} collective-permute-done((bf16[128,1024]{1,0:T(8,128)(2,1)S(1)}, bf16[128,1024]{1,0:T(8,128)(2,1)S(1)}, u32[]{:S(2)}, u32[]{:S(2)}) %collective-permute-start.42) | collective-permute-done | bytes 262176 | tf_op jit(solution)/shard_map/ppermute | solution.py:16
  123.0 5.6 %collective-permute-done.9 = bf16[128,768]{1,0:T(8,128)(2,1)S(1)} collective-permute-done((bf16[128,768]{1,0:T(8,128)(2,1)S(1)}, bf16[128,768]{1,0:T(8,128)(2,1)S(1)}, u32[]{:S(2)}, u32[]{:S(2)}) %collective-permute-start.9) | collective-permute-done | bytes 196640 | tf_op jit(solution)/shard_map/ppermute | solution.py:16
  130.0 2.8 collective-permute-done.10
  137.5 9.0 %fusion.104 = (f32[4,1024]{1,0:T(4,128)S(1)}, f32[4,1024,1024]{1,2,0:T(8,128)}) fusion(f32[4]{0:T(128)S(1)} %copy-done.60, f32[4]{0:T(128)S(1)} %copy-done.59, pred[1024,1024]{0,1:T(8,128)(4,1)S(1)} %broadcast_compare_fusion, bf16[1024,4,32]{0,2,1:T(8,128)(2,1)S(1)} %get-tuple-element.116, bf16[1024,4,32]{0,2,1:T(8,128)(2,1)S(1)} %get-tuple-element.117, ...), kind=kOutput, calls=%fused_computation.286 | convolution fusion | flops 559935488 | bytes 19939360 | tf_op jit(solution)/shard_map/qhd,khd->hqk/dot_general | solution.py:223
  146.6 8.0 %fusion.2 = f32[4,1024]{1,0:T(4,128)S(1)} fusion(f32[4,1024,1024]{1,2,0:T(8,128)} %get-tuple-element.132, f32[4,1024]{1,0:T(4,128)S(1)} %get-tuple-element.131), kind=kLoop, calls=%fused_computation.10 | loop fusion | flops 8384512 | bytes 16809984 | tf_op jit(solution)/shard_map/reduce_sum | solution.py:231
  154.6 7.6 %fusion.22 = bf16[4,64,1024]{2,1,0:T(8,128)(2,1)S(1)} fusion(bf16[1024,4,64]{0,2,1:T(8,128)(2,1)S(1)} %bitcast.232, f32[4,1024,1024]{1,2,0:T(8,128)} %get-tuple-element.132, f32[4,1024]{1,0:T(4,128)S(1)} %fusion.2, f32[4,1024]{1,0:T(4,128)S(1)} %get-tuple-element.131), kind=kOutput, calls=%fused_computation.76 | convolution fusion | flops 549715968 | bytes 17858560 | tf_op jit(solution)/shard_map/hqk,khd->qhd/dot_general | solution.py:233
  177.9 6.3 %collective-permute-done.32 = bf16[128,1024]{1,0:T(8,128)(2,1)} collective-permute-done((bf16[128,1024]{1,0:T(8,128)(2,1)}, bf16[128,1024]{1,0:T(8,128)(2,1)}, u32[]{:S(2)}, u32[]{:S(2)}) %collective-permute-start.32) | collective-permute-done | bytes 262176 | tf_op jit(solution)/shard_map/ppermute | solution.py:16
  187.3 8.1 %collective-permute-done.38 = bf16[128,1024]{1,0:T(8,128)(2,1)} collective-permute-done((bf16[128,1024]{1,0:T(8,128)(2,1)}, bf16[128,1024]{1,0:T(8,128)(2,1)}, u32[]{:S(2)}, u32[]{:S(2)}) %collective-permute-start.38) | collective-permute-done | bytes 262176 | tf_op jit(solution)/shard_map/ppermute | solution.py:16
  201.6 5.0 %collective-permute-done.45 = bf16[128,1024]{1,0:T(8,128)(2,1)S(1)} collective-permute-done((bf16[128,1024]{1,0:T(8,128)(2,1)S(1)}, bf16[128,1024]{1,0:T(8,128)(2,1)S(1)}, u32[]{:S(2)}, u32[]{:S(2)}) %collective-permute-start.45) | collective-permute-done | bytes 262176 | tf_op jit(solution)/shard_map/ppermute | solution.py:16
  207.1 5.1 %collective-permute-done.46 = bf16[128,1024]{1,0:T(8,128)(2,1)S(1)} collective-permute-done((bf16[128,1024]{1,0:T(8,128)(2,1)S(1)}, bf16[128,1024]{1,0:T(8,128)(2,1)S(1)}, u32[]{:S(2)}, u32[]{:S(2)}) %collective-permute-start.46) | collective-permute-done | bytes 262176 | tf_op jit(solution)/shard_map/ppermute | solution.py:16
  212.2 4.9 collective-permute-done.47
  217.2 2.4 fusion.93
  219.7 4.5 fusion.94
  224.1 7.1 %multiply_convert_fusion.2 = (bf16[1024,1024]{1,0:T(8,128)(2,1)S(1)}, bf16[1024,1024]{1,0:T(8,128)(2,1)S(1)}, bf16[1024,1024]{1,0:T(8,128)(2,1)S(1)}) fusion(f32[1024,1024]{1,0:T(8,128)S(1)} %fusion.93, f32[1024,1024]{1,0:T(8,128)} %fusion.94, bf16[1024,1024]{1,0:T(8,128)(2,1)S(1)} %constant_dynamic-update-slice_fusion.37, ...), kind=kOutput, calls=%fused_computation.16 | convolution fusion | flops 2170552320 | bytes 18874368 | tf_op jit(solution)/shard_map/dot_general | solution.py:140
  231.2 2.4 fusion.105
  233.8 4.3 convolution_convert_fusion
  245.3 2.4 convolution_add_fusion
  251.0 13.2 %collective-permute-done.87 = bf16[512,1024]{1,0:T(8,128)(2,1)S(1)} collective-permute-done((bf16[512,1024]{1,0:T(8,128)(2,1)S(1)}, bf16[512,1024]{1,0:T(8,128)(2,1)S(1)}, u32[]{:S(2)}, u32[]{:S(2)}) %collective-permute-start.87) | collective-permute-done | bytes 1048608 | tf_op jit(solution)/shard_map/ppermute | solution.py:16
  267.4 19.3 %collective-permute-done.79 = bf16[512,1024]{1,0:T(8,128)(2,1)S(1)} collective-permute-done((bf16[512,1024]{1,0:T(8,128)(2,1)S(1)}, bf16[512,1024]{1,0:T(8,128)(2,1)S(1)}, u32[]{:S(2)}, u32[]{:S(2)}) %collective-permute-start.79) | collective-permute-done | bytes 1048608 | tf_op jit(solution)/shard_map/ppermute | solution.py:16
  287.2 21.5 %collective-permute-done.83 = bf16[512,1024]{1,0:T(8,128)(2,1)S(1)} collective-permute-done((bf16[512,1024]{1,0:T(8,128)(2,1)S(1)}, bf16[512,1024]{1,0:T(8,128)(2,1)S(1)}, u32[]{:S(2)}, u32[]{:S(2)}) %collective-permute-start.83) | collective-permute-done | bytes 1048608 | tf_op jit(solution)/shard_map/ppermute | solution.py:16
  315.7 9.1 %collective-permute-done.80 = bf16[128,1024]{1,0:T(8,128)(2,1)S(1)} collective-permute-done((bf16[128,1024]{1,0:T(8,128)(2,1)S(1)}, bf16[128,1024]{1,0:T(8,128)(2,1)S(1)}, u32[]{:S(2)}, u32[]{:S(2)}) %collective-permute-start.80) | collective-permute-done | bytes 262176 | tf_op jit(solution)/shard_map/ppermute | solution.py:16
  326.7 6.6 %collective-permute-start.85 = (bf16[128,1024]{1,0:T(8,128)(2,1)S(1)}, bf16[128,1024]{1,0:T(8,128)(2,1)S(1)}, u32[]{:S(2)}, u32[]{:S(2)}) collective-permute-start(bf16[128,1024]{1,0:T(8,128)(2,1)S(1)} %get-tuple-element.87), channel_id=1, source_target_pairs={{0,16},{8,24},{16,0},{24,8},{1,17},{9,25},{17,1},{25,9},{2,18},{10... | collective-permute-start | bytes 786440 | tf_op jit(solution)/shard_map/ppermute | solution.py:16
  333.3 15.8 %collective-permute-done.81 = bf16[128,1024]{1,0:T(8,128)(2,1)S(1)} collective-permute-done((bf16[128,1024]{1,0:T(8,128)(2,1)S(1)}, bf16[128,1024]{1,0:T(8,128)(2,1)S(1)}, u32[]{:S(2)}, u32[]{:S(2)}) %collective-permute-start.81) | collective-permute-done | bytes 262176 | tf_op jit(solution)/shard_map/ppermute | solution.py:16
  351.6 6.9 %collective-permute-done.85 = bf16[128,1024]{1,0:T(8,128)(2,1)S(1)} collective-permute-done((bf16[128,1024]{1,0:T(8,128)(2,1)S(1)}, bf16[128,1024]{1,0:T(8,128)(2,1)S(1)}, u32[]{:S(2)}, u32[]{:S(2)}) %collective-permute-start.85) | collective-permute-done | bytes 262176 | tf_op jit(solution)/shard_map/ppermute | solution.py:16
  364.1 12.4 %collective-permute-done.57 = bf16[256,1024]{0,1:T(8,128)(2,1)S(1)} collective-permute-done((bf16[256,1024]{0,1:T(8,128)(2,1)S(1)}, bf16[256,1024]{0,1:T(8,128)(2,1)S(1)}, u32[]{:S(2)}, u32[]{:S(2)}) %collective-permute-start.57) | collective-permute-done | bytes 524320 | tf_op jit(solution)/shard_map/ppermute | solution.py:16
  378.4 3.6 convolution_convert_fusion.5
  382.0 4.6 fusion.19
  386.6 10.7 %multiply_reduce_fusion = (f32[4,1024]{1,0:T(4,128)}, f32[4,1024,1024]{1,2,0:T(8,128)}) fusion(f32[4,1024,1024]{1,2,0:T(8,128)S(1)} %bitcast.195, f32[4,1024]{1,0:T(4,128)S(1)} %log_add_fusion, bf16[1024,4,64]{0,2,1:T(8,128)(2,1)} %bitcast.90, bf16[1024,4,64]{0,2,1:T(8,128)(2,1)} %bitcast.233), kind=kOutput, calls=%fused_computation.5 | convolution fusion | flops 549449728 | bytes 34635776 | tf_op jit(solution)/shard_map/qhd,khd->hqk/dot_general | solution.py:268
  397.3 12.2 %fusion = (f32[4]{0:T(128)}, f32[4]{0:T(128)}, bf16[4,1024,1024]{1,2,0:T(8,128)(2,1)S(1)}) fusion(pred[1024,1024]{0,1:T(8,128)(4,1)} %copy-done.2, f32[4,1024,1024]{1,2,0:T(8,128)} %get-tuple-element.134, f32[4,1024]{1,0:T(4,128)} %get-tuple-element.133, f32[4,1024,1024]{1,2,0:T(8,128)S(1)} %bitcast.195, f32[4,1024]{1,0:T(4,128)S(1)} %log_add_fusion), kind=kLoop, calls=%fused_computation.2 | loop fusion | flops 37748728 | bytes 43024416 | tf_op jit(solution)/shard_map/reduce_sum | solution.py:275
  409.6 3.7 fusion.17
  425.7 3.6 collective-permute-done.77
  430.5 3.3 collective-permute-done.78
  434.8 2.4 collective-permute-start.75
  444.2 4.3 collective-permute-done.61
  451.8 2.6 collective-permute-start.71
  457.6 6.8 %collective-permute-done.71 = bf16[128,768]{1,0:T(8,128)(2,1)S(1)} collective-permute-done((bf16[128,768]{1,0:T(8,128)(2,1)S(1)}, bf16[128,768]{1,0:T(8,128)(2,1)S(1)}, u32[]{:S(2)}, u32[]{:S(2)}) %collective-permute-start.71) | collective-permute-done | bytes 196640 | tf_op jit(solution)/shard_map/ppermute | solution.py:16
  464.4 7.0 %collective-permute-done.70 = bf16[128,768]{1,0:T(8,128)(2,1)S(1)} collective-permute-done((bf16[128,768]{1,0:T(8,128)(2,1)S(1)}, bf16[128,768]{1,0:T(8,128)(2,1)S(1)}, u32[]{:S(2)}, u32[]{:S(2)}) %collective-permute-start.70) | collective-permute-done | bytes 196640 | tf_op jit(solution)/shard_map/ppermute | solution.py:16
  485.5 2.7 collective-permute-done.62
  (500 shorter events, 178.0 us)
Async XLA Ops:
  0.7 32.9 %collective-permute-start.16 = (bf16[128,256]{1,0:T(8,128)(2,1)}, bf16[128,256]{1,0:T(8,128)(2,1)}, u32[]{:S(2)}, u32[]{:S(2)}) collective-permute-start(bf16[128,256]{1,0:T(8,128)(2,1)} %param.21), channel_id=1, source_target_pairs={{0,24},{8,16},{16,8},{24,0},{1,25},{9,17},{17,9},{25,1},{2,26},{10... | collective-permute-start | bytes 196616 | tf_op jit(solution)/shard_map/ppermute | solution.py:16
  5.8 25.8 %collective-permute-start.15 = (bf16[128,256]{1,0:T(8,128)(2,1)}, bf16[128,256]{1,0:T(8,128)(2,1)}, u32[]{:S(2)}, u32[]{:S(2)}) collective-permute-start(bf16[128,256]{1,0:T(8,128)(2,1)} %param.21), channel_id=1, source_target_pairs={{0,16},{8,24},{16,0},{24,8},{1,17},{9,25},{17,1},{25,9},{2,18},{10... | collective-permute-start | bytes 196616 | tf_op jit(solution)/shard_map/ppermute | solution.py:16
  5.8 24.3 %collective-permute-start.14 = (bf16[128,256]{1,0:T(8,128)(2,1)}, bf16[128,256]{1,0:T(8,128)(2,1)}, u32[]{:S(2)}, u32[]{:S(2)}) collective-permute-start(bf16[128,256]{1,0:T(8,128)(2,1)} %param.21), channel_id=1, source_target_pairs={{0,8},{8,0},{16,24},{24,16},{1,9},{9,1},{17,25},{25,17},{2,10},{10... | collective-permute-start | bytes 196616 | tf_op jit(solution)/shard_map/ppermute | solution.py:16
  6.4 29.3 %collective-permute-start.17 = (bf16[128,256]{1,0:T(8,128)(2,1)}, bf16[128,256]{1,0:T(8,128)(2,1)}, u32[]{:S(2)}, u32[]{:S(2)}) collective-permute-start(bf16[128,256]{1,0:T(8,128)(2,1)} %param.21), channel_id=1, source_target_pairs={{0,4},{4,0},{1,5},{5,1},{2,6},{6,2},{3,7},{7,3},{8,12},{12,8},{9,1... | collective-permute-start | bytes 196616 | tf_op jit(solution)/shard_map/ppermute | solution.py:16
  8.1 78.4 %collective-permute-start.29 = (bf16[128,1024]{1,0:T(8,128)(2,1)}, bf16[128,1024]{1,0:T(8,128)(2,1)}, u32[]{:S(2)}, u32[]{:S(2)}) collective-permute-start(bf16[128,1024]{1,0:T(8,128)(2,1)} %param.23), channel_id=1, source_target_pairs={{0,24},{8,16},{16,8},{24,0},{1,25},{9,17},{17,9},{25,1},{2,26},{10... | collective-permute-start | bytes 786440 | tf_op jit(solution)/shard_map/ppermute | solution.py:16
  30.1 52.7 %collective-permute-start.28 = (bf16[128,1024]{1,0:T(8,128)(2,1)}, bf16[128,1024]{1,0:T(8,128)(2,1)}, u32[]{:S(2)}, u32[]{:S(2)}) collective-permute-start(bf16[128,1024]{1,0:T(8,128)(2,1)} %param.23), channel_id=1, source_target_pairs={{0,16},{8,24},{16,0},{24,8},{1,17},{9,25},{17,1},{25,9},{2,18},{10... | collective-permute-start | bytes 786440 | tf_op jit(solution)/shard_map/ppermute | solution.py:16
  31.6 34.5 %collective-permute-start.7 = (bf16[128,768]{1,0:T(8,128)(2,1)S(1)}, bf16[128,768]{1,0:T(8,128)(2,1)S(1)}, u32[]{:S(2)}, u32[]{:S(2)}) collective-permute-start(bf16[128,768]{1,0:T(8,128)(2,1)S(1)} %get-tuple-element.118), channel_id=1, source_target_pairs={{0,4},{4,0},{1,5},{5,1},{2,6},{6,2},{3,7},{7,3},{8,12},{12,8},{9,1... | collective-permute-start | bytes 589832 | tf_op jit(solution)/shard_map/ppermute | solution.py:16
  33.6 19.0 %collective-permute-start.4 = (bf16[128,768]{1,0:T(8,128)(2,1)S(1)}, bf16[128,768]{1,0:T(8,128)(2,1)S(1)}, u32[]{:S(2)}, u32[]{:S(2)}) collective-permute-start(bf16[128,768]{1,0:T(8,128)(2,1)S(1)} %get-tuple-element.118), channel_id=1, source_target_pairs={{0,8},{8,0},{16,24},{24,16},{1,9},{9,1},{17,25},{25,17},{2,10},{10... | collective-permute-start | bytes 589832 | tf_op jit(solution)/shard_map/ppermute | solution.py:16
  64.4 17.5 %collective-permute-start.27 = (bf16[128,1024]{1,0:T(8,128)(2,1)}, bf16[128,1024]{1,0:T(8,128)(2,1)S(1)}, u32[]{:S(2)}, u32[]{:S(2)}) collective-permute-start(bf16[128,1024]{1,0:T(8,128)(2,1)} %param.23), channel_id=1, source_target_pairs={{0,8},{8,0},{16,24},{24,16},{1,9},{9,1},{17,25},{25,17},{2,10},{10... | collective-permute-start | bytes 786440 | tf_op jit(solution)/shard_map/ppermute | solution.py:16
  72.1 17.2 %collective-permute-start.30 = (bf16[128,1024]{1,0:T(8,128)(2,1)}, bf16[128,1024]{1,0:T(8,128)(2,1)S(1)}, u32[]{:S(2)}, u32[]{:S(2)}) collective-permute-start(bf16[128,1024]{1,0:T(8,128)(2,1)} %param.23), channel_id=1, source_target_pairs={{0,4},{4,0},{1,5},{5,1},{2,6},{6,2},{3,7},{7,3},{8,12},{12,8},{9,1... | collective-permute-start | bytes 786440 | tf_op jit(solution)/shard_map/ppermute | solution.py:16
  77.8 29.3 %collective-permute-start.36 = (bf16[128,1024]{1,0:T(8,128)(2,1)S(1)}, bf16[128,1024]{1,0:T(8,128)(2,1)S(1)}, u32[]{:S(2)}, u32[]{:S(2)}) collective-permute-start(bf16[128,1024]{1,0:T(8,128)(2,1)S(1)} %copy-done.27), channel_id=1, source_target_pairs={{0,24},{8,16},{16,8},{24,0},{1,25},{9,17},{17,9},{25,1},{2,26},{10... | collective-permute-start | bytes 786440 | tf_op jit(solution)/shard_map/ppermute | solution.py:16
  81.9 23.8 %collective-permute-start.35 = (bf16[128,1024]{1,0:T(8,128)(2,1)S(1)}, bf16[128,1024]{1,0:T(8,128)(2,1)}, u32[]{:S(2)}, u32[]{:S(2)}) collective-permute-start(bf16[128,1024]{1,0:T(8,128)(2,1)S(1)} %copy-done.27), channel_id=1, source_target_pairs={{0,16},{8,24},{16,0},{24,8},{1,17},{9,25},{17,1},{25,9},{2,18},{10... | collective-permute-start | bytes 786440 | tf_op jit(solution)/shard_map/ppermute | solution.py:16
  86.4 24.2 %collective-permute-start.37 = (bf16[128,1024]{1,0:T(8,128)(2,1)S(1)}, bf16[128,1024]{1,0:T(8,128)(2,1)S(1)}, u32[]{:S(2)}, u32[]{:S(2)}) collective-permute-start(bf16[128,1024]{1,0:T(8,128)(2,1)S(1)} %copy-done.27), channel_id=1, source_target_pairs={{0,4},{4,0},{1,5},{5,1},{2,6},{6,2},{3,7},{7,3},{8,12},{12,8},{9,1... | collective-permute-start | bytes 786440 | tf_op jit(solution)/shard_map/ppermute | solution.py:16
  89.3 31.5 %collective-permute-start.43 = (bf16[128,1024]{1,0:T(8,128)(2,1)S(1)}, bf16[128,1024]{1,0:T(8,128)(2,1)S(1)}, u32[]{:S(2)}, u32[]{:S(2)}) collective-permute-start(bf16[128,1024]{1,0:T(8,128)(2,1)S(1)} %copy-done.28), channel_id=1, source_target_pairs={{0,24},{8,16},{16,8},{24,0},{1,25},{9,17},{17,9},{25,1},{2,26},{10... | collective-permute-start | bytes 786440 | tf_op jit(solution)/shard_map/ppermute | solution.py:16
  96.2 24.0 %collective-permute-start.1 = (bf16[256,1024]{0,1:T(8,128)(2,1)S(1)}, bf16[256,1024]{0,1:T(8,128)(2,1)S(1)}, u32[]{:S(2)}, u32[]{:S(2)}) collective-permute-start(bf16[256,1024]{0,1:T(8,128)(2,1)S(1)} %bitcast.246), channel_id=1, source_target_pairs={{0,2},{1,3},{2,0},{3,1},{4,6},{5,7},{6,4},{7,5},{8,10},{9,11},{10,... | collective-permute-start | bytes 1572872 | tf_op jit(solution)/shard_map/ppermute | solution.py:16
  110.6 22.2 %collective-permute-start.22 = (bf16[1024,256]{1,0:T(8,128)(2,1)}, bf16[1024,256]{1,0:T(8,128)(2,1)}, u32[]{:S(2)}, u32[]{:S(2)}) collective-permute-start(bf16[1024,256]{1,0:T(8,128)(2,1)} %constant_dynamic-update-slice_fusion.13), channel_id=1, source_target_pairs={{0,2},{1,3},{2,0},{3,1},{4,6},{5,7},{6,4},{7,5},{8,10},{9,11},{10,... | collective-permute-start | bytes 1572872 | tf_op jit(solution)/shard_map/ppermute | solution.py:16
  128.6 35.1 %collective-permute-start.44 = (bf16[128,1024]{1,0:T(8,128)(2,1)S(1)}, bf16[128,1024]{1,0:T(8,128)(2,1)}, u32[]{:S(2)}, u32[]{:S(2)}) collective-permute-start(bf16[128,1024]{1,0:T(8,128)(2,1)S(1)} %copy-done.28), channel_id=1, source_target_pairs={{0,4},{4,0},{1,5},{5,1},{2,6},{6,2},{3,7},{7,3},{8,12},{12,8},{9,1... | collective-permute-start | bytes 786440 | tf_op jit(solution)/shard_map/ppermute | solution.py:16
  132.8 34.8 %collective-permute-start.21 = (bf16[1024,256]{1,0:T(8,128)(2,1)}, bf16[1024,256]{1,0:T(8,128)(2,1)}, u32[]{:S(2)}, u32[]{:S(2)}) collective-permute-start(bf16[1024,256]{1,0:T(8,128)(2,1)} %constant_dynamic-update-slice_fusion.13), channel_id=1, source_target_pairs={{0,1},{1,0},{2,3},{3,2},{4,5},{5,4},{6,7},{7,6},{8,9},{9,8},{10,11... | collective-permute-start | bytes 1572872 | tf_op jit(solution)/shard_map/ppermute | solution.py:16
  132.9 31.4 %collective-permute-start.31 = (bf16[128,1024]{1,0:T(8,128)(2,1)S(1)}, bf16[128,1024]{1,0:T(8,128)(2,1)}, u32[]{:S(2)}, u32[]{:S(2)}) collective-permute-start(bf16[128,1024]{1,0:T(8,128)(2,1)S(1)} %collective-permute-done.27), channel_id=1, source_target_pairs={{0,4},{4,0},{1,5},{5,1},{2,6},{6,2},{3,7},{7,3},{8,12},{12,8},{9,1... | collective-permute-start | bytes 786440 | tf_op jit(solution)/shard_map/ppermute | solution.py:16
  134.3 34.8 %collective-permute-start.23 = (bf16[1024,256]{1,0:T(8,128)(2,1)}, bf16[1024,256]{1,0:T(8,128)(2,1)}, u32[]{:S(2)}, u32[]{:S(2)}) collective-permute-start(bf16[1024,256]{1,0:T(8,128)(2,1)} %collective-permute-done.22), channel_id=1, source_target_pairs={{0,1},{1,0},{2,3},{3,2},{4,5},{5,4},{6,7},{7,6},{8,9},{9,8},{10,11... | collective-permute-start | bytes 1572872 | tf_op jit(solution)/shard_map/ppermute | solution.py:16
  167.6 49.5 %collective-permute-start.52 = (bf16[256,1024]{0,1:T(8,128)(2,1)}, bf16[256,1024]{0,1:T(8,128)(2,1)}, u32[]{:S(2)}, u32[]{:S(2)}) collective-permute-start(bf16[256,1024]{0,1:T(8,128)(2,1)} %bitcast.72), channel_id=1, source_target_pairs={{0,2},{1,3},{2,0},{3,1},{4,6},{5,7},{6,4},{7,5},{8,10},{9,11},{10,... | collective-permute-start | bytes 1572872 | tf_op jit(solution)/shard_map/ppermute | solution.py:16
  169.1 16.6 %collective-permute-start.33 = (bf16[128,1024]{1,0:T(8,128)(2,1)}, bf16[128,1024]{1,0:T(8,128)(2,1)}, u32[]{:S(2)}, u32[]{:S(2)}) collective-permute-start(bf16[128,1024]{1,0:T(8,128)(2,1)} %collective-permute-done.29), channel_id=1, source_target_pairs={{0,4},{4,0},{1,5},{5,1},{2,6},{6,2},{3,7},{7,3},{8,12},{12,8},{9,1... | collective-permute-start | bytes 786440 | tf_op jit(solution)/shard_map/ppermute | solution.py:16
  171.1 25.9 %collective-permute-start.39 = (bf16[128,1024]{1,0:T(8,128)(2,1)}, bf16[128,1024]{1,0:T(8,128)(2,1)}, u32[]{:S(2)}, u32[]{:S(2)}) collective-permute-start(bf16[128,1024]{1,0:T(8,128)(2,1)} %collective-permute-done.35), channel_id=1, source_target_pairs={{0,4},{4,0},{1,5},{5,1},{2,6},{6,2},{3,7},{7,3},{8,12},{12,8},{9,1... | collective-permute-start | bytes 786440 | tf_op jit(solution)/shard_map/ppermute | solution.py:16
  171.8 23.6 %collective-permute-start.38 = (bf16[128,1024]{1,0:T(8,128)(2,1)}, bf16[128,1024]{1,0:T(8,128)(2,1)}, u32[]{:S(2)}, u32[]{:S(2)}) collective-permute-start(bf16[128,1024]{1,0:T(8,128)(2,1)} %collective-permute-done.34), channel_id=1, source_target_pairs={{0,4},{4,0},{1,5},{5,1},{2,6},{6,2},{3,7},{7,3},{8,12},{12,8},{9,1... | collective-permute-start | bytes 786440 | tf_op jit(solution)/shard_map/ppermute | solution.py:16
  184.2 22.4 %collective-permute-start.24 = (bf16[256,1024]{0,1:T(8,128)(2,1)S(1)}, bf16[256,1024]{0,1:T(8,128)(2,1)S(1)}, u32[]{:S(2)}, u32[]{:S(2)}) collective-permute-start(bf16[256,1024]{0,1:T(8,128)(2,1)S(1)} %bitcast.250), channel_id=1, source_target_pairs={{0,2},{1,3},{2,0},{3,1},{4,6},{5,7},{6,4},{7,5},{8,10},{9,11},{10,... | collective-permute-start | bytes 1572872 | tf_op jit(solution)/shard_map/ppermute | solution.py:16
  185.7 15.2 %collective-permute-start.40 = (bf16[128,1024]{1,0:T(8,128)(2,1)S(1)}, bf16[128,1024]{1,0:T(8,128)(2,1)S(1)}, u32[]{:S(2)}, u32[]{:S(2)}) collective-permute-start(bf16[128,1024]{1,0:T(8,128)(2,1)S(1)} %copy-done.30), channel_id=1, source_target_pairs={{0,4},{4,0},{1,5},{5,1},{2,6},{6,2},{3,7},{7,3},{8,12},{12,8},{9,1... | collective-permute-start | bytes 786440 | tf_op jit(solution)/shard_map/ppermute | solution.py:16
  197.0 15.1 %collective-permute-start.46 = (bf16[128,1024]{1,0:T(8,128)(2,1)S(1)}, bf16[128,1024]{1,0:T(8,128)(2,1)S(1)}, u32[]{:S(2)}, u32[]{:S(2)}) collective-permute-start(bf16[128,1024]{1,0:T(8,128)(2,1)S(1)} %copy-done.34), channel_id=1, source_target_pairs={{0,4},{4,0},{1,5},{5,1},{2,6},{6,2},{3,7},{7,3},{8,12},{12,8},{9,1... | collective-permute-start | bytes 786440 | tf_op jit(solution)/shard_map/ppermute | solution.py:16
  200.9 16.1 %collective-permute-start.47 = (bf16[128,1024]{1,0:T(8,128)(2,1)S(1)}, bf16[128,1024]{1,0:T(8,128)(2,1)S(1)}, u32[]{:S(2)}, u32[]{:S(2)}) collective-permute-start(bf16[128,1024]{1,0:T(8,128)(2,1)S(1)} %copy-done.32), channel_id=1, source_target_pairs={{0,4},{4,0},{1,5},{5,1},{2,6},{6,2},{3,7},{7,3},{8,12},{12,8},{9,1... | collective-permute-start | bytes 786440 | tf_op jit(solution)/shard_map/ppermute | solution.py:16
  238.1 26.0 %collective-permute-start.87 = (bf16[512,1024]{1,0:T(8,128)(2,1)S(1)}, bf16[512,1024]{1,0:T(8,128)(2,1)S(1)}, u32[]{:S(2)}, u32[]{:S(2)}) collective-permute-start(bf16[512,1024]{1,0:T(8,128)(2,1)S(1)} %slice.355), channel_id=1, source_target_pairs={{0,4},{4,0},{1,5},{5,1},{2,6},{6,2},{3,7},{7,3},{8,12},{12,8},{9,1... | collective-permute-start | bytes 3145736 | tf_op jit(solution)/shard_map/ppermute | solution.py:16
  238.8 26.1 %collective-permute-start.48 = (bf16[512,1024]{0,1:T(8,128)(2,1)S(1)}, bf16[512,1024]{0,1:T(8,128)(2,1)S(1)}, u32[]{:S(2)}, u32[]{:S(2)}) collective-permute-start(bf16[512,1024]{0,1:T(8,128)(2,1)S(1)} %slice.437), channel_id=1, source_target_pairs={{0,1},{1,0},{2,3},{3,2},{4,5},{5,4},{6,7},{7,6},{8,9},{9,8},{10,11... | collective-permute-start | bytes 3145736 | tf_op jit(solution)/shard_map/ppermute | solution.py:16
  243.9 42.8 %collective-permute-start.79 = (bf16[512,1024]{1,0:T(8,128)(2,1)S(1)}, bf16[512,1024]{1,0:T(8,128)(2,1)S(1)}, u32[]{:S(2)}, u32[]{:S(2)}) collective-permute-start(bf16[512,1024]{1,0:T(8,128)(2,1)S(1)} %slice.343), channel_id=1, source_target_pairs={{0,4},{4,0},{1,5},{5,1},{2,6},{6,2},{3,7},{7,3},{8,12},{12,8},{9,1... | collective-permute-start | bytes 3145736 | tf_op jit(solution)/shard_map/ppermute | solution.py:16
  250.3 58.4 %collective-permute-start.83 = (bf16[512,1024]{1,0:T(8,128)(2,1)S(1)}, bf16[512,1024]{1,0:T(8,128)(2,1)S(1)}, u32[]{:S(2)}, u32[]{:S(2)}) collective-permute-start(bf16[512,1024]{1,0:T(8,128)(2,1)S(1)} %slice.349), channel_id=1, source_target_pairs={{0,4},{4,0},{1,5},{5,1},{2,6},{6,2},{3,7},{7,3},{8,12},{12,8},{9,1... | collective-permute-start | bytes 3145736 | tf_op jit(solution)/shard_map/ppermute | solution.py:16
  251.0 58.7 %collective-permute-start.55 = (bf16[512,1024]{0,1:T(8,128)(2,1)S(1)}, bf16[512,1024]{0,1:T(8,128)(2,1)S(1)}, u32[]{:S(2)}, u32[]{:S(2)}) collective-permute-start(bf16[512,1024]{0,1:T(8,128)(2,1)S(1)} %slice.436), channel_id=1, source_target_pairs={{0,1},{1,0},{2,3},{3,2},{4,5},{5,4},{6,7},{7,6},{8,9},{9,8},{10,11... | collective-permute-start | bytes 3145736 | tf_op jit(solution)/shard_map/ppermute | solution.py:16
  264.9 45.4 %collective-permute-start.88 = (bf16[128,1024]{1,0:T(8,128)(2,1)S(1)}, bf16[128,1024]{1,0:T(8,128)(2,1)S(1)}, u32[]{:S(2)}, u32[]{:S(2)}) collective-permute-start(bf16[128,1024]{1,0:T(8,128)(2,1)S(1)} %get-tuple-element.82), channel_id=1, source_target_pairs={{0,8},{8,0},{16,24},{24,16},{1,9},{9,1},{17,25},{25,17},{2,10},{10... | collective-permute-start | bytes 786440 | tf_op jit(solution)/shard_map/ppermute | solution.py:16
  265.0 47.4 %collective-permute-start.90 = (bf16[128,1024]{1,0:T(8,128)(2,1)S(1)}, bf16[128,1024]{1,0:T(8,128)(2,1)S(1)}, u32[]{:S(2)}, u32[]{:S(2)}) collective-permute-start(bf16[128,1024]{1,0:T(8,128)(2,1)S(1)} %get-tuple-element.83), channel_id=1, source_target_pairs={{0,24},{8,16},{16,8},{24,0},{1,25},{9,17},{17,9},{25,1},{2,26},{10... | collective-permute-start | bytes 786440 | tf_op jit(solution)/shard_map/ppermute | solution.py:16
  286.6 27.2 %collective-permute-start.89 = (bf16[128,1024]{1,0:T(8,128)(2,1)S(1)}, bf16[128,1024]{1,0:T(8,128)(2,1)S(1)}, u32[]{:S(2)}, u32[]{:S(2)}) collective-permute-start(bf16[128,1024]{1,0:T(8,128)(2,1)S(1)} %get-tuple-element.84), channel_id=1, source_target_pairs={{0,16},{8,24},{16,0},{24,8},{1,17},{9,25},{17,1},{25,9},{2,18},{10... | collective-permute-start | bytes 786440 | tf_op jit(solution)/shard_map/ppermute | solution.py:16
  308.7 55.0 %collective-permute-start.49 = (bf16[256,1024]{0,1:T(8,128)(2,1)S(1)}, bf16[256,1024]{0,1:T(8,128)(2,1)S(1)}, u32[]{:S(2)}, u32[]{:S(2)}) collective-permute-start(bf16[256,1024]{0,1:T(8,128)(2,1)S(1)} %slice.440), channel_id=1, source_target_pairs={{0,2},{1,3},{2,0},{3,1},{4,6},{5,7},{6,4},{7,5},{8,10},{9,11},{10,... | collective-permute-start | bytes 1572872 | tf_op jit(solution)/shard_map/ppermute | solution.py:16
  310.3 16.4 %collective-permute-start.82 = (bf16[128,1024]{1,0:T(8,128)(2,1)S(1)}, bf16[128,1024]{1,0:T(8,128)(2,1)S(1)}, u32[]{:S(2)}, u32[]{:S(2)}) collective-permute-start(bf16[128,1024]{1,0:T(8,128)(2,1)S(1)} %get-tuple-element.89), channel_id=1, source_target_pairs={{0,24},{8,16},{16,8},{24,0},{1,25},{9,17},{17,9},{25,1},{2,26},{10... | collective-permute-start | bytes 786440 | tf_op jit(solution)/shard_map/ppermute | solution.py:16
  312.3 36.9 %collective-permute-start.81 = (bf16[128,1024]{1,0:T(8,128)(2,1)S(1)}, bf16[128,1024]{1,0:T(8,128)(2,1)S(1)}, u32[]{:S(2)}, u32[]{:S(2)}) collective-permute-start(bf16[128,1024]{1,0:T(8,128)(2,1)S(1)} %get-tuple-element.90), channel_id=1, source_target_pairs={{0,16},{8,24},{16,0},{24,8},{1,17},{9,25},{17,1},{25,9},{2,18},{10... | collective-permute-start | bytes 786440 | tf_op jit(solution)/shard_map/ppermute | solution.py:16
  313.9 37.8 %collective-permute-start.84 = (bf16[128,1024]{1,0:T(8,128)(2,1)S(1)}, bf16[128,1024]{1,0:T(8,128)(2,1)S(1)}, u32[]{:S(2)}, u32[]{:S(2)}) collective-permute-start(bf16[128,1024]{1,0:T(8,128)(2,1)S(1)} %get-tuple-element.85), channel_id=1, source_target_pairs={{0,8},{8,0},{16,24},{24,16},{1,9},{9,1},{17,25},{25,17},{2,10},{10... | collective-permute-start | bytes 786440 | tf_op jit(solution)/shard_map/ppermute | solution.py:16
  324.8 26.8 %collective-permute-start.86 = (bf16[128,1024]{1,0:T(8,128)(2,1)S(1)}, bf16[128,1024]{1,0:T(8,128)(2,1)S(1)}, u32[]{:S(2)}, u32[]{:S(2)}) collective-permute-start(bf16[128,1024]{1,0:T(8,128)(2,1)S(1)} %get-tuple-element.86), channel_id=1, source_target_pairs={{0,24},{8,16},{16,8},{24,0},{1,25},{9,17},{17,9},{25,1},{2,26},{10... | collective-permute-start | bytes 786440 | tf_op jit(solution)/shard_map/ppermute | solution.py:16
  326.7 31.8 %collective-permute-start.85 = (bf16[128,1024]{1,0:T(8,128)(2,1)S(1)}, bf16[128,1024]{1,0:T(8,128)(2,1)S(1)}, u32[]{:S(2)}, u32[]{:S(2)}) collective-permute-start(bf16[128,1024]{1,0:T(8,128)(2,1)S(1)} %get-tuple-element.87), channel_id=1, source_target_pairs={{0,16},{8,24},{16,0},{24,8},{1,17},{9,25},{17,1},{25,9},{2,18},{10... | collective-permute-start | bytes 786440 | tf_op jit(solution)/shard_map/ppermute | solution.py:16
  362.1 15.8 %collective-permute-start.58 = (bf16[256,1024]{0,1:T(8,128)(2,1)S(1)}, bf16[256,1024]{0,1:T(8,128)(2,1)S(1)}, u32[]{:S(2)}, u32[]{:S(2)}) collective-permute-start(bf16[256,1024]{0,1:T(8,128)(2,1)S(1)} %bitcast.256), channel_id=1, source_target_pairs={{0,1},{1,0},{2,3},{3,2},{4,5},{5,4},{6,7},{7,6},{8,9},{9,8},{10,11... | collective-permute-start | bytes 1572872 | tf_op jit(solution)/shard_map/ppermute | solution.py:16
  415.8 18.5 %collective-permute-start.72 = (bf16[512,256]{1,0:T(8,128)(2,1)S(1)}, bf16[512,256]{1,0:T(8,128)(2,1)S(1)}, u32[]{:S(2)}, u32[]{:S(2)}) collective-permute-start(bf16[512,256]{1,0:T(8,128)(2,1)S(1)} %slice.337), channel_id=1, source_target_pairs={{0,4},{4,0},{1,5},{5,1},{2,6},{6,2},{3,7},{7,3},{8,12},{12,8},{9,1... | collective-permute-start | bytes 786440 | tf_op jit(solution)/shard_map/ppermute | solution.py:16
  421.6 16.4 %collective-permute-start.60 = (bf16[512,1024]{0,1:T(8,128)(2,1)S(1)}, bf16[512,1024]{0,1:T(8,128)(2,1)S(1)}, u32[]{:S(2)}, u32[]{:S(2)}) collective-permute-start(bf16[512,1024]{0,1:T(8,128)(2,1)S(1)} %slice.435), channel_id=1, source_target_pairs={{0,1},{1,0},{2,3},{3,2},{4,5},{5,4},{6,7},{7,6},{8,9},{9,8},{10,11... | collective-permute-start | bytes 3145736 | tf_op jit(solution)/shard_map/ppermute | solution.py:16
  424.8 19.1 %collective-permute-start.68 = (bf16[512,768]{1,0:T(8,128)(2,1)S(1)}, bf16[512,768]{1,0:T(8,128)(2,1)S(1)}, u32[]{:S(2)}, u32[]{:S(2)}) collective-permute-start(bf16[512,768]{1,0:T(8,128)(2,1)S(1)} %slice.328), channel_id=1, source_target_pairs={{0,4},{4,0},{1,5},{5,1},{2,6},{6,2},{3,7},{7,3},{8,12},{12,8},{9,1... | collective-permute-start | bytes 2359304 | tf_op jit(solution)/shard_map/ppermute | solution.py:16
  454.4 17.0 %collective-permute-start.70 = (bf16[128,768]{1,0:T(8,128)(2,1)S(1)}, bf16[128,768]{1,0:T(8,128)(2,1)S(1)}, u32[]{:S(2)}, u32[]{:S(2)}) collective-permute-start(bf16[128,768]{1,0:T(8,128)(2,1)S(1)} %get-tuple-element.95), channel_id=1, source_target_pairs={{0,16},{8,24},{16,0},{24,8},{1,17},{9,25},{17,1},{25,9},{2,18},{10... | collective-permute-start | bytes 589832 | tf_op jit(solution)/shard_map/ppermute | solution.py:16
  454.5 17.1 %collective-permute-start.64 = (f32[2,1024]{1,0:T(2,128)S(1)}, f32[2,1024]{1,0:T(2,128)S(1)}, u32[]{:S(2)}, u32[]{:S(2)}) collective-permute-start(f32[2,1024]{1,0:T(2,128)S(1)} %fusion.87), channel_id=1, source_target_pairs={{0,2},{1,3},{2,0},{3,1},{4,6},{5,7},{6,4},{7,5},{8,10},{9,11},{10,... | collective-permute-start | bytes 24584 | tf_op jit(solution)/shard_map/ppermute | solution.py:16
  (121 other events, 2433.7 us)

commit v2 on v1

v2 whole, which is shorter than its diff:
```python
import functools
import jax
import jax.numpy as jnp
from jax import lax
from jax.sharding import PartitionSpec as P
from jax.experimental import pallas as pl
from jax.experimental.pallas import tpu as pltpu

HEADS = 16
HEAD = 64
EPS = 1e-05
NEG = -1e30
F32 = jnp.float32
BF16 = jnp.bfloat16
LANES = 128
QUERIES = 256
STEP = 128
VMEM_LIMIT = 56 * 1024 * 1024


def nt_dot(left, right):
    return lax.dot_general(left, right, (((1,), (1,)), ((), ())), preferred_element_type=F32)


def nn_dot(left, right):
    return lax.dot_general(left, right, (((1,), (0,)), ((), ())), preferred_element_type=F32)


def tn_dot(left, right):
    return lax.dot_general(left, right, (((0,), (0,)), ((), ())), preferred_element_type=F32)


def lane_of(shape):
    return lax.broadcasted_iota(jnp.int32, shape, len(shape) - 1)


def half_swap(values):
    lane = lane_of(values.shape)
    forward = pltpu.roll(values, LANES - HEAD // 2, 1)
    back = pltpu.roll(values, HEAD // 2, 1)
    return jnp.where(lane % HEAD < HEAD // 2, forward, back)


def fwd_kernel(row_parts, weight_parts, heads, *refs):
    tables, refs = refs[0], refs[1:]
    rows, refs = refs[:row_parts], refs[row_parts:]
    weights, refs = refs[:weight_parts], refs[weight_parts:]
    outs_w, refs = refs[:weight_parts], refs[weight_parts:]
    cosine, sine, seg_row, seg_wide, feature, coef = refs[:6]
    q_aug, k_aug, v_out, mixed_out, lse_out, keep_out, send_out = refs[6:13]
    full, out_full, mixed_wide, v_turn = refs[13:]
    pairs = heads // 2
    proj = heads * HEAD
    length = q_aug.shape[1]
    block = weights[0].shape[0]
    part = rows[0].shape[0]
    share = part // 2
    for i in range(weight_parts):
        full[i * block : (i + 1) * block, :] = weights[i][...]
        out_full[i * block : (i + 1) * block, :] = outs_w[i][...]
    for p in range(row_parts):
        raw = nn_dot(rows[p][...], full[...])
        for k in range(2):
            piece = raw[k * share : (k + 1) * share]
            start = pl.multiple_of(tables[0, 2 * p + k] * share, share)
            at = pl.ds(start, share)
            cos_now, sin_now, feat = cosine[at, :], sine[at, :], feature[at, :].astype(F32)
            lane = lane_of((share, LANES))
            for pair in range(pairs):
                low = pair * LANES
                q = piece[:, low : low + LANES]
                q = (q * cos_now + half_swap(q) * sin_now).astype(BF16).astype(F32) * HEAD**-0.5
                kk = piece[:, proj + low : proj + low + LANES]
                kk = kk * cos_now + half_swap(kk) * sin_now
                v_out[pair, at, :] = piece[:, 2 * proj + low : 2 * proj + low + LANES].astype(BF16)
                for odd in range(2):
                    head = 2 * pair + odd
                    q_now = pltpu.roll(q, HEAD, 1) if odd else q
                    k_now = pltpu.roll(kk, HEAD, 1) if odd else kk
                    q_feat = feat * coef[head : head + 1, :]
                    q_aug[head, at, :] = jnp.where(lane < HEAD, q_now, q_feat).astype(BF16)
                    k_aug[head, at, :] = jnp.where(lane < HEAD, k_now, feat).astype(BF16)
    for pair in range(pairs):
        for b in range(length // LANES):
            tile = v_out[pair, b * LANES : (b + 1) * LANES, :].astype(F32)
            v_turn[pair, :, b * LANES : (b + 1) * LANES] = tile.T.astype(BF16)

    def query_block(b, carry):
        at = pl.ds(pl.multiple_of(b * QUERIES, QUERIES), QUERIES)
        seg_q = seg_row[pl.ds(b, 1), :]
        first = pl.multiple_of(tables[1, b] * LANES, LANES)
        for kind in range(1, length // STEP + 1):

            @pl.when(tables[2, b] == kind)
            def _(kind=kind):
                win = pl.ds(first, kind * STEP)
                keep = seg_wide[win, :] == seg_q
                scores = [nt_dot(k_aug[h, win, :], q_aug[h, at, :]) for h in range(heads)]
                probs, totals = [], []
                for head in range(heads):
                    s = jnp.where(keep, scores[head], NEG)
                    top = jnp.max(s, axis=0, keepdims=True)
                    p = jnp.exp(s - top)
                    total = jnp.sum(p, axis=0, keepdims=True)
                    probs.append(p.astype(BF16))
                    totals.append(total)
                    lse_out[head, pl.ds(b, 1), :] = top + jnp.log(total)
                for pair in range(pairs):
                    outs = []
                    for odd in range(2):
                        head = 2 * pair + odd
                        turn = v_turn[pair, odd * HEAD : (odd + 1) * HEAD, win]
                        outs.append(nn_dot(turn, probs[head]) / totals[head])
                    mixed = jnp.concatenate(outs, axis=0).T
                    mixed_wide[at, pair * LANES : (pair + 1) * LANES] = mixed

        return carry

    lax.fori_loop(0, length // QUERIES, query_block, 0)
    for slot in range(2 * row_parts):
        start = pl.multiple_of(tables[0, slot] * share, share)
        piece = mixed_wide[pl.ds(start, share), :]
        mixed_out[slot * share : (slot + 1) * share, :] = piece.astype(BF16)
    half = row_parts // 2
    for p in range(row_parts):
        back = nt_dot(mixed_out[p * part : (p + 1) * part, :], out_full[...])
        if p < half:
            keep_out[p * part : (p + 1) * part, :] = back
        else:
            send_out[(p - half) * part : (p - half + 1) * part, :] = back.astype(BF16)


def vmem():
    return pl.BlockSpec(memory_space=pltpu.VMEM)


def smem():
    return pl.BlockSpec(memory_space=pltpu.SMEM)


def attention_forward(tables, rows, weights, outs_w, cosine, sine, seg_row, seg_wide, feature, coef, heads):
    proj = heads * HEAD
    length = cosine.shape[0]
    width = rows[0].shape[1]
    shapes = (
        jax.ShapeDtypeStruct((heads, length, LANES), BF16),
        jax.ShapeDtypeStruct((heads, length, LANES), BF16),
        jax.ShapeDtypeStruct((heads // 2, length, LANES), BF16),
        jax.ShapeDtypeStruct((length, proj), BF16),
        jax.ShapeDtypeStruct((heads, length // QUERIES, QUERIES), F32),
        jax.ShapeDtypeStruct((length // 2, width), F32),
        jax.ShapeDtypeStruct((length // 2, width), BF16),
    )
    count = len(rows) + 2 * len(weights) + 6
    return pl.pallas_call(
        functools.partial(fwd_kernel, len(rows), len(weights), heads),
        out_shape=shapes,
        in_specs=[smem()] + [vmem()] * count,
        out_specs=[vmem()] * 7,
        scratch_shapes=[
            pltpu.VMEM((width, 3 * proj), BF16),
            pltpu.VMEM((width, proj), BF16),
            pltpu.VMEM((length, proj), F32),
            pltpu.VMEM((heads // 2, LANES, length), BF16),
        ],
        compiler_params=pltpu.CompilerParams(vmem_limit_bytes=VMEM_LIMIT),
        cost_estimate=pl.CostEstimate(
            flops=2 * length * width * 3 * proj, bytes_accessed=8 << 20, transcendentals=length * length * heads // 2
        ),
        name="attn_fwd",
    )(tables, *rows, *weights, *outs_w, cosine, sine, seg_row, seg_wide, feature, coef)


def bwd_kernel(row_parts, weight_parts, heads, *refs):
    tables, refs = refs[0], refs[1:]
    rows, refs = refs[:row_parts], refs[row_parts:]
    outs_w, refs = refs[:weight_parts], refs[weight_parts:]
    weights, refs = refs[:weight_parts], refs[weight_parts:]
    q_aug, k_aug, v_in, lse, cosine, sine, seg_row, seg_wide, hot_rows = refs[:9]
    keep_out, send_out, d_qkv_out, bias_out = refs[9:13]
    full, out_full, d_out, k_turn, dq_acc, dk_acc, dv_acc = refs[13:]
    pairs = heads // 2
    proj = heads * HEAD
    length = q_aug.shape[1]
    block = weights[0].shape[0]
    part = rows[0].shape[0]
    share = part // 2
    for i in range(weight_parts):
        full[i * block : (i + 1) * block, :] = weights[i][...]
        out_full[i * block : (i + 1) * block, :] = outs_w[i][...]
    for p in range(row_parts):
        raw = nn_dot(rows[p][...], out_full[...]).astype(BF16)
        for k in range(2):
            start = pl.multiple_of(tables[0, 2 * p + k] * share, share)
            d_out[pl.ds(start, share), :] = raw[k * share : (k + 1) * share]
    for head in range(heads):
        for b in range(length // LANES):
            tile = k_aug[head, b * LANES : (b + 1) * LANES, :].astype(F32)
            k_turn[head, :, b * LANES : (b + 1) * LANES] = tile.T.astype(BF16)
    dk_acc[...] = jnp.zeros(dk_acc.shape, F32)
    dv_acc[...] = jnp.zeros(dv_acc.shape, F32)
    bias_out[...] = jnp.zeros(bias_out.shape, F32)

    def query_block(b, carry):
        at = pl.ds(pl.multiple_of(b * QUERIES, QUERIES), QUERIES)
        seg_q = seg_row[pl.ds(b, 1), :]
        hot = hot_rows[:, at]
        first = pl.multiple_of(tables[1, b] * LANES, LANES)
        for kind in range(1, length // STEP + 1):

            @pl.when(tables[2, b] == kind)
            def _(kind=kind):
                win = pl.ds(first, kind * STEP)
                keep = seg_wide[win, :] == seg_q
                owns = []
                for head in range(heads):
                    chunk = slice(head // 2 * LANES, (head // 2 + 1) * LANES)
                    d_pair = d_out[at, chunk]
                    lane = lane_of(d_pair.shape)
                    owns.append(jnp.where((lane >= HEAD) == (head % 2 == 1), d_pair, jnp.zeros_like(d_pair)))
                turned = []
                for base in range(0, heads, 2):
                    group = range(base, base + 2)
                    s = [nt_dot(k_aug[h, win, :], q_aug[h, at, :]) for h in group]
                    dp = [nt_dot(v_in[h // 2, win, :], owns[h]) for h in group]
                    low, ds = [], []
                    for i, h in enumerate(group):
                        p = jnp.exp(jnp.where(keep, s[i] - lse[h, pl.ds(b, 1), :], NEG))
                        low.append(p.astype(BF16))
                        ds.append((p * (dp[i] - jnp.sum(p * dp[i], axis=0, keepdims=True))).astype(BF16))
                    for i, h in enumerate(group):
                        if i % 2 == 0:
                            both = jnp.concatenate(low[i : i + 2], axis=1)
                            dv_acc[h // 2, win, :] += nn_dot(both, jnp.concatenate(owns[h : h + 2], axis=0))
                        dk_acc[h, win, :] += nn_dot(ds[i], q_aug[h, at, :])
                        dq = nn_dot(k_turn[h, :, win], ds[i])
                        turned.append(dq[:HEAD])
                        sums = dq[HEAD : HEAD + 8]
                        bias_out[h] += jnp.concatenate([sums * hot[:8], sums * hot[8:]], axis=0)
                for pair in range(pairs):
                    chunk = slice(pair * LANES, (pair + 1) * LANES)
                    dq_acc[at, chunk] = jnp.concatenate(turned[2 * pair : 2 * pair + 2], axis=0).T * HEAD**-0.5

        return carry

    lax.fori_loop(0, length // QUERIES, query_block, 0)
    for p in range(row_parts):
        for k in range(2):
            slot = 2 * p + k
            at = pl.ds(pl.multiple_of(tables[0, slot] * share, share), share)
            to = slice(slot * share, (slot + 1) * share)
            cos_now, sin_now = cosine[at, :], sine[at, :]
            lane = lane_of((share, LANES))
            for pair in range(pairs):
                low = pair * LANES
                dq = dq_acc[at, low : low + LANES]
                dk = jnp.where(lane < HEAD, dk_acc[2 * pair, at, :], pltpu.roll(dk_acc[2 * pair + 1, at, :], HEAD, 1))
                d_qkv_out[to, low : low + LANES] = (dq * cos_now - half_swap(dq) * sin_now).astype(BF16)
                d_qkv_out[to, proj + low : proj + low + LANES] = (dk * cos_now - half_swap(dk) * sin_now).astype(BF16)
                d_qkv_out[to, 2 * proj + low : 2 * proj + low + LANES] = dv_acc[pair, at, :].astype(BF16)
        part_rows = d_qkv_out[p * part : (p + 1) * part, :]
        back = nt_dot(part_rows, full[...])
        half = row_parts // 2
        if p < half:
            keep_out[p * part : (p + 1) * part, :] = back
        else:
            send_out[(p - half) * part : (p - half + 1) * part, :] = back.astype(BF16)


def attention_backward(tables, rows, outs_w, weights, q_aug, k_aug, v_in, lse, cosine, sine, seg_row, seg_wide, hot_rows, heads):
    proj = heads * HEAD
    length = cosine.shape[0]
    width = rows[0].shape[1]
    shapes = (
        jax.ShapeDtypeStruct((length // 2, width), F32),
        jax.ShapeDtypeStruct((length // 2, width), BF16),
        jax.ShapeDtypeStruct((length, 3 * proj), BF16),
        jax.ShapeDtypeStruct((heads, 16, QUERIES), F32),
    )
    count = len(rows) + 2 * len(weights) + 9
    return pl.pallas_call(
        functools.partial(bwd_kernel, len(rows), len(weights), heads),
        out_shape=shapes,
        in_specs=[smem()] + [vmem()] * count,
        out_specs=[vmem()] * 4,
        scratch_shapes=[
            pltpu.VMEM((width, 3 * proj), BF16),
            pltpu.VMEM((width, proj), BF16),
            pltpu.VMEM((length, proj), BF16),
            pltpu.VMEM((heads, LANES, length), BF16),
            pltpu.VMEM((length, proj), F32),
            pltpu.VMEM((heads, length, LANES), F32),
            pltpu.VMEM((heads // 2, length, LANES), F32),
        ],
        compiler_params=pltpu.CompilerParams(vmem_limit_bytes=VMEM_LIMIT),
        cost_estimate=pl.CostEstimate(
            flops=2 * length * width * 4 * proj, bytes_accessed=12 << 20, transcendentals=length * length * heads // 2
        ),
        name="attn_bwd",
    )(tables, *rows, *outs_w, *weights, q_aug, k_aug, v_in, lse, cosine, sine, seg_row, seg_wide, hot_rows)


def attention_tables(segments, variates, times, variate_bias, order, share):
    length = segments.shape[0]
    heads = variate_bias.shape[1]
    count = length // QUERIES
    half = HEAD // 2
    frequency = 10000.0 ** (-2.0 * jnp.arange(half, dtype=F32) / HEAD)
    angles = times.astype(F32)[:, None] * frequency
    cos_half, sin_half = jnp.cos(angles), jnp.sin(angles)
    cosine = jnp.concatenate([cos_half] * 4, axis=1)
    sine = jnp.concatenate([-sin_half, sin_half] * 2, axis=1)
    seg_row = segments.reshape(count, QUERIES)
    seg_wide = jnp.broadcast_to(segments[:, None], (length, QUERIES))
    lane = jnp.arange(LANES)
    live = (lane >= HEAD) & (lane < HEAD + 12)
    feature = ((variates[:, None] == (lane % 4)[None, :]) & live[None, :]).astype(BF16)
    gap = variate_bias[0] - variate_bias[1]
    high = lax.reduce_precision(gap, 8, 7)
    mid = lax.reduce_precision(gap - high, 8, 7)
    low = lax.reduce_precision(gap - high - mid, 8, 7)
    parts = jnp.repeat(jnp.stack([high, mid, low], axis=1), 4, axis=1)
    coef = jnp.pad(parts, ((0, -heads % 8), (HEAD, LANES - HEAD - 12)))
    kinds = jnp.arange(4)
    same = (variates[None, :] == kinds[:, None]).astype(F32)
    zeros = jnp.zeros_like(same)
    hot_rows = jnp.concatenate([same, zeros, 1.0 - same, zeros], axis=0)
    ends = segments.reshape(count, QUERIES)
    start = jnp.sum(segments[None, :] < ends[:, :1], axis=1)
    stop = jnp.sum(segments[None, :] <= ends[:, -1:], axis=1)
    first = start // LANES
    kind = (stop - first * LANES + STEP - 1) // STEP
    first = jnp.minimum(first, (length - kind * STEP) // LANES)
    size = max(count, order.shape[0])
    pad = lambda a: jnp.pad(a.astype(jnp.int32), (0, size - a.shape[0]))
    tables = jnp.stack([pad(order), pad(first), pad(kind)])
    return tables, cosine, sine, seg_row, seg_wide, feature, coef, hot_rows

def ffn_kernel(row_parts, weight_parts, *refs):
    rows, refs = refs[:row_parts], refs[row_parts:]
    grads, refs = refs[:row_parts], refs[row_parts:]
    gates, refs = refs[:weight_parts], refs[weight_parts:]
    ups, refs = refs[:weight_parts], refs[weight_parts:]
    downs, refs = refs[:weight_parts], refs[weight_parts:]
    act_out, d_gate_out, d_up_out, keep_out, send_out, gate_full, up_full, down_full = refs
    block = gates[0].shape[0]
    part = rows[0].shape[0]
    for i in range(weight_parts):
        at = slice(i * block, (i + 1) * block)
        gate_full[at, :] = gates[i][...]
        up_full[at, :] = ups[i][...]
        down_full[at, :] = downs[i][...]
    half = row_parts // 2
    for p in list(range(half, row_parts)) + list(range(half)):
        at = slice(p * part, (p + 1) * part)
        gate = nn_dot(rows[p][...], gate_full[...])
        up = nn_dot(rows[p][...], up_full[...])
        d_act = nn_dot(grads[p][...], down_full[...])
        sig = 1.0 / (1.0 + jnp.exp(-gate))
        silu = gate * sig
        act_out[at, :] = (silu * up).astype(BF16)
        d_gate_out[at, :] = (d_act * up * (sig + silu * (1.0 - sig))).astype(BF16)
        d_up_out[at, :] = (d_act * silu).astype(BF16)
        back = nt_dot(d_gate_out[at, :], gate_full[...]) + nt_dot(d_up_out[at, :], up_full[...])
        if p < half:
            keep_out[at, :] = back
        else:
            send_out[(p - half) * part : (p - half + 1) * part, :] = back.astype(BF16)


def ffn_middle(rows, grads, gates, ups, downs):
    part, width = rows[0].shape
    length = part * len(rows)
    hidden = gates[0].shape[1]
    units = jax.ShapeDtypeStruct((length, hidden), BF16)
    return pl.pallas_call(
        functools.partial(ffn_kernel, len(rows), len(gates)),
        out_shape=(
            units,
            units,
            units,
            jax.ShapeDtypeStruct((length // 2, width), F32),
            jax.ShapeDtypeStruct((length // 2, width), BF16),
        ),
        in_specs=[vmem()] * (2 * len(rows) + 3 * len(gates)),
        out_specs=[vmem()] * 5,
        scratch_shapes=[pltpu.VMEM((width, hidden), BF16)] * 3,
        compiler_params=pltpu.CompilerParams(vmem_limit_bytes=VMEM_LIMIT),
        cost_estimate=pl.CostEstimate(
            flops=10 * length * width * hidden, bytes_accessed=20 << 20, transcendentals=length * hidden
        ),
        name="ffn_middle",
    )(*rows, *grads, *gates, *ups, *downs)


def grad_kernel(row_parts, blocks, *refs):
    rows, refs = refs[:row_parts], refs[row_parts:]
    right, refs = refs[0], refs[1:]
    keeps, send, left = refs[:blocks], refs[blocks], refs[blocks + 1]
    part, width = rows[0].shape
    for p in range(row_parts):
        for c in range(width // LANES):
            tile = rows[p][:, c * LANES : (c + 1) * LANES].astype(F32)
            left[c * LANES : (c + 1) * LANES, p * part : (p + 1) * part] = tile.T.astype(BF16)
    step = width // 4
    block = keeps[0].shape[0]
    send[: step, :] = nn_dot(left[2 * step : 3 * step, :], right[...]).astype(BF16)
    send[step :, :] = nn_dot(left[3 * step :, :], right[...]).astype(BF16)
    for s in range(2):
        both = nn_dot(left[s * step : (s + 1) * step, :], right[...])
        for k in range(step // block):
            keeps[s * step // block + k][...] = both[k * block : (k + 1) * block].astype(keeps[0].dtype)


def weight_partials(rows, right, blocks):
    part, width = rows[0].shape
    length, cols = right.shape
    block = width // (2 * blocks)
    return pl.pallas_call(
        functools.partial(grad_kernel, len(rows), blocks),
        out_shape=(jax.ShapeDtypeStruct((block, cols), BF16),) * blocks
        + (jax.ShapeDtypeStruct((width // 2, cols), BF16),),
        in_specs=[vmem()] * (len(rows) + 1),
        out_specs=[vmem()] * (blocks + 1),
        scratch_shapes=[pltpu.VMEM((width, length), BF16)],
        compiler_params=pltpu.CompilerParams(vmem_limit_bytes=VMEM_LIMIT),
        cost_estimate=pl.CostEstimate(
            flops=2 * length * width * cols, bytes_accessed=8 << 20, transcendentals=0
        ),
        name="weight_partials",
    )(*rows, right)


def hop(values, axis, flip):
    size = lax.axis_size(axis)
    return lax.ppermute(values, axis, [(i, i ^ flip) for i in range(size)])


def swap_blocks(values, axis, index, size):
    shape = values.shape
    bit = 1
    while bit < size:
        split = shape[:axis] + (size // (2 * bit), 2, bit) + shape[axis + 1 :]
        cut = values.reshape(split)
        cut = jnp.where((index & bit) != 0, jnp.flip(cut, axis + 1), cut)
        values = cut.reshape(shape)
        bit *= 2
    return values


def gather_weight(block):
    nz = lax.axis_size("fsdp")
    mine = [block] + [hop(block, "fsdp", k) for k in range(1, nz)]
    return mine + [hop(piece, "ctx", 1) for piece in mine]


def scatter_weight(partials):
    keeps, send = partials[:-1], partials[-1]
    rows = keeps[0].shape[0]
    other = hop(send, "ctx", 1)
    out = None
    for k, keep in enumerate(keeps):
        total = keep.astype(F32) + other[k * rows : (k + 1) * rows].astype(F32)
        if k == 0:
            out = total
        else:
            out = out + hop(total.astype(BF16), "fsdp", k).astype(F32)
    return out


def gather_rows(block):
    nt = lax.axis_size("tp")
    mine = [block] + [hop(block, "tp", 2 * k) for k in range(1, nt // 2)]
    return mine + [hop(piece, "tp", 1) for piece in mine]


def scatter_rows(keep, send):
    nt = lax.axis_size("tp")
    rows = 2 * keep.shape[0] // nt
    other = hop(send, "tp", 1)
    total = keep + other.astype(F32)
    out = total[:rows]
    for k in range(1, nt // 2):
        out = out + hop(total[k * rows : (k + 1) * rows].astype(BF16), "tp", 2 * k).astype(F32)
    return out


def psum_over(values, axes):
    for axis in axes:
        bit = 1
        while bit < lax.axis_size(axis):
            values = values + hop(values, axis, bit)
            bit *= 2
    return values


def inverse_rms(values):
    return lax.rsqrt(jnp.mean(values * values, axis=-1, keepdims=True) + EPS)


def norm_back(values, inv, gain, grad):
    scaled = grad * gain
    normed = values * inv
    d_gain = jnp.sum(grad * normed, axis=0, keepdims=True)
    d_values = inv * (scaled - normed * jnp.mean(scaled * normed, axis=-1, keepdims=True))
    return d_values, d_gain


def shards(
    layer_in,
    attn_gain,
    ffn_gain,
    query_weight,
    key_weight,
    value_weight,
    out_weight,
    variate_bias,
    gate_weight,
    up_weight,
    down_weight,
    segment_ids,
    variate_ids,
    time_ids,
    out_grad,
):
    seq_count, share, width = layer_in.shape
    nz, nx, nt = lax.axis_size("fsdp"), lax.axis_size("ctx"), lax.axis_size("tp")
    iz, ix, it = lax.axis_index("fsdp"), lax.axis_index("ctx"), lax.axis_index("tp")
    assert nx == 2 and seq_count == nx
    length = segment_ids.shape[1]
    heads = variate_bias.shape[1]
    proj = heads * HEAD

    def to_slots(values):
        cut = values.reshape(values.shape[0], nz, nx, width // (nz * nx))
        cut = swap_blocks(swap_blocks(cut, 1, iz, nz), 2, ix, nx)
        return cut.transpose(0, 2, 1, 3).reshape(values.shape)

    def from_slots(values):
        cut = values.reshape(values.shape[0], nx, nz, width // (nz * nx)).transpose(0, 2, 1, 3)
        return swap_blocks(swap_blocks(cut, 1, iz, nz), 2, ix, nx).reshape(values.shape)

    def own_sequence(values):
        mine = lax.dynamic_index_in_dim(values, ix, 0, keepdims=False)
        other = lax.dynamic_index_in_dim(values, 1 - ix, 0, keepdims=False)
        return to_slots(jnp.concatenate([mine, hop(other, "ctx", 1)], axis=0))

    def both_sequences(values):
        values = from_slots(values)
        mine, other = values[:share], hop(values[share:], "ctx", 1)
        first = jnp.where(ix == 0, mine, other)
        second = jnp.where(ix == 0, other, mine)
        return jnp.stack([first, second])

    def own_ids(table):
        return lax.dynamic_index_in_dim(table, ix, 0, keepdims=False)

    order = jnp.arange(nx * nt).reshape(nx, nt // 2, 2)
    order = swap_blocks(swap_blocks(swap_blocks(order, 0, ix, nx), 1, it // 2, nt // 2), 2, it % 2, 2)
    order = order.transpose(2, 1, 0).reshape(nx * nt)
    tables, cosine, sine, seg_row, seg_wide, feature, coef, hot_rows = attention_tables(
        own_ids(segment_ids), own_ids(variate_ids), own_ids(time_ids), variate_bias, order, share
    )
    gain_one = to_slots(attn_gain.astype(F32)[None])
    gain_two = to_slots(ffn_gain.astype(F32)[None])
    low_inputs = own_sequence(layer_in)
    inputs = low_inputs.astype(F32)
    inv_one = inverse_rms(inputs)
    rows_one = gather_rows((inputs * inv_one * gain_one).astype(BF16))
    qkv_w = gather_weight(jnp.concatenate([query_weight, key_weight, value_weight], axis=1))
    out_w = gather_weight(out_weight)
    gate_w = gather_weight(gate_weight)
    up_w = gather_weight(up_weight)
    down_w = gather_weight(down_weight)
    grads = own_sequence(out_grad)
    grad_rows = gather_rows(grads)

    q_aug, k_aug, v_rows, mixed, lse, keep, send = attention_forward(
        tables, rows_one, qkv_w, out_w, cosine, sine, seg_row, seg_wide, feature, coef, heads
    )
    hidden = inputs + scatter_rows(keep, send)
    inv_two = inverse_rms(hidden)
    rows_two = gather_rows((hidden * inv_two * gain_two).astype(BF16))
    act, d_gate, d_up, keep, send = ffn_middle(rows_two, grad_rows, gate_w, up_w, down_w)
    d_normed_two = scatter_rows(keep, send)
    down_grad = scatter_weight(weight_partials(grad_rows, act, nz))
    gate_grad = scatter_weight(weight_partials(rows_two, d_gate, nz))
    up_grad = scatter_weight(weight_partials(rows_two, d_up, nz))

    down_full = jnp.concatenate(down_w, axis=0)
    ffn = lax.dot_general(act, down_full, (((1,), (1,)), ((), ())), preferred_element_type=F32)
    ffn = scatter_rows(ffn[: length // 2], ffn[length // 2 :].astype(BF16))
    layer_out = both_sequences((hidden + ffn).astype(BF16))

    d_hidden_norm, d_gain_two = norm_back(hidden, inv_two, gain_two, d_normed_two)
    d_hidden = grads.astype(F32) + d_hidden_norm
    branch_rows = gather_rows(d_hidden.astype(BF16))
    keep, send, d_qkv, bias_parts = attention_backward(
        tables, branch_rows, out_w, qkv_w, q_aug, k_aug, v_rows, lse, cosine, sine, seg_row, seg_wide, hot_rows, heads
    )
    d_normed_one = scatter_rows(keep, send)
    out_weight_grad = scatter_weight(weight_partials(branch_rows, mixed, nz))
    qkv_grad = scatter_weight(weight_partials(rows_one, d_qkv, nz))
    sums = jnp.sum(bias_parts, axis=2)
    bias_grad = jnp.stack([jnp.sum(sums[:, :8], axis=1), jnp.sum(sums[:, 8:], axis=1)])
    bias_grad = psum_over(bias_grad, ("ctx", "fsdp"))

    d_input_norm, d_gain_one = norm_back(inputs, inv_one, gain_one, d_normed_one)
    in_grad = both_sequences((d_hidden + d_input_norm).astype(BF16))
    gain_grads = from_slots(jnp.concatenate([d_gain_one, d_gain_two], axis=0))
    gain_grads = psum_over(gain_grads, ("tp", "ctx", "fsdp"))
    return (
        layer_out,
        in_grad,
        gain_grads[0],
        gain_grads[1],
        qkv_grad[:, :proj],
        qkv_grad[:, proj : 2 * proj],
        qkv_grad[:, 2 * proj :],
        out_weight_grad,
        bias_grad,
        gate_grad,
        up_grad,
        down_grad,
    )


def solution(mesh):
    rows = P("fsdp", ("ctx", "tp"), None)
    weight = P(("fsdp", "ctx"), "tp")
    ids = P("fsdp", None)
    bias = P(None, "tp")
    in_specs = (rows, P(), P()) + (weight,) * 4 + (bias,) + (weight,) * 3 + (ids,) * 3 + (rows,)
    out_specs = (rows, rows, P(), P()) + (weight,) * 4 + (bias,) + (weight,) * 3
    return jax.shard_map(shards, mesh=mesh, in_specs=in_specs, out_specs=out_specs, check_vma=False)
```

time: 498 us -> 476 us (0.956)
  Pallas kernels: 0 us -> 78.6 us
  waiting for transfers between devices: 215 us -> 139 us
  matrix products: 79.4 us -> 3.96 us
  starting transfers between devices: 105 us -> 158 us
  local copies, waits for them, and re-layouts: 48.3 us -> 37.2 us
  other arithmetic: 38.8 us -> 48.3 us
    pallas_call x0 -> x8, Pallas kernels: none -> 78.6 us  [the longest x5 26.1 us: weight_partials(): pl.pallas_call(functools.partial(grad_kernel, len(rows), blocks), out_sha...]
    ppermute x91 -> x87, waiting for transfers between devices: 215 us -> 139 us  [hop(): return lax.ppermute(values, axis, [(i, i ^ flip) for i in range(size)])]
    dot_general x21 -> x1, matrix products: 79.4 us -> 3.96 us  [shards(): lax.dot_general(act, down_full, (((1,), (1,)), ((), ())), preferred_eleme...]
    ppermute x91 -> x87, starting transfers between devices: 105 us -> 158 us  [hop(): return lax.ppermute(values, axis, [(i, i ^ flip) for i in range(size)])]
    unnamed x196 -> x173, local copies, waits for them, and re-layouts: 33.7 us -> 12.3 us
    reduce_sum x4 -> x5, other arithmetic: 21.3 us -> 2.77 us  [the longest x2 1.45 us: norm_back(): d_gain = jnp.sum(grad * normed, axis=0, keepdims=True)]
    add x20 -> x17, other arithmetic: 5.8 us -> 12 us  [the longest x5 6.98 us: scatter_weight(): out = out + hop(total.astype(BF16), 'fsdp', k).astype(F32)]
  transfers between devices with their start and end apart: 91 -> 87, of which waited for: 40 -> 34; matrix products, arithmetic and copies ran while one was open for 22% -> 16% of each run, Pallas kernels for 0% -> 4%
where the time goes in v2:
time: 476 us; the launch traced here: 468 us
  starting transfers between devices  158 us (33%)
  waiting for transfers between devices  139 us (29%)
  Pallas kernels  78.6 us (17%)
  other arithmetic  48.3 us (10%)
  local copies, waits for them, and re-layouts  37.2 us (8%)
    ppermute x87, starting transfers between devices, hop(): return lax.ppermute(values, axis, [(i, i ^ flip) for i in range(size)])  158 us
    ppermute x87, waiting for transfers between devices, hop(): return lax.ppermute(values, axis, [(i, i ^ flip) for i in range(size)])  139 us
    pallas_call x5, Pallas kernels, weight_partials(): pl.pallas_call(functools.partial(grad_kernel, len(rows), blocks), out_sha...  26.1 us
    pallas_call x1, Pallas kernels, ffn_middle(): pl.pallas_call(functools.partial(ffn_kernel, len(rows), len(gates)), out_...  18.1 us
    pallas_call x1, Pallas kernels, attention_backward(): pl.pallas_call(functools.partial(bwd_kernel, len(rows), len(weights), hea...  17.8 us
    pallas_call x1, Pallas kernels, attention_forward(): pl.pallas_call(functools.partial(fwd_kernel, len(rows), len(weights), hea...  16.6 us
    unnamed x173, local copies, waits for them, and re-layouts  12.3 us
  transfers between devices with their start and end apart: 87, of which 34 were waited for; matrix products, arithmetic and copies ran while one was open for 16% of the time, Pallas kernels for 4%

profile of v2, /device:TPU:0, one launch (start us, length us, event | category | flops | bytes accessed | tf_op | source)
XLA Modules:
  0.0 467.7 jit_solution(2388644998648116718)
XLA Ops:
  0.7 3.1 collective-permute-start.11
  3.8 2.6 collective-permute-start.12
  26.6 3.6 collective-permute-start.6
  37.5 2.9 collective-permute-start.5
  43.3 4.3 collective-permute-done.4.refs_6_.refs_14_
  55.5 4.2 collective-permute-done.8.refs_10_.refs_18_
  59.7 2.6 collective-permute-done.9.refs_11_.refs_19_
  63.6 16.6 %attn_fwd.1 = (bf16[4,1024,128]{2,1,0:T(8,128)(2,1)}, bf16[4,1024,128]{2,1,0:T(8,128)(2,1)}, bf16[2,1024,128]{2,1,0:T(8,128)(2,1)}, bf16[1024,256]{1,0:T(8,128)(...) custom-call(s32[3,8]{1,0:T(4,128)} %pad_add_fusion.refs_0_, ...), custom_call_target="tpu_custom_call" | custom-call | flops 1610612736 | bytes 8388608 | tf_op jit(solution)/shard_map/attn_fwd/pallas_call | solution.py:155
  80.5 2.6 collective-permute-start.42
  88.6 5.2 %collective-permute-done.23 = bf16[128,1024]{0,1:T(8,128)(2,1)} collective-permute-done((bf16[128,1024]{0,1:T(8,128)(2,1)}, bf16[128,1024]{0,1:T(8,128)(2,1)}, u32[]{:S(2)}, u32[]{:S(2)}) %collective-permute-start.23) | collective-permute-done | bytes 262176 | tf_op jit(solution)/shard_map/ppermute | solution.py:436
  99.8 2.4 collective-permute-start.28
  104.2 15.4 %collective-permute-start.34 = (bf16[128,1024]{1,0:T(8,128)(2,1)}, bf16[128,1024]{1,0:T(8,128)(2,1)}, u32[]{:S(2)}, u32[]{:S(2)}) collective-permute-start(bf16[128,1024]{1,0:T(8,128)(2,1)} %refs_16_.1), channel_id=1, source_target_pairs={{0,8},{8,0},{16,24},{24,16},{1,9},{9,1},{17,25},{25,17},{2,10},{10... | collective-permute-start | bytes 786440 | tf_op jit(solution)/shard_map/ppermute | solution.py:436
  121.3 3.4 collective-permute-done.28.refs_10_
  124.7 4.0 collective-permute-start.36
  128.7 3.1 collective-permute-start.30
  133.5 13.5 %collective-permute-done.35.refs_18_ = bf16[128,1024]{1,0:T(8,128)(2,1)S(1)} collective-permute-done((bf16[128,1024]{1,0:T(8,128)(2,1)}, bf16[128,1024]{1,0:T(8,128)(2,1)S(1)}, u32[]{:S(2)}, u32[]{:S(2)}) %collective-permute-start.35) | collective-permute-done | bytes 262176 | tf_op jit(solution)/shard_map/ppermute | solution.py:436
  153.1 5.2 %collective-permute-done.45.refs_29_ = bf16[128,1024]{1,0:T(8,128)(2,1)S(1)} collective-permute-done((bf16[128,1024]{1,0:T(8,128)(2,1)}, bf16[128,1024]{1,0:T(8,128)(2,1)S(1)}, u32[]{:S(2)}, u32[]{:S(2)}) %collective-permute-start.45) | collective-permute-done | bytes 262176 | tf_op jit(solution)/shard_map/ppermute | solution.py:436
  158.6 5.4 %collective-permute-done.46.refs_30_ = bf16[128,1024]{1,0:T(8,128)(2,1)S(1)} collective-permute-done((bf16[128,1024]{1,0:T(8,128)(2,1)}, bf16[128,1024]{1,0:T(8,128)(2,1)S(1)}, u32[]{:S(2)}, u32[]{:S(2)}) %collective-permute-start.46) | collective-permute-done | bytes 262176 | tf_op jit(solution)/shard_map/ppermute | solution.py:436
  165.5 4.1 collective-permute-done.47.refs_31_
  171.1 4.1 collective-permute-done.31.refs_13_
  183.3 3.2 collective-permute-done.33.refs_15_
  187.1 5.0 %collective-permute-done.38.refs_21_ = bf16[128,1024]{1,0:T(8,128)(2,1)S(1)} collective-permute-done((bf16[128,1024]{1,0:T(8,128)(2,1)}, bf16[128,1024]{1,0:T(8,128)(2,1)S(1)}, u32[]{:S(2)}, u32[]{:S(2)}) %collective-permute-start.38) | collective-permute-done | bytes 262176 | tf_op jit(solution)/shard_map/ppermute | solution.py:436
  197.0 5.1 %collective-permute-done.40.refs_23_ = bf16[128,1024]{1,0:T(8,128)(2,1)S(1)} collective-permute-done((bf16[128,1024]{1,0:T(8,128)(2,1)S(1)}, bf16[128,1024]{1,0:T(8,128)(2,1)S(1)}, u32[]{:S(2)}, u32[]{:S(2)}) %collective-permute-start.40) | collective-permute-done | bytes 262176 | tf_op jit(solution)/shard_map/ppermute | solution.py:436
  203.9 18.1 %ffn_middle.1 = (bf16[1024,1024]{1,0:T(8,128)(2,1)}, bf16[1024,1024]{1,0:T(8,128)(2,1)}, bf16[1024,1024]{1,0:T(8,128)(2,1)}, f32[512,1024]{1,0:T(8,128)}, bf16[512,1024]{1,0:T(8,128)(2,1)}) custom-call(bf16[256,1024]{1,0:T(8,128)(2,1)} %copy-done.24, bf16[256,1024]{1,0:T(8,128)(2,1)} %copy-done.66, bf16[256,1024]{1,0:T(8,128)(2,1)} %copy-done.68, ...), custom_call_target="tpu_custom_call" | custom-call | flops 10737418240 | bytes 20971520 | tf_op jit(solution)/shard_map/ffn_middle/pallas_call | solution.py:376
  222.0 5.8 %weight_partials.9 = (bf16[128,1024]{1,0:T(8,128)(2,1)}, bf16[128,1024]{1,0:T(8,128)(2,1)}, bf16[128,1024]{1,0:T(8,128)(2,1)}, bf16[128,1024]{1,0:T(8,128)(2,1)}, bf16[512,1024]{1,0:T(8,128)(2,1)}) custom-call(bf16[256,1024]{1,0:T(8,128)(2,1)} %copy-done.12, bf16[256,1024]{1,0:T(8,128)(2,1)} %copy-done.67, bf16[256,1024]{1,0:T(8,128)(2,1)} %copy-done.69, ...), custom_call_target="tpu_custom_call" | custom-call | flops 2147483648 | bytes 8388608 | tf_op jit(solution)/shard_map/weight_partials/pallas_call | solution.py:419
  229.3 4.0 fusion.24
  236.5 5.7 %weight_partials.8 = (bf16[128,1024]{1,0:T(8,128)(2,1)}, bf16[128,1024]{1,0:T(8,128)(2,1)}, bf16[128,1024]{1,0:T(8,128)(2,1)}, bf16[128,1024]{1,0:T(8,128)(2,1)}, bf16[512,1024]{1,0:T(8,128)(2,1)}) custom-call(bf16[256,1024]{1,0:T(8,128)(2,1)} %copy-done.24, bf16[256,1024]{1,0:T(8,128)(2,1)} %copy-done.66, bf16[256,1024]{1,0:T(8,128)(2,1)} %copy-done.68, ...), custom_call_target="tpu_custom_call" | custom-call | flops 2147483648 | bytes 8388608 | tf_op jit(solution)/shard_map/weight_partials/pallas_call | solution.py:419
  243.6 6.1 %weight_partials.7 = (bf16[128,1024]{1,0:T(8,128)(2,1)}, bf16[128,1024]{1,0:T(8,128)(2,1)}, bf16[128,1024]{1,0:T(8,128)(2,1)}, bf16[128,1024]{1,0:T(8,128)(2,1)}, bf16[512,1024]{1,0:T(8,128)(2,1)}) custom-call(bf16[256,1024]{1,0:T(8,128)(2,1)} %copy-done.24, bf16[256,1024]{1,0:T(8,128)(2,1)} %copy-done.66, bf16[256,1024]{1,0:T(8,128)(2,1)} %copy-done.68, ...), custom_call_target="tpu_custom_call" | custom-call | flops 2147483648 | bytes 8388608 | tf_op jit(solution)/shard_map/weight_partials/pallas_call | solution.py:419
  251.3 3.0 collective-permute-done.83
  255.7 10.2 %collective-permute-start.84 = (bf16[128,1024]{1,0:T(8,128)(2,1)S(1)}, bf16[128,1024]{1,0:T(8,128)(2,1)S(1)}, u32[]{:S(2)}, u32[]{:S(2)}) collective-permute-start(bf16[128,1024]{1,0:T(8,128)(2,1)S(1)} %get-tuple-element.114), channel_id=1, source_target_pairs={{0,8},{8,0},{16,24},{24,16},{1,9},{9,1},{17,25},{25,17},{2,10},{10... | collective-permute-start | bytes 786440 | tf_op jit(solution)/shard_map/ppermute | solution.py:436
  268.1 8.6 %collective-permute-done.79 = bf16[512,1024]{1,0:T(8,128)(2,1)} collective-permute-done((bf16[512,1024]{1,0:T(8,128)(2,1)}, bf16[512,1024]{1,0:T(8,128)(2,1)}, u32[]{:S(2)}, u32[]{:S(2)}) %collective-permute-start.79) | collective-permute-done | bytes 1048608 | tf_op jit(solution)/shard_map/ppermute | solution.py:436
  279.8 9.5 %collective-permute-start.80 = (bf16[128,1024]{1,0:T(8,128)(2,1)S(1)}, bf16[128,1024]{1,0:T(8,128)(2,1)S(1)}, u32[]{:S(2)}, u32[]{:S(2)}) collective-permute-start(bf16[128,1024]{1,0:T(8,128)(2,1)S(1)} %get-tuple-element.117), channel_id=1, source_target_pairs={{0,8},{8,0},{16,24},{24,16},{1,9},{9,1},{17,25},{25,17},{2,10},{10... | collective-permute-start | bytes 786440 | tf_op jit(solution)/shard_map/ppermute | solution.py:436
  289.8 5.8 %collective-permute-done.75 = bf16[512,1024]{1,0:T(8,128)(2,1)S(1)} collective-permute-done((bf16[512,1024]{1,0:T(8,128)(2,1)}, bf16[512,1024]{1,0:T(8,128)(2,1)S(1)}, u32[]{:S(2)}, u32[]{:S(2)}) %collective-permute-start.75) | collective-permute-done | bytes 1048608 | tf_op jit(solution)/shard_map/ppermute | solution.py:436
  295.6 10.4 %collective-permute-start.81 = (bf16[128,1024]{1,0:T(8,128)(2,1)S(1)}, bf16[128,1024]{1,0:T(8,128)(2,1)S(1)}, u32[]{:S(2)}, u32[]{:S(2)}) collective-permute-start(bf16[128,1024]{1,0:T(8,128)(2,1)S(1)} %get-tuple-element.119), channel_id=1, source_target_pairs={{0,16},{8,24},{16,0},{24,8},{1,17},{9,25},{17,1},{25,9},{2,18},{10... | collective-permute-start | bytes 786440 | tf_op jit(solution)/shard_map/ppermute | solution.py:436
  314.9 15.3 %collective-permute-done.81 = bf16[128,1024]{1,0:T(8,128)(2,1)S(1)} collective-permute-done((bf16[128,1024]{1,0:T(8,128)(2,1)S(1)}, bf16[128,1024]{1,0:T(8,128)(2,1)S(1)}, u32[]{:S(2)}, u32[]{:S(2)}) %collective-permute-start.81) | collective-permute-done | bytes 262176 | tf_op jit(solution)/shard_map/ppermute | solution.py:436
  336.3 5.8 %collective-permute-done.49 = bf16[256,1024]{1,0:T(8,128)(2,1)S(1)} collective-permute-done((bf16[256,1024]{1,0:T(8,128)(2,1)S(1)}, bf16[256,1024]{1,0:T(8,128)(2,1)S(1)}, u32[]{:S(2)}, u32[]{:S(2)}) %collective-permute-start.49) | collective-permute-done | bytes 524320 | tf_op jit(solution)/shard_map/ppermute | solution.py:436
  360.0 3.0 collective-permute-done.50
  365.9 17.8 %attn_bwd.1 = (f32[512,1024]{1,0:T(8,128)}, bf16[512,1024]{1,0:T(8,128)(2,1)}, bf16[1024,768]{1,0:T(8,128)(2,1)}, f32[4,16,256]{2,1,0:T(8,128)}) custom-call(s32[3,8]{1,0:T(4,128)} %pad_add_fusion.refs_0_, bf16[256,1024]{1,0:T(8,128)(2,1)} %copy-done.1, bf16[256,1024]{1,0:T(8,128)(2,1)} %copy-done.4, bf16[256,1024]{1,0:T(8,128)(2,1)} %copy-done.5, ...), custom_call_target="tpu_custom_call" | custom-call | flops 2147483648 | bytes 12582912 | tf_op jit(solution)/shard_map/attn_bwd/pallas_call | solution.py:281
  385.0 3.3 weight_partials.6
  390.4 5.1 %weight_partials.5 = (bf16[128,768]{1,0:T(8,128)(2,1)}, bf16[128,768]{1,0:T(8,128)(2,1)}, bf16[128,768]{1,0:T(8,128)(2,1)}, bf16[128,768]{1,0:T(8,128)(2,1)}, bf16[512,768]{1,0:T(8,128)(2,1)}) custom-call(bf16[256,1024]{1,0:T(8,128)(2,1)} %copy-done.10, bf16[256,1024]{1,0:T(8,128)(2,1)} %collective-permute-done.1.refs_2_.refs_1_, ...), custom_call_target="tpu_custom_call" | custom-call | flops 1610612736 | bytes 8388608 | tf_op jit(solution)/shard_map/weight_partials/pallas_call | solution.py:419
  395.5 6.4 %collective-permute-start.73 = (f32[2,4]{1,0:T(2,128)S(1)}, f32[2,4]{1,0:T(2,128)S(1)}, u32[]{:S(2)}, u32[]{:S(2)}) collective-permute-start(f32[2,4]{1,0:T(2,128)S(1)} %fusion.16), channel_id=1, source_target_pairs={{0,8},{8,0},{16,24},{24,16},{1,9},{9,1},{17,25},{25,17},{2,10},{10... | collective-permute-start | bytes 104 | tf_op jit(solution)/shard_map/ppermute | solution.py:436
  403.5 2.8 collective-permute-start.74
  415.2 5.2 %collective-permute-start.65 = (bf16[128,768]{1,0:T(8,128)(2,1)S(1)}, bf16[128,768]{1,0:T(8,128)(2,1)S(1)}, u32[]{:S(2)}, u32[]{:S(2)}) collective-permute-start(bf16[128,768]{1,0:T(8,128)(2,1)S(1)} %get-tuple-element.124), channel_id=1, source_target_pairs={{0,8},{8,0},{16,24},{24,16},{1,9},{9,1},{17,25},{25,17},{2,10},{10... | collective-permute-start | bytes 589832 | tf_op jit(solution)/shard_map/ppermute | solution.py:436
  423.6 4.2 collective-permute-done.65
  427.8 9.8 %collective-permute-done.66 = bf16[128,768]{1,0:T(8,128)(2,1)S(1)} collective-permute-done((bf16[128,768]{1,0:T(8,128)(2,1)S(1)}, bf16[128,768]{1,0:T(8,128)(2,1)S(1)}, u32[]{:S(2)}, u32[]{:S(2)}) %collective-permute-start.66) | collective-permute-done | bytes 196640 | tf_op jit(solution)/shard_map/ppermute | solution.py:436
  443.0 2.5 add_convert_fusion
  448.9 2.8 collective-permute-done.60
  455.3 3.6 collective-permute-start.62
  (448 shorter events, 168.8 us)
Async XLA Ops:
  0.7 25.9 %collective-permute-start.11 = (bf16[128,256]{1,0:T(8,128)(2,1)}, bf16[128,256]{1,0:T(8,128)(2,1)S(1)}, u32[]{:S(2)}, u32[]{:S(2)}) collective-permute-start(bf16[128,256]{1,0:T(8,128)(2,1)} %refs_5_.1), channel_id=1, source_target_pairs={{0,8},{8,0},{16,24},{24,16},{1,9},{9,1},{17,25},{25,17},{2,10},{10... | collective-permute-start | bytes 196616 | tf_op jit(solution)/shard_map/ppermute | solution.py:436
  3.8 26.4 %collective-permute-start.12 = (bf16[128,256]{1,0:T(8,128)(2,1)}, bf16[128,256]{1,0:T(8,128)(2,1)S(1)}, u32[]{:S(2)}, u32[]{:S(2)}) collective-permute-start(bf16[128,256]{1,0:T(8,128)(2,1)} %refs_5_.1), channel_id=1, source_target_pairs={{0,16},{8,24},{16,0},{24,8},{1,17},{9,25},{17,1},{25,9},{2,18},{10... | collective-permute-start | bytes 196616 | tf_op jit(solution)/shard_map/ppermute | solution.py:436
  6.4 26.0 %collective-permute-start.13 = (bf16[128,256]{1,0:T(8,128)(2,1)}, bf16[128,256]{1,0:T(8,128)(2,1)S(1)}, u32[]{:S(2)}, u32[]{:S(2)}) collective-permute-start(bf16[128,256]{1,0:T(8,128)(2,1)} %refs_5_.1), channel_id=1, source_target_pairs={{0,24},{8,16},{16,8},{24,0},{1,25},{9,17},{17,9},{25,1},{2,26},{10... | collective-permute-start | bytes 196616 | tf_op jit(solution)/shard_map/ppermute | solution.py:436
  6.4 26.6 %collective-permute-start.14 = (bf16[128,256]{1,0:T(8,128)(2,1)}, bf16[128,256]{1,0:T(8,128)(2,1)}, u32[]{:S(2)}, u32[]{:S(2)}) collective-permute-start(bf16[128,256]{1,0:T(8,128)(2,1)} %refs_5_.1), channel_id=1, source_target_pairs={{0,4},{4,0},{1,5},{5,1},{2,6},{6,2},{3,7},{7,3},{8,12},{12,8},{9,1... | collective-permute-start | bytes 196616 | tf_op jit(solution)/shard_map/ppermute | solution.py:436
  34.7 27.6 %collective-permute-start.2 = (bf16[256,1024]{1,0:T(8,128)(2,1)S(1)}, bf16[256,1024]{1,0:T(8,128)(2,1)}, u32[]{:S(2)}, u32[]{:S(2)}) collective-permute-start(bf16[256,1024]{1,0:T(8,128)(2,1)S(1)} %multiply_convert_fusion.1.refs_1_.refs_0_), channel_id=1, source_target_pairs={{0,1},{1,0},{2,3},{3,2},{4,5},{5,4},{6,7},{7,6},{8,9},{9,8},{10,11... | collective-permute-start | bytes 1572872 | tf_op jit(solution)/shard_map/ppermute | solution.py:436
  34.9 27.4 %collective-permute-start.3 = (bf16[256,1024]{1,0:T(8,128)(2,1)}, bf16[256,1024]{1,0:T(8,128)(2,1)}, u32[]{:S(2)}, u32[]{:S(2)}) collective-permute-start(bf16[256,1024]{1,0:T(8,128)(2,1)} %collective-permute-done.1.refs_2_.refs_1_), channel_id=1, source_target_pairs={{0,1},{1,0},{2,3},{3,2},{4,5},{5,4},{6,7},{7,6},{8,9},{9,8},{10,11... | collective-permute-start | bytes 1572872 | tf_op jit(solution)/shard_map/ppermute | solution.py:436
  80.4 19.4 %collective-permute-start.41 = (bf16[128,1024]{1,0:T(8,128)(2,1)}, bf16[128,1024]{1,0:T(8,128)(2,1)}, u32[]{:S(2)}, u32[]{:S(2)}) collective-permute-start(bf16[128,1024]{1,0:T(8,128)(2,1)} %refs_24_.1), channel_id=1, source_target_pairs={{0,8},{8,0},{16,24},{24,16},{1,9},{9,1},{17,25},{25,17},{2,10},{10... | collective-permute-start | bytes 786440 | tf_op jit(solution)/shard_map/ppermute | solution.py:436
  80.5 21.7 %collective-permute-start.42 = (bf16[128,1024]{1,0:T(8,128)(2,1)}, bf16[128,1024]{1,0:T(8,128)(2,1)}, u32[]{:S(2)}, u32[]{:S(2)}) collective-permute-start(bf16[128,1024]{1,0:T(8,128)(2,1)} %refs_24_.1), channel_id=1, source_target_pairs={{0,16},{8,24},{16,0},{24,8},{1,17},{9,25},{17,1},{25,9},{2,18},{10... | collective-permute-start | bytes 786440 | tf_op jit(solution)/shard_map/ppermute | solution.py:436
  83.0 21.2 %collective-permute-start.43 = (bf16[128,1024]{1,0:T(8,128)(2,1)}, bf16[128,1024]{1,0:T(8,128)(2,1)}, u32[]{:S(2)}, u32[]{:S(2)}) collective-permute-start(bf16[128,1024]{1,0:T(8,128)(2,1)} %refs_24_.1), channel_id=1, source_target_pairs={{0,24},{8,16},{16,8},{24,0},{1,25},{9,17},{17,9},{25,1},{2,26},{10... | collective-permute-start | bytes 786440 | tf_op jit(solution)/shard_map/ppermute | solution.py:436
  93.8 26.9 %collective-permute-start.27 = (bf16[128,1024]{1,0:T(8,128)(2,1)}, bf16[128,1024]{1,0:T(8,128)(2,1)}, u32[]{:S(2)}, u32[]{:S(2)}) collective-permute-start(bf16[128,1024]{1,0:T(8,128)(2,1)} %refs_8_.1), channel_id=1, source_target_pairs={{0,8},{8,0},{16,24},{24,16},{1,9},{9,1},{17,25},{25,17},{2,10},{10... | collective-permute-start | bytes 786440 | tf_op jit(solution)/shard_map/ppermute | solution.py:436
  97.8 34.1 %collective-permute-start.19 = (bf16[256,1024]{1,0:T(8,128)(2,1)S(1)}, bf16[256,1024]{1,0:T(8,128)(2,1)}, u32[]{:S(2)}, u32[]{:S(2)}) collective-permute-start(bf16[256,1024]{1,0:T(8,128)(2,1)S(1)} %slice.300), channel_id=1, source_target_pairs={{0,2},{1,3},{2,0},{3,1},{4,6},{5,7},{6,4},{7,5},{8,10},{9,11},{10,... | collective-permute-start | bytes 1572872 | tf_op jit(solution)/shard_map/ppermute | solution.py:436
  99.8 24.9 %collective-permute-start.28 = (bf16[128,1024]{1,0:T(8,128)(2,1)S(1)}, bf16[128,1024]{1,0:T(8,128)(2,1)}, u32[]{:S(2)}, u32[]{:S(2)}) collective-permute-start(bf16[128,1024]{1,0:T(8,128)(2,1)S(1)} %copy-done.71), channel_id=1, source_target_pairs={{0,16},{8,24},{16,0},{24,8},{1,17},{9,25},{17,1},{25,9},{2,18},{10... | collective-permute-start | bytes 786440 | tf_op jit(solution)/shard_map/ppermute | solution.py:436
  102.2 26.5 %collective-permute-start.29 = (bf16[128,1024]{1,0:T(8,128)(2,1)S(1)}, bf16[128,1024]{1,0:T(8,128)(2,1)}, u32[]{:S(2)}, u32[]{:S(2)}) collective-permute-start(bf16[128,1024]{1,0:T(8,128)(2,1)S(1)} %copy-done.71), channel_id=1, source_target_pairs={{0,24},{8,16},{16,8},{24,0},{1,25},{9,17},{17,9},{25,1},{2,26},{10... | collective-permute-start | bytes 786440 | tf_op jit(solution)/shard_map/ppermute | solution.py:436
  104.2 24.5 %collective-permute-start.34 = (bf16[128,1024]{1,0:T(8,128)(2,1)}, bf16[128,1024]{1,0:T(8,128)(2,1)}, u32[]{:S(2)}, u32[]{:S(2)}) collective-permute-start(bf16[128,1024]{1,0:T(8,128)(2,1)} %refs_16_.1), channel_id=1, source_target_pairs={{0,8},{8,0},{16,24},{24,16},{1,9},{9,1},{17,25},{25,17},{2,10},{10... | collective-permute-start | bytes 786440 | tf_op jit(solution)/shard_map/ppermute | solution.py:436
  120.7 26.4 %collective-permute-start.35 = (bf16[128,1024]{1,0:T(8,128)(2,1)}, bf16[128,1024]{1,0:T(8,128)(2,1)S(1)}, u32[]{:S(2)}, u32[]{:S(2)}) collective-permute-start(bf16[128,1024]{1,0:T(8,128)(2,1)} %refs_16_.1), channel_id=1, source_target_pairs={{0,16},{8,24},{16,0},{24,8},{1,17},{9,25},{17,1},{25,9},{2,18},{10... | collective-permute-start | bytes 786440 | tf_op jit(solution)/shard_map/ppermute | solution.py:436
  124.7 24.2 %collective-permute-start.36 = (bf16[128,1024]{1,0:T(8,128)(2,1)}, bf16[128,1024]{1,0:T(8,128)(2,1)S(1)}, u32[]{:S(2)}, u32[]{:S(2)}) collective-permute-start(bf16[128,1024]{1,0:T(8,128)(2,1)} %refs_16_.1), channel_id=1, source_target_pairs={{0,24},{8,16},{16,8},{24,0},{1,25},{9,17},{17,9},{25,1},{2,26},{10... | collective-permute-start | bytes 786440 | tf_op jit(solution)/shard_map/ppermute | solution.py:436
  128.7 21.7 %collective-permute-start.44 = (bf16[128,1024]{1,0:T(8,128)(2,1)}, bf16[128,1024]{1,0:T(8,128)(2,1)S(1)}, u32[]{:S(2)}, u32[]{:S(2)}) collective-permute-start(bf16[128,1024]{1,0:T(8,128)(2,1)} %refs_24_.1), channel_id=1, source_target_pairs={{0,4},{4,0},{1,5},{5,1},{2,6},{6,2},{3,7},{7,3},{8,12},{12,8},{9,1... | collective-permute-start | bytes 786440 | tf_op jit(solution)/shard_map/ppermute | solution.py:436
  128.7 22.2 %collective-permute-start.30 = (bf16[128,1024]{1,0:T(8,128)(2,1)S(1)}, bf16[128,1024]{1,0:T(8,128)(2,1)S(1)}, u32[]{:S(2)}, u32[]{:S(2)}) collective-permute-start(bf16[128,1024]{1,0:T(8,128)(2,1)S(1)} %copy-done.71), channel_id=1, source_target_pairs={{0,4},{4,0},{1,5},{5,1},{2,6},{6,2},{3,7},{7,3},{8,12},{12,8},{9,1... | collective-permute-start | bytes 786440 | tf_op jit(solution)/shard_map/ppermute | solution.py:436
  131.9 20.6 %collective-permute-start.37 = (bf16[128,1024]{1,0:T(8,128)(2,1)}, bf16[128,1024]{1,0:T(8,128)(2,1)S(1)}, u32[]{:S(2)}, u32[]{:S(2)}) collective-permute-start(bf16[128,1024]{1,0:T(8,128)(2,1)} %refs_16_.1), channel_id=1, source_target_pairs={{0,4},{4,0},{1,5},{5,1},{2,6},{6,2},{3,7},{7,3},{8,12},{12,8},{9,1... | collective-permute-start | bytes 786440 | tf_op jit(solution)/shard_map/ppermute | solution.py:436
  147.1 39.5 %collective-permute-start.24 = (bf16[256,1024]{1,0:T(8,128)(2,1)S(1)}, bf16[256,1024]{1,0:T(8,128)(2,1)S(1)}, u32[]{:S(2)}, u32[]{:S(2)}) collective-permute-start(bf16[256,1024]{1,0:T(8,128)(2,1)S(1)} %reshape.232.refs_4_.refs_0_), channel_id=1, source_target_pairs={{0,2},{1,3},{2,0},{3,1},{4,6},{5,7},{6,4},{7,5},{8,10},{9,11},{10,... | collective-permute-start | bytes 1572872 | tf_op jit(solution)/shard_map/ppermute | solution.py:436
  150.9 18.6 %collective-permute-start.47 = (bf16[128,1024]{1,0:T(8,128)(2,1)}, bf16[128,1024]{1,0:T(8,128)(2,1)S(1)}, u32[]{:S(2)}, u32[]{:S(2)}) collective-permute-start(bf16[128,1024]{1,0:T(8,128)(2,1)} %collective-permute-done.43.refs_27_), channel_id=1, source_target_pairs={{0,4},{4,0},{1,5},{5,1},{2,6},{6,2},{3,7},{7,3},{8,12},{12,8},{9,1... | collective-permute-start | bytes 786440 | tf_op jit(solution)/shard_map/ppermute | solution.py:436
  152.4 22.8 %collective-permute-start.31 = (bf16[128,1024]{1,0:T(8,128)(2,1)}, bf16[128,1024]{1,0:T(8,128)(2,1)S(1)}, u32[]{:S(2)}, u32[]{:S(2)}) collective-permute-start(bf16[128,1024]{1,0:T(8,128)(2,1)} %collective-permute-done.27.refs_9_), channel_id=1, source_target_pairs={{0,4},{4,0},{1,5},{5,1},{2,6},{6,2},{3,7},{7,3},{8,12},{12,8},{9,1... | collective-permute-start | bytes 786440 | tf_op jit(solution)/shard_map/ppermute | solution.py:436
  158.3 33.7 %collective-permute-start.20 = (bf16[256,1024]{1,0:T(8,128)(2,1)S(1)}, bf16[256,1024]{1,0:T(8,128)(2,1)S(1)}, u32[]{:S(2)}, u32[]{:S(2)}) collective-permute-start(bf16[256,1024]{1,0:T(8,128)(2,1)S(1)} %multiply_convert_fusion.refs_0_), channel_id=1, source_target_pairs={{0,2},{1,3},{2,0},{3,1},{4,6},{5,7},{6,4},{7,5},{8,10},{9,11},{10,... | collective-permute-start | bytes 1572872 | tf_op jit(solution)/shard_map/ppermute | solution.py:436
  164.0 16.9 %collective-permute-start.32 = (bf16[128,1024]{1,0:T(8,128)(2,1)}, bf16[128,1024]{1,0:T(8,128)(2,1)S(1)}, u32[]{:S(2)}, u32[]{:S(2)}) collective-permute-start(bf16[128,1024]{1,0:T(8,128)(2,1)} %collective-permute-done.28.refs_10_), channel_id=1, source_target_pairs={{0,4},{4,0},{1,5},{5,1},{2,6},{6,2},{3,7},{7,3},{8,12},{12,8},{9,1... | collective-permute-start | bytes 786440 | tf_op jit(solution)/shard_map/ppermute | solution.py:436
  169.6 17.0 %collective-permute-start.33 = (bf16[128,1024]{1,0:T(8,128)(2,1)}, bf16[128,1024]{1,0:T(8,128)(2,1)}, u32[]{:S(2)}, u32[]{:S(2)}) collective-permute-start(bf16[128,1024]{1,0:T(8,128)(2,1)} %collective-permute-done.29.refs_11_), channel_id=1, source_target_pairs={{0,4},{4,0},{1,5},{5,1},{2,6},{6,2},{3,7},{7,3},{8,12},{12,8},{9,1... | collective-permute-start | bytes 786440 | tf_op jit(solution)/shard_map/ppermute | solution.py:436
  175.2 16.9 %collective-permute-start.38 = (bf16[128,1024]{1,0:T(8,128)(2,1)}, bf16[128,1024]{1,0:T(8,128)(2,1)S(1)}, u32[]{:S(2)}, u32[]{:S(2)}) collective-permute-start(bf16[128,1024]{1,0:T(8,128)(2,1)} %collective-permute-done.34.refs_17_), channel_id=1, source_target_pairs={{0,4},{4,0},{1,5},{5,1},{2,6},{6,2},{3,7},{7,3},{8,12},{12,8},{9,1... | collective-permute-start | bytes 786440 | tf_op jit(solution)/shard_map/ppermute | solution.py:436
  227.8 26.4 %collective-permute-start.83 = (bf16[512,1024]{1,0:T(8,128)(2,1)}, bf16[512,1024]{1,0:T(8,128)(2,1)}, u32[]{:S(2)}, u32[]{:S(2)}) collective-permute-start(bf16[512,1024]{1,0:T(8,128)(2,1)} %get-tuple-element.90), channel_id=1, source_target_pairs={{0,4},{4,0},{1,5},{5,1},{2,6},{6,2},{3,7},{7,3},{8,12},{12,8},{9,1... | collective-permute-start | bytes 3145736 | tf_op jit(solution)/shard_map/ppermute | solution.py:436
  236.4 29.4 %collective-permute-start.48 = (bf16[512,1024]{1,0:T(8,128)(2,1)}, bf16[512,1024]{1,0:T(8,128)(2,1)}, u32[]{:S(2)}, u32[]{:S(2)}) collective-permute-start(bf16[512,1024]{1,0:T(8,128)(2,1)} %slice.296), channel_id=1, source_target_pairs={{0,1},{1,0},{2,3},{3,2},{4,5},{5,4},{6,7},{7,6},{8,9},{9,8},{10,11... | collective-permute-start | bytes 3145736 | tf_op jit(solution)/shard_map/ppermute | solution.py:436
  242.2 34.5 %collective-permute-start.79 = (bf16[512,1024]{1,0:T(8,128)(2,1)}, bf16[512,1024]{1,0:T(8,128)(2,1)}, u32[]{:S(2)}, u32[]{:S(2)}) collective-permute-start(bf16[512,1024]{1,0:T(8,128)(2,1)} %get-tuple-element.85), channel_id=1, source_target_pairs={{0,4},{4,0},{1,5},{5,1},{2,6},{6,2},{3,7},{7,3},{8,12},{12,8},{9,1... | collective-permute-start | bytes 3145736 | tf_op jit(solution)/shard_map/ppermute | solution.py:436
  243.4 36.4 %collective-permute-start.51 = (bf16[512,1024]{1,0:T(8,128)(2,1)}, bf16[512,1024]{1,0:T(8,128)(2,1)S(1)}, u32[]{:S(2)}, u32[]{:S(2)}) collective-permute-start(bf16[512,1024]{1,0:T(8,128)(2,1)} %get-tuple-element.57), channel_id=1, source_target_pairs={{0,1},{1,0},{2,3},{3,2},{4,5},{5,4},{6,7},{7,6},{8,9},{9,8},{10,11... | collective-permute-start | bytes 3145736 | tf_op jit(solution)/shard_map/ppermute | solution.py:436
  249.8 45.9 %collective-permute-start.75 = (bf16[512,1024]{1,0:T(8,128)(2,1)}, bf16[512,1024]{1,0:T(8,128)(2,1)S(1)}, u32[]{:S(2)}, u32[]{:S(2)}) collective-permute-start(bf16[512,1024]{1,0:T(8,128)(2,1)} %get-tuple-element.79), channel_id=1, source_target_pairs={{0,4},{4,0},{1,5},{5,1},{2,6},{6,2},{3,7},{7,3},{8,12},{12,8},{9,1... | collective-permute-start | bytes 3145736 | tf_op jit(solution)/shard_map/ppermute | solution.py:436
  255.7 51.4 %collective-permute-start.84 = (bf16[128,1024]{1,0:T(8,128)(2,1)S(1)}, bf16[128,1024]{1,0:T(8,128)(2,1)S(1)}, u32[]{:S(2)}, u32[]{:S(2)}) collective-permute-start(bf16[128,1024]{1,0:T(8,128)(2,1)S(1)} %get-tuple-element.114), channel_id=1, source_target_pairs={{0,8},{8,0},{16,24},{24,16},{1,9},{9,1},{17,25},{25,17},{2,10},{10... | collective-permute-start | bytes 786440 | tf_op jit(solution)/shard_map/ppermute | solution.py:436
  265.8 43.0 %collective-permute-start.85 = (bf16[128,1024]{1,0:T(8,128)(2,1)S(1)}, bf16[128,1024]{1,0:T(8,128)(2,1)S(1)}, u32[]{:S(2)}, u32[]{:S(2)}) collective-permute-start(bf16[128,1024]{1,0:T(8,128)(2,1)S(1)} %get-tuple-element.116), channel_id=1, source_target_pairs={{0,16},{8,24},{16,0},{24,8},{1,17},{9,25},{17,1},{25,9},{2,18},{10... | collective-permute-start | bytes 786440 | tf_op jit(solution)/shard_map/ppermute | solution.py:436
  276.7 32.2 %collective-permute-start.86 = (bf16[128,1024]{1,0:T(8,128)(2,1)S(1)}, bf16[128,1024]{1,0:T(8,128)(2,1)S(1)}, u32[]{:S(2)}, u32[]{:S(2)}) collective-permute-start(bf16[128,1024]{1,0:T(8,128)(2,1)S(1)} %get-tuple-element.115), channel_id=1, source_target_pairs={{0,24},{8,16},{16,8},{24,0},{1,25},{9,17},{17,9},{25,1},{2,26},{10... | collective-permute-start | bytes 786440 | tf_op jit(solution)/shard_map/ppermute | solution.py:436
  279.8 32.9 %collective-permute-start.80 = (bf16[128,1024]{1,0:T(8,128)(2,1)S(1)}, bf16[128,1024]{1,0:T(8,128)(2,1)S(1)}, u32[]{:S(2)}, u32[]{:S(2)}) collective-permute-start(bf16[128,1024]{1,0:T(8,128)(2,1)S(1)} %get-tuple-element.117), channel_id=1, source_target_pairs={{0,8},{8,0},{16,24},{24,16},{1,9},{9,1},{17,25},{25,17},{2,10},{10... | collective-permute-start | bytes 786440 | tf_op jit(solution)/shard_map/ppermute | solution.py:436
  295.6 34.6 %collective-permute-start.81 = (bf16[128,1024]{1,0:T(8,128)(2,1)S(1)}, bf16[128,1024]{1,0:T(8,128)(2,1)S(1)}, u32[]{:S(2)}, u32[]{:S(2)}) collective-permute-start(bf16[128,1024]{1,0:T(8,128)(2,1)S(1)} %get-tuple-element.119), channel_id=1, source_target_pairs={{0,16},{8,24},{16,0},{24,8},{1,17},{9,25},{17,1},{25,9},{2,18},{10... | collective-permute-start | bytes 786440 | tf_op jit(solution)/shard_map/ppermute | solution.py:436
  307.1 25.2 %collective-permute-start.82 = (bf16[128,1024]{1,0:T(8,128)(2,1)S(1)}, bf16[128,1024]{1,0:T(8,128)(2,1)S(1)}, u32[]{:S(2)}, u32[]{:S(2)}) collective-permute-start(bf16[128,1024]{1,0:T(8,128)(2,1)S(1)} %get-tuple-element.118), channel_id=1, source_target_pairs={{0,24},{8,16},{16,8},{24,0},{1,25},{9,17},{17,9},{25,1},{2,26},{10... | collective-permute-start | bytes 786440 | tf_op jit(solution)/shard_map/ppermute | solution.py:436
  308.9 45.2 %collective-permute-start.76 = (bf16[128,1024]{1,0:T(8,128)(2,1)}, bf16[128,1024]{1,0:T(8,128)(2,1)}, u32[]{:S(2)}, u32[]{:S(2)}) collective-permute-start(bf16[128,1024]{1,0:T(8,128)(2,1)} %get-tuple-element.120), channel_id=1, source_target_pairs={{0,8},{8,0},{16,24},{24,16},{1,9},{9,1},{17,25},{25,17},{2,10},{10... | collective-permute-start | bytes 786440 | tf_op jit(solution)/shard_map/ppermute | solution.py:436
  308.9 26.9 %collective-permute-start.52 = (bf16[256,1024]{1,0:T(8,128)(2,1)S(1)}, bf16[256,1024]{1,0:T(8,128)(2,1)S(1)}, u32[]{:S(2)}, u32[]{:S(2)}) collective-permute-start(bf16[256,1024]{1,0:T(8,128)(2,1)S(1)} %slice.298), channel_id=1, source_target_pairs={{0,2},{1,3},{2,0},{3,1},{4,6},{5,7},{6,4},{7,5},{8,10},{9,11},{10,... | collective-permute-start | bytes 1572872 | tf_op jit(solution)/shard_map/ppermute | solution.py:436
  312.7 43.1 %collective-permute-start.77 = (bf16[128,1024]{1,0:T(8,128)(2,1)}, bf16[128,1024]{1,0:T(8,128)(2,1)}, u32[]{:S(2)}, u32[]{:S(2)}) collective-permute-start(bf16[128,1024]{1,0:T(8,128)(2,1)} %get-tuple-element.122), channel_id=1, source_target_pairs={{0,16},{8,24},{16,0},{24,8},{1,17},{9,25},{17,1},{25,9},{2,18},{10... | collective-permute-start | bytes 786440 | tf_op jit(solution)/shard_map/ppermute | solution.py:436
  330.3 25.5 %collective-permute-start.78 = (bf16[128,1024]{1,0:T(8,128)(2,1)}, bf16[128,1024]{1,0:T(8,128)(2,1)}, u32[]{:S(2)}, u32[]{:S(2)}) collective-permute-start(bf16[128,1024]{1,0:T(8,128)(2,1)} %get-tuple-element.121), channel_id=1, source_target_pairs={{0,24},{8,16},{16,8},{24,0},{1,25},{9,17},{17,9},{25,1},{2,26},{10... | collective-permute-start | bytes 786440 | tf_op jit(solution)/shard_map/ppermute | solution.py:436
  345.5 19.5 %collective-permute-start.54 = (bf16[256,1024]{1,0:T(8,128)(2,1)S(1)}, bf16[256,1024]{1,0:T(8,128)(2,1)S(1)}, u32[]{:S(2)}, u32[]{:S(2)}) collective-permute-start(bf16[256,1024]{1,0:T(8,128)(2,1)S(1)} %get-tuple-element.104.refs_1_.refs_0_), channel_id=1, source_target_pairs={{0,1},{1,0},{2,3},{3,2},{4,5},{5,4},{6,7},{7,6},{8,9},{9,8},{10,11... | collective-permute-start | bytes 1572872 | tf_op jit(solution)/shard_map/ppermute | solution.py:436
  384.7 28.5 %collective-permute-start.56 = (bf16[512,1024]{1,0:T(8,128)(2,1)}, bf16[512,1024]{1,0:T(8,128)(2,1)S(1)}, u32[]{:S(2)}, u32[]{:S(2)}) collective-permute-start(bf16[512,1024]{1,0:T(8,128)(2,1)} %get-tuple-element.63), channel_id=1, source_target_pairs={{0,1},{1,0},{2,3},{3,2},{4,5},{5,4},{6,7},{7,6},{8,9},{9,8},{10,11... | collective-permute-start | bytes 3145736 | tf_op jit(solution)/shard_map/ppermute | solution.py:436
  388.4 20.2 %collective-permute-start.68 = (bf16[512,256]{1,0:T(8,128)(2,1)}, bf16[512,256]{1,0:T(8,128)(2,1)S(1)}, u32[]{:S(2)}, u32[]{:S(2)}) collective-permute-start(bf16[512,256]{1,0:T(8,128)(2,1)} %get-tuple-element.72), channel_id=1, source_target_pairs={{0,4},{4,0},{1,5},{5,1},{2,6},{6,2},{3,7},{7,3},{8,12},{12,8},{9,1... | collective-permute-start | bytes 786440 | tf_op jit(solution)/shard_map/ppermute | solution.py:436
  395.5 19.6 %collective-permute-start.64 = (bf16[512,768]{1,0:T(8,128)(2,1)}, bf16[512,768]{1,0:T(8,128)(2,1)S(1)}, u32[]{:S(2)}, u32[]{:S(2)}) collective-permute-start(bf16[512,768]{1,0:T(8,128)(2,1)} %get-tuple-element.66), channel_id=1, source_target_pairs={{0,4},{4,0},{1,5},{5,1},{2,6},{6,2},{3,7},{7,3},{8,12},{12,8},{9,1... | collective-permute-start | bytes 2359304 | tf_op jit(solution)/shard_map/ppermute | solution.py:436
  413.6 24.1 %collective-permute-start.57 = (bf16[256,1024]{1,0:T(8,128)(2,1)S(1)}, bf16[256,1024]{1,0:T(8,128)(2,1)S(1)}, u32[]{:S(2)}, u32[]{:S(2)}) collective-permute-start(bf16[256,1024]{1,0:T(8,128)(2,1)S(1)} %slice.297), channel_id=1, source_target_pairs={{0,2},{1,3},{2,0},{3,1},{4,6},{5,7},{6,4},{7,5},{8,10},{9,11},{10,... | collective-permute-start | bytes 1572872 | tf_op jit(solution)/shard_map/ppermute | solution.py:436
  420.5 17.2 %collective-permute-start.66 = (bf16[128,768]{1,0:T(8,128)(2,1)S(1)}, bf16[128,768]{1,0:T(8,128)(2,1)S(1)}, u32[]{:S(2)}, u32[]{:S(2)}) collective-permute-start(bf16[128,768]{1,0:T(8,128)(2,1)S(1)} %get-tuple-element.126), channel_id=1, source_target_pairs={{0,16},{8,24},{16,0},{24,8},{1,17},{9,25},{17,1},{25,9},{2,18},{10... | collective-permute-start | bytes 589832 | tf_op jit(solution)/shard_map/ppermute | solution.py:436
  421.3 16.4 %collective-permute-start.67 = (bf16[128,768]{1,0:T(8,128)(2,1)S(1)}, bf16[128,768]{1,0:T(8,128)(2,1)S(1)}, u32[]{:S(2)}, u32[]{:S(2)}) collective-permute-start(bf16[128,768]{1,0:T(8,128)(2,1)S(1)} %get-tuple-element.125), channel_id=1, source_target_pairs={{0,24},{8,16},{16,8},{24,0},{1,25},{9,17},{17,9},{25,1},{2,26},{10... | collective-permute-start | bytes 589832 | tf_op jit(solution)/shard_map/ppermute | solution.py:436
  (120 other events, 1742.7 us)

commit v3 on v2

--- a/solution.py
+++ b/solution.py
@@ -45,7 +45,6 @@
     tables, refs = refs[0], refs[1:]
     rows, refs = refs[:row_parts], refs[row_parts:]
     weights, refs = refs[:weight_parts], refs[weight_parts:]
-    outs_w, refs = refs[:weight_parts], refs[weight_parts:]
     cosine, sine, seg_row, seg_wide, feature, coef = refs[:6]
     q_aug, k_aug, v_out, mixed_out, lse_out, keep_out, send_out = refs[6:13]
     full, out_full, mixed_wide, v_turn = refs[13:]
@@ -56,8 +55,9 @@
     part = rows[0].shape[0]
     share = part // 2
     for i in range(weight_parts):
-        full[i * block : (i + 1) * block, :] = weights[i][...]
-        out_full[i * block : (i + 1) * block, :] = outs_w[i][...]
+        at = pl.ds(pl.multiple_of(tables[3, i] * block, block), block)
+        full[at, :] = weights[i][:, : 3 * proj]
+        out_full[at, :] = weights[i][:, 3 * proj :]
     for p in range(row_parts):
         raw = nn_dot(rows[p][...], full[...])
         for k in range(2):
@@ -138,7 +138,7 @@
     return pl.BlockSpec(memory_space=pltpu.SMEM)
 
 
-def attention_forward(tables, rows, weights, outs_w, cosine, sine, seg_row, seg_wide, feature, coef, heads):
+def attention_forward(tables, rows, weights, cosine, sine, seg_row, seg_wide, feature, coef, heads):
     proj = heads * HEAD
     length = cosine.shape[0]
     width = rows[0].shape[1]
@@ -151,7 +151,7 @@
         jax.ShapeDtypeStruct((length // 2, width), F32),
         jax.ShapeDtypeStruct((length // 2, width), BF16),
     )
-    count = len(rows) + 2 * len(weights) + 6
+    count = len(rows) + len(weights) + 6
     return pl.pallas_call(
         functools.partial(fwd_kernel, len(rows), len(weights), heads),
         out_shape=shapes,
@@ -168,13 +168,12 @@
             flops=2 * length * width * 3 * proj, bytes_accessed=8 << 20, transcendentals=length * length * heads // 2
         ),
         name="attn_fwd",
-    )(tables, *rows, *weights, *outs_w, cosine, sine, seg_row, seg_wide, feature, coef)
+    )(tables, *rows, *weights, cosine, sine, seg_row, seg_wide, feature, coef)
 
 
 def bwd_kernel(row_parts, weight_parts, heads, *refs):
     tables, refs = refs[0], refs[1:]
     rows, refs = refs[:row_parts], refs[row_parts:]
-    outs_w, refs = refs[:weight_parts], refs[weight_parts:]
     weights, refs = refs[:weight_parts], refs[weight_parts:]
     q_aug, k_aug, v_in, lse, cosine, sine, seg_row, seg_wide, hot_rows = refs[:9]
     keep_out, send_out, d_qkv_out, bias_out = refs[9:13]
@@ -186,8 +185,9 @@
     part = rows[0].shape[0]
     share = part // 2
     for i in range(weight_parts):
-        full[i * block : (i + 1) * block, :] = weights[i][...]
-        out_full[i * block : (i + 1) * block, :] = outs_w[i][...]
+        at = pl.ds(pl.multiple_of(tables[3, i] * block, block), block)
+        full[at, :] = weights[i][:, : 3 * proj]
+        out_full[at, :] = weights[i][:, 3 * proj :]
     for p in range(row_parts):
         raw = nn_dot(rows[p][...], out_full[...]).astype(BF16)
         for k in range(2):
@@ -267,7 +267,7 @@
             send_out[(p - half) * part : (p - half + 1) * part, :] = back.astype(BF16)
 
 
-def attention_backward(tables, rows, outs_w, weights, q_aug, k_aug, v_in, lse, cosine, sine, seg_row, seg_wide, hot_rows, heads):
+def attention_backward(tables, rows, weights, q_aug, k_aug, v_in, lse, cosine, sine, seg_row, seg_wide, hot_rows, heads):
     proj = heads * HEAD
     length = cosine.shape[0]
     width = rows[0].shape[1]
@@ -277,7 +277,7 @@
         jax.ShapeDtypeStruct((length, 3 * proj), BF16),
         jax.ShapeDtypeStruct((heads, 16, QUERIES), F32),
     )
-    count = len(rows) + 2 * len(weights) + 9
+    count = len(rows) + len(weights) + 9
     return pl.pallas_call(
         functools.partial(bwd_kernel, len(rows), len(weights), heads),
         out_shape=shapes,
@@ -297,10 +297,10 @@
             flops=2 * length * width * 4 * proj, bytes_accessed=12 << 20, transcendentals=length * length * heads // 2
         ),
         name="attn_bwd",
-    )(tables, *rows, *outs_w, *weights, q_aug, k_aug, v_in, lse, cosine, sine, seg_row, seg_wide, hot_rows)
-
-
-def attention_tables(segments, variates, times, variate_bias, order, share):
+    )(tables, *rows, *weights, q_aug, k_aug, v_in, lse, cosine, sine, seg_row, seg_wide, hot_rows)
+
+
+def attention_tables(segments, variates, times, variate_bias, order, places):
     length = segments.shape[0]
     heads = variate_bias.shape[1]
     count = length // QUERIES
@@ -331,88 +331,150 @@
     first = start // LANES
     kind = (stop - first * LANES + STEP - 1) // STEP
     first = jnp.minimum(first, (length - kind * STEP) // LANES)
-    size = max(count, order.shape[0])
+    size = max(count, order.shape[0], places.shape[0])
     pad = lambda a: jnp.pad(a.astype(jnp.int32), (0, size - a.shape[0]))
-    tables = jnp.stack([pad(order), pad(first), pad(kind)])
+    tables = jnp.stack([pad(order), pad(first), pad(kind), pad(places)])
     return tables, cosine, sine, seg_row, seg_wide, feature, coef, hot_rows
 
-def ffn_kernel(row_parts, weight_parts, *refs):
+
+def ffn_kernel(row_parts, seq, *refs):
     rows, refs = refs[:row_parts], refs[row_parts:]
     grads, refs = refs[:row_parts], refs[row_parts:]
-    gates, refs = refs[:weight_parts], refs[weight_parts:]
-    ups, refs = refs[:weight_parts], refs[weight_parts:]
-    downs, refs = refs[:weight_parts], refs[weight_parts:]
-    act_out, d_gate_out, d_up_out, keep_out, send_out, gate_full, up_full, down_full = refs
-    block = gates[0].shape[0]
+    weight, act_out, d_both_out, keep_out, send_out = refs
     part = rows[0].shape[0]
-    for i in range(weight_parts):
-        at = slice(i * block, (i + 1) * block)
-        gate_full[at, :] = gates[i][...]
-        up_full[at, :] = ups[i][...]
-        down_full[at, :] = downs[i][...]
+    cols = act_out.shape[1]
     half = row_parts // 2
     for p in list(range(half, row_parts)) + list(range(half)):
         at = slice(p * part, (p + 1) * part)
-        gate = nn_dot(rows[p][...], gate_full[...])
-        up = nn_dot(rows[p][...], up_full[...])
-        d_act = nn_dot(grads[p][...], down_full[...])
+        both = nn_dot(rows[p][...], weight[:, : 2 * cols])
+        d_act = nn_dot(grads[p][seq * part : (seq + 1) * part, :], weight[:, 2 * cols :])
+        gate, up = both[:, :cols], both[:, cols:]
         sig = 1.0 / (1.0 + jnp.exp(-gate))
         silu = gate * sig
         act_out[at, :] = (silu * up).astype(BF16)
-        d_gate_out[at, :] = (d_act * up * (sig + silu * (1.0 - sig))).astype(BF16)
-        d_up_out[at, :] = (d_act * silu).astype(BF16)
-        back = nt_dot(d_gate_out[at, :], gate_full[...]) + nt_dot(d_up_out[at, :], up_full[...])
+        d_both_out[at, :cols] = (d_act * up * (sig + silu * (1.0 - sig))).astype(BF16)
+        d_both_out[at, cols:] = (d_act * silu).astype(BF16)
+        back = nt_dot(d_both_out[at, :], weight[:, : 2 * cols])
         if p < half:
             keep_out[at, :] = back
         else:
             send_out[(p - half) * part : (p - half + 1) * part, :] = back.astype(BF16)
 
 
-def ffn_middle(rows, grads, gates, ups, downs):
+def ffn_middle(seq, rows, grads, weight):
     part, width = rows[0].shape
     length = part * len(rows)
-    hidden = gates[0].shape[1]
-    units = jax.ShapeDtypeStruct((length, hidden), BF16)
+    cols = weight.shape[1] // 3
     return pl.pallas_call(
-        functools.partial(ffn_kernel, len(rows), len(gates)),
+        functools.partial(ffn_kernel, len(rows), seq),
         out_shape=(
-            units,
-            units,
-            units,
+            jax.ShapeDtypeStruct((length, cols), BF16),
+            jax.ShapeDtypeStruct((length, 2 * cols), BF16),
             jax.ShapeDtypeStruct((length // 2, width), F32),
             jax.ShapeDtypeStruct((length // 2, width), BF16),
         ),
-        in_specs=[vmem()] * (2 * len(rows) + 3 * len(gates)),
-        out_specs=[vmem()] * 5,
-        scratch_shapes=[pltpu.VMEM((width, hidden), BF16)] * 3,
+        in_specs=[vmem()] * (2 * len(rows) + 1),
+        out_specs=[vmem()] * 4,
         compiler_params=pltpu.CompilerParams(vmem_limit_bytes=VMEM_LIMIT),
         cost_estimate=pl.CostEstimate(
-            flops=10 * length * width * hidden, bytes_accessed=20 << 20, transcendentals=length * hidden
+            flops=10 * length * width * cols, bytes_accessed=16 << 20, transcendentals=length * cols
         ),
         name="ffn_middle",
-    )(*rows, *grads, *gates, *ups, *downs)
-
-
-def grad_kernel(row_parts, blocks, *refs):
+    )(*rows, *grads, weight)
+
+
+def ffn_grad_kernel(row_parts, *refs):
+    own, refs = refs[:row_parts], refs[row_parts:]
+    other, refs = refs[:row_parts], refs[row_parts:]
+    grads, refs = refs[:row_parts], refs[row_parts:]
+    act_own, act_other, d_own, d_other, out, left = refs
+    part, width = own[0].shape
+    length = part * row_parts
+    cols = act_own.shape[1]
+    for what in range(2):
+        for seq in range(2):
+            for p in range(row_parts):
+                for c in range(width // LANES):
+                    lanes = slice(c * LANES, (c + 1) * LANES)
+                    if what == 0:
+                        tile = grads[p][seq * part : (seq + 1) * part, lanes]
+                    else:
+                        tile = (own, other)[seq][p][:, lanes]
+                    at = seq * length + p * part
+                    left[lanes, at : at + part] = tile.astype(F32).T.astype(BF16)
+        first, second = ((act_own, act_other), (d_own, d_other))[what]
+        to = slice(2 * cols, 3 * cols) if what == 0 else slice(0, 2 * cols)
+        step = width // 4
+        for s in range(4):
+            at = slice(s * step, (s + 1) * step)
+            total = nn_dot(left[at, :length], first[...]) + nn_dot(left[at, length:], second[...])
+            out[at, to] = total.astype(BF16)
+
+
+def ffn_partials(own, other, grads, act_own, act_other, d_own, d_other):
+    part, width = own[0].shape
+    length = part * len(own)
+    cols = act_own.shape[1]
+    return pl.pallas_call(
+        functools.partial(ffn_grad_kernel, len(own)),
+        out_shape=jax.ShapeDtypeStruct((width, 3 * cols), BF16),
+        in_specs=[vmem()] * (3 * len(own) + 4),
+        out_specs=vmem(),
+        scratch_shapes=[pltpu.VMEM((width, 2 * length), BF16)],
+        compiler_params=pltpu.CompilerParams(vmem_limit_bytes=VMEM_LIMIT),
+        cost_estimate=pl.CostEstimate(
+            flops=12 * length * width * cols, bytes_accessed=17 << 20, transcendentals=0
+        ),
+        name="ffn_partials",
+    )(*own, *other, *grads, act_own, act_other, d_own, d_other)
+
+
+def ffn_out_kernel(act_own, act_other, weight, keep_out, send_out):
+    length, cols = act_own.shape
+    half = length // 2
+    down = weight[:, 2 * cols :]
+    for seq, act in enumerate((act_own, act_other)):
+        at = slice(seq * half, (seq + 1) * half)
+        keep_out[at, :] = nt_dot(act[:half, :], down)
+        send_out[at, :] = nt_dot(act[half:, :], down).astype(BF16)
+
+
+def ffn_result(act_own, act_other, weight):
+    length, cols = act_own.shape
+    width = weight.shape[0]
+    return pl.pallas_call(
+        ffn_out_kernel,
+        out_shape=(jax.ShapeDtypeStruct((length, width), F32), jax.ShapeDtypeStruct((length, width), BF16)),
+        in_specs=[vmem()] * 3,
+        out_specs=[vmem()] * 2,
+        compiler_params=pltpu.CompilerParams(vmem_limit_bytes=VMEM_LIMIT),
+        cost_estimate=pl.CostEstimate(
+            flops=4 * length * width * cols, bytes_accessed=12 << 20, transcendentals=0
+        ),
+        name="ffn_result",
+    )(act_own, act_other, weight)
+
+
+def grad_kernel(row_parts, blocks, tables, *refs):
     rows, refs = refs[:row_parts], refs[row_parts:]
     right, refs = refs[0], refs[1:]
     keeps, send, left = refs[:blocks], refs[blocks], refs[blocks + 1]
     part, width = rows[0].shape
+    block = keeps[0].shape[0]
     for p in range(row_parts):
         for c in range(width // LANES):
             tile = rows[p][:, c * LANES : (c + 1) * LANES].astype(F32)
             left[c * LANES : (c + 1) * LANES, p * part : (p + 1) * part] = tile.T.astype(BF16)
-    step = width // 4
-    block = keeps[0].shape[0]
-    send[: step, :] = nn_dot(left[2 * step : 3 * step, :], right[...]).astype(BF16)
-    send[step :, :] = nn_dot(left[3 * step :, :], right[...]).astype(BF16)
-    for s in range(2):
-        both = nn_dot(left[s * step : (s + 1) * step, :], right[...])
-        for k in range(step // block):
-            keeps[s * step // block + k][...] = both[k * block : (k + 1) * block].astype(keeps[0].dtype)
-
-
-def weight_partials(rows, right, blocks):
+    for s in range(2 * blocks):
+        at = pl.ds(pl.multiple_of(tables[3, s] * block, block), block)
+        total = nn_dot(left[at, :], right[...]).astype(BF16)
+        if s < blocks:
+            keeps[s][...] = total
+        else:
+            send[(s - blocks) * block : (s - blocks + 1) * block, :] = total
+
+
+def weight_partials(tables, rows, right, blocks):
     part, width = rows[0].shape
     length, cols = right.shape
     block = width // (2 * blocks)
@@ -420,7 +482,7 @@
         functools.partial(grad_kernel, len(rows), blocks),
         out_shape=(jax.ShapeDtypeStruct((block, cols), BF16),) * blocks
         + (jax.ShapeDtypeStruct((width // 2, cols), BF16),),
-        in_specs=[vmem()] * (len(rows) + 1),
+        in_specs=[smem()] + [vmem()] * (len(rows) + 1),
         out_specs=[vmem()] * (blocks + 1),
         scratch_shapes=[pltpu.VMEM((width, length), BF16)],
         compiler_params=pltpu.CompilerParams(vmem_limit_bytes=VMEM_LIMIT),
@@ -428,7 +490,7 @@
             flops=2 * length * width * cols, bytes_accessed=8 << 20, transcendentals=0
         ),
         name="weight_partials",
-    )(*rows, right)
+    )(tables, *rows, right)
 
 
 def hop(values, axis, flip):
@@ -468,10 +530,17 @@
     return out
 
 
+def gather_chips(block):
+    nt = lax.axis_size("tp")
+    return [block] + [hop(block, "tp", 2 * k) for k in range(1, nt // 2)]
+
+
+def with_twins(blocks):
+    return blocks + [hop(block, "tp", 1) for block in blocks]
+
+
 def gather_rows(block):
-    nt = lax.axis_size("tp")
-    mine = [block] + [hop(block, "tp", 2 * k) for k in range(1, nt // 2)]
-    return mine + [hop(piece, "tp", 1) for piece in mine]
+    return with_twins(gather_chips(block))
 
 
 def scatter_rows(keep, send):
@@ -485,13 +554,13 @@
     return out
 
 
-def psum_over(values, axes):
-    for axis in axes:
-        bit = 1
-        while bit < lax.axis_size(axis):
-            values = values + hop(values, axis, bit)
-            bit *= 2
-    return values
+def total_over(values):
+    nt, nz = lax.axis_size("tp"), lax.axis_size("fsdp")
+    values = values + hop(values, "tp", 1)
+    across = hop(values, "ctx", 1)
+    values = values + across
+    values = sum([hop(values, "tp", 2 * k) for k in range(1, nt // 2)], values)
+    return sum([hop(values, "fsdp", k) for k in range(1, nz)], values)
 
 
 def inverse_rms(values):
@@ -531,89 +600,95 @@
     heads = variate_bias.shape[1]
     proj = heads * HEAD
 
-    def to_slots(values):
-        cut = values.reshape(values.shape[0], nz, nx, width // (nz * nx))
-        cut = swap_blocks(swap_blocks(cut, 1, iz, nz), 2, ix, nx)
-        return cut.transpose(0, 2, 1, 3).reshape(values.shape)
-
-    def from_slots(values):
-        cut = values.reshape(values.shape[0], nx, nz, width // (nz * nx)).transpose(0, 2, 1, 3)
-        return swap_blocks(swap_blocks(cut, 1, iz, nz), 2, ix, nx).reshape(values.shape)
-
-    def own_sequence(values):
-        mine = lax.dynamic_index_in_dim(values, ix, 0, keepdims=False)
-        other = lax.dynamic_index_in_dim(values, 1 - ix, 0, keepdims=False)
-        return to_slots(jnp.concatenate([mine, hop(other, "ctx", 1)], axis=0))
-
-    def both_sequences(values):
-        values = from_slots(values)
-        mine, other = values[:share], hop(values[share:], "ctx", 1)
-        first = jnp.where(ix == 0, mine, other)
-        second = jnp.where(ix == 0, other, mine)
-        return jnp.stack([first, second])
-
-    def own_ids(table):
-        return lax.dynamic_index_in_dim(table, ix, 0, keepdims=False)
+    def pick(table, which):
+        return lax.dynamic_index_in_dim(table, which, 0, keepdims=False)
+
+    def swap(mine, theirs):
+        return jnp.where(ix == 0, mine, theirs), jnp.where(ix == 0, theirs, mine)
 
     order = jnp.arange(nx * nt).reshape(nx, nt // 2, 2)
     order = swap_blocks(swap_blocks(swap_blocks(order, 0, ix, nx), 1, it // 2, nt // 2), 2, it % 2, 2)
     order = order.transpose(2, 1, 0).reshape(nx * nt)
+    places = jnp.arange(nz * nx).reshape(nz, nx)
+    places = swap_blocks(swap_blocks(places, 0, iz, nz), 1, ix, nx).transpose(1, 0).reshape(nz * nx)
     tables, cosine, sine, seg_row, seg_wide, feature, coef, hot_rows = attention_tables(
-        own_ids(segment_ids), own_ids(variate_ids), own_ids(time_ids), variate_bias, order, share
+        pick(segment_ids, ix), pick(variate_ids, ix), pick(time_ids, ix), variate_bias, order, places
     )
-    gain_one = to_slots(attn_gain.astype(F32)[None])
-    gain_two = to_slots(ffn_gain.astype(F32)[None])
-    low_inputs = own_sequence(layer_in)
-    inputs = low_inputs.astype(F32)
+    gain_one = attn_gain.astype(F32)[None]
+    gain_two = ffn_gain.astype(F32)[None]
+
+    inputs = jnp.concatenate([pick(layer_in, ix), hop(pick(layer_in, 1 - ix), "ctx", 1)], axis=0).astype(F32)
     inv_one = inverse_rms(inputs)
     rows_one = gather_rows((inputs * inv_one * gain_one).astype(BF16))
-    qkv_w = gather_weight(jnp.concatenate([query_weight, key_weight, value_weight], axis=1))
-    out_w = gather_weight(out_weight)
-    gate_w = gather_weight(gate_weight)
-    up_w = gather_weight(up_weight)
-    down_w = gather_weight(down_weight)
-    grads = own_sequence(out_grad)
-    grad_rows = gather_rows(grads)
+    attn_w = gather_weight(jnp.concatenate([query_weight, key_weight, value_weight, out_weight], axis=1))
+
+    cols = gate_weight.shape[1] // 2
+    pieces = [w.reshape(w.shape[0], 2, cols) for w in (gate_weight, up_weight, down_weight)]
+    mine = jnp.concatenate([lax.dynamic_index_in_dim(w, ix, 1, keepdims=False) for w in pieces], axis=1)
+    theirs = jnp.concatenate([lax.dynamic_index_in_dim(w, 1 - ix, 1, keepdims=False) for w in pieces], axis=1)
+    ffn_w = jnp.concatenate(swap(mine, hop(theirs, "ctx", 1)), axis=0)
+    ffn_w = lax.all_gather(ffn_w, "fsdp", axis=0, tiled=True)
+
+    other_grad = hop(out_grad, "ctx", 1)
+    grads = jnp.concatenate([pick(out_grad, ix), pick(other_grad, ix)], axis=0)
+    grads_next = jnp.concatenate([pick(other_grad, 1 - ix), pick(out_grad, 1 - ix)], axis=0)
+    grad_rows = gather_rows(jnp.concatenate([grads, grads_next], axis=0))
 
     q_aug, k_aug, v_rows, mixed, lse, keep, send = attention_forward(
-        tables, rows_one, qkv_w, out_w, cosine, sine, seg_row, seg_wide, feature, coef, heads
+        tables, rows_one, attn_w, cosine, sine, seg_row, seg_wide, feature, coef, heads
     )
     hidden = inputs + scatter_rows(keep, send)
     inv_two = inverse_rms(hidden)
-    rows_two = gather_rows((hidden * inv_two * gain_two).astype(BF16))
-    act, d_gate, d_up, keep, send = ffn_middle(rows_two, grad_rows, gate_w, up_w, down_w)
+    chips_two = gather_chips((hidden * inv_two * gain_two).astype(BF16))
+    rows_two = with_twins(chips_two)
+    rows_next = with_twins([hop(block, "ctx", 1) for block in chips_two])
+    act, d_both, keep, send = ffn_middle(0, rows_two, grad_rows, ffn_w)
     d_normed_two = scatter_rows(keep, send)
-    down_grad = scatter_weight(weight_partials(grad_rows, act, nz))
-    gate_grad = scatter_weight(weight_partials(rows_two, d_gate, nz))
-    up_grad = scatter_weight(weight_partials(rows_two, d_up, nz))
-
-    down_full = jnp.concatenate(down_w, axis=0)
-    ffn = lax.dot_general(act, down_full, (((1,), (1,)), ((), ())), preferred_element_type=F32)
-    ffn = scatter_rows(ffn[: length // 2], ffn[length // 2 :].astype(BF16))
-    layer_out = both_sequences((hidden + ffn).astype(BF16))
+    act_next, d_both_next, keep, send = ffn_middle(1, rows_next, grad_rows, ffn_w)
+    d_normed_two = d_normed_two + hop(scatter_rows(keep, send).astype(BF16), "ctx", 1).astype(F32)
+
+    ffn_grad = ffn_partials(rows_two, rows_next, grad_rows, act, act_next, d_both, d_both_next)
+    ffn_grad = lax.psum_scatter(ffn_grad, "fsdp", scatter_dimension=0, tiled=True)
+    ffn_grad = ffn_grad.reshape(nx, ffn_grad.shape[0] // nx, ffn_grad.shape[1])
+    low, high = swap(pick(ffn_grad, ix), hop(pick(ffn_grad, 1 - ix), "ctx", 1))
+    gate_grad, up_grad, down_grad = [
+        jnp.concatenate([low[:, k * cols : (k + 1) * cols], high[:, k * cols : (k + 1) * cols]], axis=1).astype(F32)
+        for k in range(3)
+    ]
+
+    keep, send = ffn_result(act, act_next, ffn_w)
+    other = hop(send, "tp", 1)
+    total = (keep + other.astype(F32)).reshape(2, nt // 2, nx * share, width)
+    ffn = total[:, 0]
+    for k in range(1, nt // 2):
+        ffn = ffn + hop(total[:, k].astype(BF16), "tp", 2 * k).astype(F32)
+    mine, theirs = (ffn[0] + hidden).reshape(2, share, width), ffn[1].reshape(2, share, width)
+    sent = hop(jnp.stack([mine[1], theirs[0]]).astype(BF16), "ctx", 1).astype(F32)
+    layer_out = jnp.stack(swap(mine[0] + sent[1], theirs[1] + sent[0])).astype(BF16)
 
     d_hidden_norm, d_gain_two = norm_back(hidden, inv_two, gain_two, d_normed_two)
     d_hidden = grads.astype(F32) + d_hidden_norm
     branch_rows = gather_rows(d_hidden.astype(BF16))
     keep, send, d_qkv, bias_parts = attention_backward(
-        tables, branch_rows, out_w, qkv_w, q_aug, k_aug, v_rows, lse, cosine, sine, seg_row, seg_wide, hot_rows, heads
+        tables, branch_rows, attn_w, q_aug, k_aug, v_rows, lse, cosine, sine, seg_row, seg_wide, hot_rows, heads
     )
     d_normed_one = scatter_rows(keep, send)
-    out_weight_grad = scatter_weight(weight_partials(branch_rows, mixed, nz))
-    qkv_grad = scatter_weight(weight_partials(rows_one, d_qkv, nz))
+    out_weight_grad = scatter_weight(weight_partials(tables, branch_rows, mixed, nz))
+    qkv_grad = scatter_weight(weight_partials(tables, rows_one, d_qkv, nz))
+
+    d_input_norm, d_gain_one = norm_back(inputs, inv_one, gain_one, d_normed_one)
+    d_inputs = (d_hidden + d_input_norm).astype(BF16)
+    in_grad = jnp.stack(swap(d_inputs[:share], hop(d_inputs[share:], "ctx", 1)))
     sums = jnp.sum(bias_parts, axis=2)
-    bias_grad = jnp.stack([jnp.sum(sums[:, :8], axis=1), jnp.sum(sums[:, 8:], axis=1)])
-    bias_grad = psum_over(bias_grad, ("ctx", "fsdp"))
-
-    d_input_norm, d_gain_one = norm_back(inputs, inv_one, gain_one, d_normed_one)
-    in_grad = both_sequences((d_hidden + d_input_norm).astype(BF16))
-    gain_grads = from_slots(jnp.concatenate([d_gain_one, d_gain_two], axis=0))
-    gain_grads = psum_over(gain_grads, ("tp", "ctx", "fsdp"))
+    bias_sums = jnp.stack([jnp.sum(sums[:, :8], axis=1), jnp.sum(sums[:, 8:], axis=1)])
+    spread = lax.dynamic_update_slice(jnp.zeros((2, width), F32), bias_sums, (0, it * heads))
+    totals = total_over(jnp.concatenate([d_gain_one, d_gain_two, spread], axis=0))
+    bias_grad = lax.dynamic_slice(totals, (2, it * heads), (2, heads))
     return (
         layer_out,
         in_grad,
-        gain_grads[0],
-        gain_grads[1],
+        totals[0],
+        totals[1],
         qkv_grad[:, :proj],
         qkv_grad[:, proj : 2 * proj],
         qkv_grad[:, 2 * proj :],

time: 476 us -> 380 us (0.80)
  starting transfers between devices: 158 us -> 57.3 us
  waiting for transfers between devices: 139 us -> 154 us
  between operations: 2.39 us -> 15.2 us
  other arithmetic: 48.3 us -> 37.5 us
  local copies, waits for them, and re-layouts: 37.2 us -> 27.6 us
    ppermute x87 -> x54, starting transfers between devices: 158 us -> 57 us  [hop(): return lax.ppermute(values, axis, [(i, i ^ flip) for i in range(size)])]
    pallas_call x1 -> x4, Pallas kernels: 18.1 us -> 44.7 us  [the longest x2 23.8 us: ffn_middle(): pl.pallas_call(functools.partial(ffn_kernel, len(rows), seq), out_shape=(...]
    pallas_call x5 -> x2, Pallas kernels: 26.1 us -> 9.18 us  [weight_partials(): pl.pallas_call(functools.partial(grad_kernel, len(rows), blocks), out_sha...]
    ppermute x87 -> x54, waiting for transfers between devices: 139 us -> 154 us  [hop(): return lax.ppermute(values, axis, [(i, i ^ flip) for i in range(size)])]
    slice x12 -> x6, local copies, waits for them, and re-layouts: 6.74 us -> 1.69 us  [the longest x1 0.97 us: shards(): in_grad = jnp.stack(swap(d_inputs[:share], hop(d_inputs[share:], 'ctx', 1)))]
    unnamed x173 -> x117, local copies, waits for them, and re-layouts: 12.3 us -> 9.33 us
  transfers between devices with their start and end apart: 87 -> 56, of which waited for: 34 -> 28; matrix products, arithmetic and copies ran while one was open for 16% -> 14% of each run, Pallas kernels for 4% -> 22%
where the time goes in v3:
time: 380 us; the launch traced here: 374 us
  waiting for transfers between devices  154 us (41%)
  Pallas kernels  82.5 us (22%)
  starting transfers between devices  57.3 us (15%)
  other arithmetic  37.5 us (10%)
  local copies, waits for them, and re-layouts  27.6 us (7%)
  between operations  15.2 us (4%)
    ppermute x54, waiting for transfers between devices, hop(): return lax.ppermute(values, axis, [(i, i ^ flip) for i in range(size)])  154 us
    ppermute x54, starting transfers between devices, hop(): return lax.ppermute(values, axis, [(i, i ^ flip) for i in range(size)])  57 us
    pallas_call x2, Pallas kernels, ffn_middle(): pl.pallas_call(functools.partial(ffn_kernel, len(rows), seq), out_shape=(...  23.8 us
    pallas_call x1, Pallas kernels, attention_backward(): pl.pallas_call(functools.partial(bwd_kernel, len(rows), len(weights), hea...  15.9 us
    pallas_call x1, Pallas kernels, ffn_partials(): pl.pallas_call(functools.partial(ffn_grad_kernel, len(own)), out_shape=ja...  13.7 us
    pallas_call x1, Pallas kernels, attention_forward(): pl.pallas_call(functools.partial(fwd_kernel, len(rows), len(weights), hea...  12.7 us
    unnamed x117, local copies, waits for them, and re-layouts  9.33 us
    pallas_call x2, Pallas kernels, weight_partials(): pl.pallas_call(functools.partial(grad_kernel, len(rows), blocks), out_sha...  9.18 us
  transfers between devices with their start and end apart: 56, of which 28 were waited for; matrix products, arithmetic and copies ran while one was open for 14% of the time, Pallas kernels for 22%

profile of v3, /device:TPU:0, one launch (start us, length us, event | category | flops | bytes accessed | tf_op | source)
XLA Modules:
  0.0 373.7 jit_solution(14085877794618488507)
XLA Ops:
  10.6 2.9 collective-permute-start.7
  13.6 3.6 collective-permute-start.6
  21.3 1.9 constant_dynamic-slice_fusion.3
  28.5 1.9 fusion.18
  33.6 6.6 %collective-permute-done = bf16[128,1024]{1,0:T(8,128)(2,1)S(1)} collective-permute-done((bf16[128,1024]{1,0:T(8,128)(2,1)S(1)}, bf16[128,1024]{1,0:T(8,128)(2,1)S(1)}, u32[]{:S(2)}, u32[]{:S(2)}) %collective-permute-start) | collective-permute-done | bytes 262176 | tf_op jit(solution)/shard_map/ppermute | solution.py:498
  44.1 8.9 %collective-permute-done.1.refs_2_.refs_1_ = bf16[256,1024]{1,0:T(8,128)(2,1)} collective-permute-done((bf16[256,1024]{1,0:T(8,128)(2,1)S(1)}, bf16[256,1024]{1,0:T(8,128)(2,1)}, u32[]{:S(2)}, u32[]{:S(2)}) %collective-permute-start.1) | collective-permute-done | bytes 524320 | tf_op jit(solution)/shard_map/ppermute | solution.py:498
  58.7 4.9 %collective-permute-done.10.refs_12_ = bf16[128,1024]{1,0:T(8,128)(2,1)S(1)} collective-permute-done((bf16[128,1024]{1,0:T(8,128)(2,1)}, bf16[128,1024]{1,0:T(8,128)(2,1)S(1)}, u32[]{:S(2)}, u32[]{:S(2)}) %collective-permute-start.10) | collective-permute-done | bytes 262176 | tf_op jit(solution)/shard_map/ppermute | solution.py:498
  63.6 5.6 %collective-permute-done.9.refs_11_ = bf16[128,1024]{1,0:T(8,128)(2,1)S(1)} collective-permute-done((bf16[128,1024]{1,0:T(8,128)(2,1)}, bf16[128,1024]{1,0:T(8,128)(2,1)S(1)}, u32[]{:S(2)}, u32[]{:S(2)}) %collective-permute-start.9) | collective-permute-done | bytes 262176 | tf_op jit(solution)/shard_map/ppermute | solution.py:498
  69.2 5.2 %collective-permute-done.8.refs_10_ = bf16[128,1024]{1,0:T(8,128)(2,1)S(1)} collective-permute-done((bf16[128,1024]{1,0:T(8,128)(2,1)S(1)}, bf16[128,1024]{1,0:T(8,128)(2,1)S(1)}, u32[]{:S(2)}, u32[]{:S(2)}) %collective-permute-start.8) | collective-permute-done | bytes 262176 | tf_op jit(solution)/shard_map/ppermute | solution.py:498
  75.7 12.7 %attn_fwd.1 = (bf16[4,1024,128]{2,1,0:T(8,128)(2,1)}, bf16[4,1024,128]{2,1,0:T(8,128)(2,1)}, bf16[2,1024,128]{2,1,0:T(8,128)(2,1)}, bf16[1024,256]{1,0:T(8,128)(...) custom-call(s32[4,8]{1,0:T(4,128)} %pad_add_fusion.refs_0_.tables, ...), custom_call_target="tpu_custom_call" | custom-call | flops 1610612736 | bytes 8388608 | tf_op jit(solution)/shard_map/attn_fwd/pallas_call | solution.py:155
  88.4 1.8 collective-permute-start.16
  91.3 1.9 convert_add_fusion.4
  94.9 7.8 %collective-permute-done.16 = bf16[2,128,1024]{2,1,0:T(8,128)(2,1)S(1)} collective-permute-done((bf16[2,128,1024]{2,1,0:T(8,128)(2,1)S(1)}, bf16[2,128,1024]{2,1,0:T(8,128)(2,1)S(1)}, u32[]{:S(2)}, u32[]{:S(2)}) %collective-permute-start.16) | collective-permute-done | bytes 524320 | tf_op jit(solution)/shard_map/ppermute | solution.py:498
  104.5 3.6 collective-permute-done.12
  110.2 20.4 %collective-permute-done.17.refs_5_.refs_9_ = bf16[512,1024]{1,0:T(8,128)(2,1)S(1)} collective-permute-done((bf16[512,1024]{1,0:T(8,128)(2,1)S(1)}, bf16[512,1024]{1,0:T(8,128)(2,1)S(1)}, u32[]{:S(2)}, u32[]{:S(2)}) %collective-permute-start.17) | collective-permute-done | bytes 1048608 | tf_op jit(solution)/shard_map/ppermute | solution.py:498
  130.6 1.7 collective-permute-start.21
  132.3 8.8 %collective-permute-done.13.refs_1_ = bf16[256,1024]{1,0:T(8,128)(2,1)} collective-permute-done((bf16[256,1024]{1,0:T(8,128)(2,1)S(1)}, bf16[256,1024]{1,0:T(8,128)(2,1)}, u32[]{:S(2)}, u32[]{:S(2)}) %collective-permute-start.13) | collective-permute-done | bytes 524320 | tf_op jit(solution)/shard_map/ppermute | solution.py:498
  141.1 1.7 collective-permute-start.22
  142.9 2.5 collective-permute-done.21.refs_0_.refs_4_
  145.3 10.8 %collective-permute-done.22.refs_1_.refs_5_ = bf16[256,1024]{1,0:T(8,128)(2,1)S(1)} collective-permute-done((bf16[256,1024]{1,0:T(8,128)(2,1)}, bf16[256,1024]{1,0:T(8,128)(2,1)S(1)}, u32[]{:S(2)}, u32[]{:S(2)}) %collective-permute-start.22) | collective-permute-done | bytes 524320 | tf_op jit(solution)/shard_map/ppermute | solution.py:498
  159.6 11.7 %ffn_middle.3 = (bf16[1024,512]{1,0:T(8,128)(2,1)}, bf16[1024,1024]{1,0:T(8,128)(2,1)}, f32[512,1024]{1,0:T(8,128)}, bf16[512,1024]{1,0:T(8,128)(2,1)}) custom-call(bf16[256,1024]{1,0:T(8,128)(2,1)} %copy-done.50, bf16[256,1024]{1,0:T(8,128)(2,1)} %copy-done.51, bf16[256,1024]{1,0:T(8,128)(2,1)} %copy-done.52, ...), custom_call_target="tpu_custom_call" | custom-call | flops 5368709120 | bytes 16777216 | tf_op jit(solution)/shard_map/ffn_middle/pallas_call | solution.py:368
  172.1 12.0 %ffn_middle.2 = (bf16[1024,512]{1,0:T(8,128)(2,1)}, bf16[1024,1024]{1,0:T(8,128)(2,1)}, f32[512,1024]{1,0:T(8,128)}, bf16[512,1024]{1,0:T(8,128)(2,1)}) custom-call(bf16[256,1024]{1,0:T(8,128)(2,1)} %copy-done.31, bf16[256,1024]{1,0:T(8,128)(2,1)} %collective-permute-done.13.refs_1_, bf16[256,1024]{1,0:T(8,128)(2,1)} %collective-permute-done.14.refs_2_, ...), custom_call_target="tpu_custom_call" | custom-call | flops 5368709120 | bytes 16777216 | tf_op jit(solution)/shard_map/ffn_middle/pallas_call | solution.py:368
  184.2 7.2 %ffn_result.1 = (f32[1024,1024]{1,0:T(8,128)}, bf16[1024,1024]{1,0:T(8,128)(2,1)}) custom-call(bf16[1024,512]{1,0:T(8,128)(2,1)} %get-tuple-element.45.act_own.refs_12_, bf16[1024,512]{1,0:T(8,128)(2,1)} %get-tuple-element.46.act_other.refs_13_, bf16[1024,1536]{1,0:T(8,128)(2,1)} %all-gather.2.cloned.1.call-done.refs_8_.weight), custom_call_target="tpu_custom_call" | custom-call | flops 2147483648 | bytes 12582912 | tf_op jit(solution)/shard_map/ffn_result/pallas_call | solution.py:445
  193.8 3.2 collective-permute-done.28
  199.7 7.3 %collective-permute-done.31 = bf16[256,1024]{1,0:T(8,128)(2,1)S(1)} collective-permute-done((bf16[256,1024]{1,0:T(8,128)(2,1)S(1)}, bf16[256,1024]{1,0:T(8,128)(2,1)S(1)}, u32[]{:S(2)}, u32[]{:S(2)}) %collective-permute-start.31) | collective-permute-done | bytes 524320 | tf_op jit(solution)/shard_map/ppermute | solution.py:498
  210.8 2.0 copy-done
  215.5 13.7 %ffn_partials.1 = bf16[1024,1536]{1,0:T(8,128)(2,1)} custom-call(bf16[256,1024]{1,0:T(8,128)(2,1)} %copy-done.31, bf16[256,1024]{1,0:T(8,128)(2,1)} %collective-permute-done.13.refs_1_, bf16[256,1024]{1,0:T(8,128)(2,1)} %collective-permute-done.14.refs_2_, bf16[256,1024]{1,0:T(8,128)(2,1)} %copy-done.53, bf16[256,1024]{1,0:T(8,128)(2,1)} %copy-done.50, ...), custom_call_target="tpu_custom_call" | custom-call | flops 6442450944 | bytes 17825792 | tf_op jit(solution)/shard_map/ffn_partials/pallas_call | solution.py:418
  230.9 9.5 %collective-permute-done.26 = bf16[2,256,1024]{2,1,0:T(8,128)(2,1)} collective-permute-done((bf16[2,256,1024]{2,1,0:T(8,128)(2,1)}, bf16[2,256,1024]{2,1,0:T(8,128)(2,1)}, u32[]{:S(2)}, u32[]{:S(2)}) %collective-permute-start.26) | collective-permute-done | bytes 1048608 | tf_op jit(solution)/shard_map/ppermute | solution.py:498
  240.4 2.3 fusion
  242.8 3.4 fusion.25
  247.8 11.9 %collective-permute-done.33.refs_2_.refs_1_ = bf16[256,1024]{1,0:T(8,128)(2,1)S(1)} collective-permute-done((bf16[256,1024]{1,0:T(8,128)(2,1)S(1)}, bf16[256,1024]{1,0:T(8,128)(2,1)S(1)}, u32[]{:S(2)}, u32[]{:S(2)}) %collective-permute-start.33) | collective-permute-done | bytes 524320 | tf_op jit(solution)/shard_map/ppermute | solution.py:498
  260.7 1.7 collective-permute-start.27
  264.1 15.9 %attn_bwd.1 = (f32[512,1024]{1,0:T(8,128)}, bf16[512,1024]{1,0:T(8,128)(2,1)}, bf16[1024,768]{1,0:T(8,128)(2,1)}, f32[4,16,256]{2,1,0:T(8,128)}) custom-call(s32[4,8]{1,0:T(4,128)} %pad_add_fusion.refs_0_.tables, bf16[256,1024]{1,0:T(8,128)(2,1)} %copy-done.4, bf16[256,1024]{1,0:T(8,128)(2,1)} %copy-done.16, bf16[256,1024]{1,0:T(8,128)(2,1)} %copy-done.17, ...), custom_call_target="tpu_custom_call" | custom-call | flops 2147483648 | bytes 12582912 | tf_op jit(solution)/shard_map/attn_bwd/pallas_call | solution.py:281
  282.7 3.7 weight_partials.3
  286.5 2.4 collective-permute-start.49
  288.9 5.5 %weight_partials.2 = (bf16[128,768]{1,0:T(8,128)(2,1)}, bf16[128,768]{1,0:T(8,128)(2,1)}, bf16[128,768]{1,0:T(8,128)(2,1)}, bf16[128,768]{1,0:T(8,128)(2,1)}, bf16[512,768]{1,0:T(8,128)(2,1)}) custom-call(s32[4,8]{1,0:T(4,128)} %pad_add_fusion.refs_0_.tables, bf16[256,1024]{1,0:T(8,128)(2,1)} %copy-done.12, ...), custom_call_target="tpu_custom_call" | custom-call | flops 1610612736 | bytes 8388608 | tf_op jit(solution)/shard_map/weight_partials/pallas_call | solution.py:481
  297.4 4.2 %collective-permute-start.52 = (bf16[128,256]{1,0:T(8,128)(2,1)}, bf16[128,256]{1,0:T(8,128)(2,1)}, u32[]{:S(2)}, u32[]{:S(2)}) collective-permute-start(bf16[128,256]{1,0:T(8,128)(2,1)} %get-tuple-element.122), channel_id=1, source_target_pairs={{0,24},{8,16},{16,8},{24,0},{1,25},{9,17},{17,9},{25,1},{2,26},{10... | collective-permute-start | bytes 196616 | tf_op jit(solution)/shard_map/ppermute | solution.py:498
  305.5 1.8 collective-permute-done.51
  308.9 5.2 %collective-permute-done.45 = bf16[512,768]{1,0:T(8,128)(2,1)} collective-permute-done((bf16[512,768]{1,0:T(8,128)(2,1)}, bf16[512,768]{1,0:T(8,128)(2,1)}, u32[]{:S(2)}, u32[]{:S(2)}) %collective-permute-start.45) | collective-permute-done | bytes 786464 | tf_op jit(solution)/shard_map/ppermute | solution.py:498
  316.4 3.9 %collective-permute-start.48 = (bf16[128,768]{1,0:T(8,128)(2,1)S(1)}, bf16[128,768]{1,0:T(8,128)(2,1)S(1)}, u32[]{:S(2)}, u32[]{:S(2)}) collective-permute-start(bf16[128,768]{1,0:T(8,128)(2,1)S(1)} %get-tuple-element.100), channel_id=1, source_target_pairs={{0,24},{8,16},{16,8},{24,0},{1,25},{9,17},{17,9},{25,1},{2,26},{10... | collective-permute-start | bytes 589832 | tf_op jit(solution)/shard_map/ppermute | solution.py:498
  321.6 8.8 %collective-permute-done.48 = bf16[128,768]{1,0:T(8,128)(2,1)S(1)} collective-permute-done((bf16[128,768]{1,0:T(8,128)(2,1)S(1)}, bf16[128,768]{1,0:T(8,128)(2,1)S(1)}, u32[]{:S(2)}, u32[]{:S(2)}) %collective-permute-start.48) | collective-permute-done | bytes 196640 | tf_op jit(solution)/shard_map/ppermute | solution.py:498
  330.5 5.4 %collective-permute-done.47 = bf16[128,768]{1,0:T(8,128)(2,1)S(1)} collective-permute-done((bf16[128,768]{1,0:T(8,128)(2,1)S(1)}, bf16[128,768]{1,0:T(8,128)(2,1)S(1)}, u32[]{:S(2)}, u32[]{:S(2)}) %collective-permute-start.47) | collective-permute-done | bytes 196640 | tf_op jit(solution)/shard_map/ppermute | solution.py:498
  338.3 2.4 collective-permute-done.40
  342.2 2.2 collective-permute-done.41
  344.5 2.6 collective-permute-start.44
  347.1 1.7 collective-permute-start.42
  355.5 4.2 %collective-permute-done.38 = bf16[128,1024]{1,0:T(8,128)(2,1)S(1)} collective-permute-done((bf16[128,1024]{1,0:T(8,128)(2,1)S(1)}, bf16[128,1024]{1,0:T(8,128)(2,1)S(1)}, u32[]{:S(2)}, u32[]{:S(2)}) %collective-permute-start.38) | collective-permute-done | bytes 262176 | tf_op jit(solution)/shard_map/ppermute | solution.py:498
  361.6 2.4 collective-permute-done.53
  (307 shorter events, 84.7 us)
Async XLA Ops:
  7.2 152.4 %all-gather.2.cloned.1.call-start = ((), (), s32[]{:S(2)}) async-start(), calls=%async_computation.1 | async-start | bytes 3932160 | tf_op jit(solution)/shard_map/all_gather | solution.py:630
  10.6 33.4 %collective-permute-start.7 = (bf16[128,1024]{1,0:T(8,128)(2,1)S(1)}, bf16[128,1024]{1,0:T(8,128)(2,1)}, u32[]{:S(2)}, u32[]{:S(2)}) collective-permute-start(bf16[128,1024]{1,0:T(8,128)(2,1)S(1)} %constant_dynamic-update-slice_fusion.refs_5_), channel_id=1, source_target_pairs={{0,4},{4,0},{1,5},{5,1},{2,6},{6,2},{3,7},{7,3},{8,12},{12,8},{9,1... | collective-permute-start | bytes 786440 | tf_op jit(solution)/shard_map/ppermute | solution.py:498
  13.6 40.7 %collective-permute-start.6 = (bf16[128,1024]{1,0:T(8,128)(2,1)S(1)}, bf16[128,1024]{1,0:T(8,128)(2,1)}, u32[]{:S(2)}, u32[]{:S(2)}) collective-permute-start(bf16[128,1024]{1,0:T(8,128)(2,1)S(1)} %constant_dynamic-update-slice_fusion.refs_5_), channel_id=1, source_target_pairs={{0,24},{8,16},{16,8},{24,0},{1,25},{9,17},{17,9},{25,1},{2,26},{10... | collective-permute-start | bytes 786440 | tf_op jit(solution)/shard_map/ppermute | solution.py:498
  17.2 37.7 %collective-permute-start.5 = (bf16[128,1024]{1,0:T(8,128)(2,1)S(1)}, bf16[128,1024]{1,0:T(8,128)(2,1)}, u32[]{:S(2)}, u32[]{:S(2)}) collective-permute-start(bf16[128,1024]{1,0:T(8,128)(2,1)S(1)} %constant_dynamic-update-slice_fusion.refs_5_), channel_id=1, source_target_pairs={{0,16},{8,24},{16,0},{24,8},{1,17},{9,25},{17,1},{25,9},{2,18},{10... | collective-permute-start | bytes 786440 | tf_op jit(solution)/shard_map/ppermute | solution.py:498
  24.0 18.2 %collective-permute-start.20 = (bf16[128,1536]{1,0:T(8,128)(2,1)}, bf16[128,1536]{1,0:T(8,128)(2,1)}, u32[]{:S(2)}, u32[]{:S(2)}) collective-permute-start(bf16[128,1536]{1,0:T(8,128)(2,1)} %pad_maximum_fusion.9), channel_id=1, source_target_pairs={{0,4},{4,0},{1,5},{5,1},{2,6},{6,2},{3,7},{7,3},{8,12},{12,8},{9,1... | collective-permute-start | bytes 1179656 | tf_op jit(solution)/shard_map/ppermute | solution.py:498
  24.6 15.5 %collective-permute-start = (bf16[128,1024]{1,0:T(8,128)(2,1)S(1)}, bf16[128,1024]{1,0:T(8,128)(2,1)S(1)}, u32[]{:S(2)}, u32[]{:S(2)}) collective-permute-start(bf16[128,1024]{1,0:T(8,128)(2,1)S(1)} %get-tuple-element.111), channel_id=1, source_target_pairs={{0,4},{4,0},{1,5},{5,1},{2,6},{6,2},{3,7},{7,3},{8,12},{12,8},{9,1... | collective-permute-start | bytes 786440 | tf_op jit(solution)/shard_map/ppermute | solution.py:498
  40.5 12.5 %collective-permute-start.1 = (bf16[256,1024]{1,0:T(8,128)(2,1)S(1)}, bf16[256,1024]{1,0:T(8,128)(2,1)}, u32[]{:S(2)}, u32[]{:S(2)}) collective-permute-start(bf16[256,1024]{1,0:T(8,128)(2,1)S(1)} %fusion.5.refs_1_.refs_0_), channel_id=1, source_target_pairs={{0,2},{1,3},{2,0},{3,1},{4,6},{5,7},{6,4},{7,5},{8,10},{9,11},{10,... | collective-permute-start | bytes 1572872 | tf_op jit(solution)/shard_map/ppermute | solution.py:498
  42.2 14.1 %collective-permute-start.4 = (bf16[128,1024]{1,0:T(8,128)(2,1)S(1)}, bf16[128,1024]{1,0:T(8,128)(2,1)S(1)}, u32[]{:S(2)}, u32[]{:S(2)}) collective-permute-start(bf16[128,1024]{1,0:T(8,128)(2,1)S(1)} %constant_dynamic-update-slice_fusion.refs_5_), channel_id=1, source_target_pairs={{0,8},{8,0},{16,24},{24,16},{1,9},{9,1},{17,25},{25,17},{2,10},{10... | collective-permute-start | bytes 786440 | tf_op jit(solution)/shard_map/ppermute | solution.py:498
  44.0 30.5 %collective-permute-start.2 = (bf16[256,1024]{1,0:T(8,128)(2,1)S(1)}, bf16[256,1024]{1,0:T(8,128)(2,1)S(1)}, u32[]{:S(2)}, u32[]{:S(2)}) collective-permute-start(bf16[256,1024]{1,0:T(8,128)(2,1)S(1)} %fusion.5.refs_1_.refs_0_), channel_id=1, source_target_pairs={{0,1},{1,0},{2,3},{3,2},{4,5},{5,4},{6,7},{7,6},{8,9},{9,8},{10,11... | collective-permute-start | bytes 1572872 | tf_op jit(solution)/shard_map/ppermute | solution.py:498
  53.0 21.5 %collective-permute-start.3 = (bf16[256,1024]{1,0:T(8,128)(2,1)}, bf16[256,1024]{1,0:T(8,128)(2,1)}, u32[]{:S(2)}, u32[]{:S(2)}) collective-permute-start(bf16[256,1024]{1,0:T(8,128)(2,1)} %collective-permute-done.1.refs_2_.refs_1_), channel_id=1, source_target_pairs={{0,1},{1,0},{2,3},{3,2},{4,5},{5,4},{6,7},{7,6},{8,9},{9,8},{10,11... | collective-permute-start | bytes 1572872 | tf_op jit(solution)/shard_map/ppermute | solution.py:498
  54.0 298.4 %reduce-scatter.2.cloned.1.call-start = ((), (), s32[]{:S(2)}) async-start(), calls=%async_computation.2 | async-start | bytes 3932160 | tf_op jit(solution)/shard_map/reduce_scatter | solution.py:651
  54.2 9.4 %collective-permute-start.10 = (bf16[128,1024]{1,0:T(8,128)(2,1)}, bf16[128,1024]{1,0:T(8,128)(2,1)S(1)}, u32[]{:S(2)}, u32[]{:S(2)}) collective-permute-start(bf16[128,1024]{1,0:T(8,128)(2,1)} %collective-permute-done.6.refs_8_), channel_id=1, source_target_pairs={{0,4},{4,0},{1,5},{5,1},{2,6},{6,2},{3,7},{7,3},{8,12},{12,8},{9,1... | collective-permute-start | bytes 786440 | tf_op jit(solution)/shard_map/ppermute | solution.py:498
  54.8 14.4 %collective-permute-start.9 = (bf16[128,1024]{1,0:T(8,128)(2,1)}, bf16[128,1024]{1,0:T(8,128)(2,1)S(1)}, u32[]{:S(2)}, u32[]{:S(2)}) collective-permute-start(bf16[128,1024]{1,0:T(8,128)(2,1)} %collective-permute-done.5.refs_7_), channel_id=1, source_target_pairs={{0,4},{4,0},{1,5},{5,1},{2,6},{6,2},{3,7},{7,3},{8,12},{12,8},{9,1... | collective-permute-start | bytes 786440 | tf_op jit(solution)/shard_map/ppermute | solution.py:498
  56.3 18.1 %collective-permute-start.8 = (bf16[128,1024]{1,0:T(8,128)(2,1)S(1)}, bf16[128,1024]{1,0:T(8,128)(2,1)S(1)}, u32[]{:S(2)}, u32[]{:S(2)}) collective-permute-start(bf16[128,1024]{1,0:T(8,128)(2,1)S(1)} %collective-permute-done.4.refs_6_), channel_id=1, source_target_pairs={{0,4},{4,0},{1,5},{5,1},{2,6},{6,2},{3,7},{7,3},{8,12},{12,8},{9,1... | collective-permute-start | bytes 786440 | tf_op jit(solution)/shard_map/ppermute | solution.py:498
  88.4 14.3 %collective-permute-start.16 = (bf16[2,128,1024]{2,1,0:T(8,128)(2,1)S(1)}, bf16[2,128,1024]{2,1,0:T(8,128)(2,1)S(1)}, u32[]{:S(2)}, u32[]{:S(2)}) collective-permute-start(bf16[2,128,1024]{2,1,0:T(8,128)(2,1)S(1)} %copy-done.30), channel_id=1, source_target_pairs={{0,4},{4,0},{1,5},{5,1},{2,6},{6,2},{3,7},{7,3},{8,12},{12,8},{9,1... | collective-permute-start | bytes 1572872 | tf_op jit(solution)/shard_map/ppermute | solution.py:498
  93.3 14.8 %collective-permute-start.12 = (bf16[256,1024]{1,0:T(8,128)(2,1)S(1)}, bf16[256,1024]{1,0:T(8,128)(2,1)S(1)}, u32[]{:S(2)}, u32[]{:S(2)}) collective-permute-start(bf16[256,1024]{1,0:T(8,128)(2,1)S(1)} %slice.307), channel_id=1, source_target_pairs={{0,2},{1,3},{2,0},{3,1},{4,6},{5,7},{6,4},{7,5},{8,10},{9,11},{10,... | collective-permute-start | bytes 1572872 | tf_op jit(solution)/shard_map/ppermute | solution.py:498
  102.9 27.7 %collective-permute-start.17 = (bf16[512,1024]{1,0:T(8,128)(2,1)S(1)}, bf16[512,1024]{1,0:T(8,128)(2,1)S(1)}, u32[]{:S(2)}, u32[]{:S(2)}) collective-permute-start(bf16[512,1024]{1,0:T(8,128)(2,1)S(1)} %pad_maximum_fusion.refs_4_.refs_8_), channel_id=1, source_target_pairs={{0,2},{1,3},{2,0},{3,1},{4,6},{5,7},{6,4},{7,5},{8,10},{9,11},{10,... | collective-permute-start | bytes 3145736 | tf_op jit(solution)/shard_map/ppermute | solution.py:498
  108.6 32.5 %collective-permute-start.13 = (bf16[256,1024]{1,0:T(8,128)(2,1)S(1)}, bf16[256,1024]{1,0:T(8,128)(2,1)}, u32[]{:S(2)}, u32[]{:S(2)}) collective-permute-start(bf16[256,1024]{1,0:T(8,128)(2,1)S(1)} %multiply_convert_fusion.refs_0_), channel_id=1, source_target_pairs={{0,2},{1,3},{2,0},{3,1},{4,6},{5,7},{6,4},{7,5},{8,10},{9,11},{10,... | collective-permute-start | bytes 1572872 | tf_op jit(solution)/shard_map/ppermute | solution.py:498
  110.2 46.5 %collective-permute-start.18 = (bf16[512,1024]{1,0:T(8,128)(2,1)S(1)}, bf16[512,1024]{1,0:T(8,128)(2,1)S(1)}, u32[]{:S(2)}, u32[]{:S(2)}) collective-permute-start(bf16[512,1024]{1,0:T(8,128)(2,1)S(1)} %pad_maximum_fusion.refs_4_.refs_8_), channel_id=1, source_target_pairs={{0,1},{1,0},{2,3},{3,2},{4,5},{5,4},{6,7},{7,6},{8,9},{9,8},{10,11... | collective-permute-start | bytes 3145736 | tf_op jit(solution)/shard_map/ppermute | solution.py:498
  130.6 26.2 %collective-permute-start.19 = (bf16[512,1024]{1,0:T(8,128)(2,1)S(1)}, bf16[512,1024]{1,0:T(8,128)(2,1)S(1)}, u32[]{:S(2)}, u32[]{:S(2)}) collective-permute-start(bf16[512,1024]{1,0:T(8,128)(2,1)S(1)} %collective-permute-done.17.refs_5_.refs_9_), channel_id=1, source_target_pairs={{0,1},{1,0},{2,3},{3,2},{4,5},{5,4},{6,7},{7,6},{8,9},{9,8},{10,11... | collective-permute-start | bytes 3145736 | tf_op jit(solution)/shard_map/ppermute | solution.py:498
  130.6 14.7 %collective-permute-start.21 = (bf16[256,1024]{1,0:T(8,128)(2,1)S(1)}, bf16[256,1024]{1,0:T(8,128)(2,1)S(1)}, u32[]{:S(2)}, u32[]{:S(2)}) collective-permute-start(bf16[256,1024]{1,0:T(8,128)(2,1)S(1)} %multiply_convert_fusion.refs_0_), channel_id=1, source_target_pairs={{0,4},{4,0},{1,5},{5,1},{2,6},{6,2},{3,7},{7,3},{8,12},{12,8},{9,1... | collective-permute-start | bytes 1572872 | tf_op jit(solution)/shard_map/ppermute | solution.py:498
  141.1 15.0 %collective-permute-start.22 = (bf16[256,1024]{1,0:T(8,128)(2,1)}, bf16[256,1024]{1,0:T(8,128)(2,1)S(1)}, u32[]{:S(2)}, u32[]{:S(2)}) collective-permute-start(bf16[256,1024]{1,0:T(8,128)(2,1)} %collective-permute-done.13.refs_1_), channel_id=1, source_target_pairs={{0,4},{4,0},{1,5},{5,1},{2,6},{6,2},{3,7},{7,3},{8,12},{12,8},{9,1... | collective-permute-start | bytes 1572872 | tf_op jit(solution)/shard_map/ppermute | solution.py:498
  145.3 12.5 %collective-permute-start.23 = (bf16[256,1024]{1,0:T(8,128)(2,1)S(1)}, bf16[256,1024]{1,0:T(8,128)(2,1)S(1)}, u32[]{:S(2)}, u32[]{:S(2)}) collective-permute-start(bf16[256,1024]{1,0:T(8,128)(2,1)S(1)} %collective-permute-done.21.refs_0_.refs_4_), channel_id=1, source_target_pairs={{0,1},{1,0},{2,3},{3,2},{4,5},{5,4},{6,7},{7,6},{8,9},{9,8},{10,11... | collective-permute-start | bytes 1572872 | tf_op jit(solution)/shard_map/ppermute | solution.py:498
  156.2 15.1 %collective-permute-start.14 = (bf16[256,1024]{1,0:T(8,128)(2,1)S(1)}, bf16[256,1024]{1,0:T(8,128)(2,1)}, u32[]{:S(2)}, u32[]{:S(2)}) collective-permute-start(bf16[256,1024]{1,0:T(8,128)(2,1)S(1)} %multiply_convert_fusion.refs_0_), channel_id=1, source_target_pairs={{0,1},{1,0},{2,3},{3,2},{4,5},{5,4},{6,7},{7,6},{8,9},{9,8},{10,11... | collective-permute-start | bytes 1572872 | tf_op jit(solution)/shard_map/ppermute | solution.py:498
  156.7 14.6 %collective-permute-start.15 = (bf16[256,1024]{1,0:T(8,128)(2,1)}, bf16[256,1024]{1,0:T(8,128)(2,1)S(1)}, u32[]{:S(2)}, u32[]{:S(2)}) collective-permute-start(bf16[256,1024]{1,0:T(8,128)(2,1)} %collective-permute-done.13.refs_1_), channel_id=1, source_target_pairs={{0,1},{1,0},{2,3},{3,2},{4,5},{5,4},{6,7},{7,6},{8,9},{9,8},{10,11... | collective-permute-start | bytes 1572872 | tf_op jit(solution)/shard_map/ppermute | solution.py:498
  171.3 20.6 %collective-permute-start.30 = (bf16[512,1024]{1,0:T(8,128)(2,1)}, bf16[512,1024]{1,0:T(8,128)(2,1)S(1)}, u32[]{:S(2)}, u32[]{:S(2)}) collective-permute-start(bf16[512,1024]{1,0:T(8,128)(2,1)} %get-tuple-element.52), channel_id=1, source_target_pairs={{0,1},{1,0},{2,3},{3,2},{4,5},{5,4},{6,7},{7,6},{8,9},{9,8},{10,11... | collective-permute-start | bytes 3145736 | tf_op jit(solution)/shard_map/ppermute | solution.py:498
  191.3 18.4 %collective-permute-start.25 = (bf16[1024,1024]{1,0:T(8,128)(2,1)}, bf16[1024,1024]{1,0:T(8,128)(2,1)S(1)}, u32[]{:S(2)}, u32[]{:S(2)}) collective-permute-start(bf16[1024,1024]{1,0:T(8,128)(2,1)} %get-tuple-element.48), channel_id=1, source_target_pairs={{0,1},{1,0},{2,3},{3,2},{4,5},{5,4},{6,7},{7,6},{8,9},{9,8},{10,11... | collective-permute-start | bytes 6291464 | tf_op jit(solution)/shard_map/ppermute | solution.py:498
  192.3 14.8 %collective-permute-start.31 = (bf16[256,1024]{1,0:T(8,128)(2,1)S(1)}, bf16[256,1024]{1,0:T(8,128)(2,1)S(1)}, u32[]{:S(2)}, u32[]{:S(2)}) collective-permute-start(bf16[256,1024]{1,0:T(8,128)(2,1)S(1)} %slice.305), channel_id=1, source_target_pairs={{0,2},{1,3},{2,0},{3,1},{4,6},{5,7},{6,4},{7,5},{8,10},{9,11},{10,... | collective-permute-start | bytes 1572872 | tf_op jit(solution)/shard_map/ppermute | solution.py:498
  198.2 31.0 %collective-permute-start.29 = (bf16[256,1024]{1,0:T(8,128)(2,1)}, bf16[256,1024]{1,0:T(8,128)(2,1)}, u32[]{:S(2)}, u32[]{:S(2)}) collective-permute-start(bf16[256,1024]{1,0:T(8,128)(2,1)} %slice.306), channel_id=1, source_target_pairs={{0,2},{1,3},{2,0},{3,1},{4,6},{5,7},{6,4},{7,5},{8,10},{9,11},{10,... | collective-permute-start | bytes 1572872 | tf_op jit(solution)/shard_map/ppermute | solution.py:498
  208.0 21.2 %collective-permute-start.32 = (bf16[256,1024]{1,0:T(8,128)(2,1)}, bf16[256,1024]{1,0:T(8,128)(2,1)}, u32[]{:S(2)}, u32[]{:S(2)}) collective-permute-start(bf16[256,1024]{1,0:T(8,128)(2,1)} %fusion.14), channel_id=1, source_target_pairs={{0,4},{4,0},{1,5},{5,1},{2,6},{6,2},{3,7},{7,3},{8,12},{12,8},{9,1... | collective-permute-start | bytes 1572872 | tf_op jit(solution)/shard_map/ppermute | solution.py:498
  213.9 26.5 %collective-permute-start.26 = (bf16[2,256,1024]{2,1,0:T(8,128)(2,1)}, bf16[2,256,1024]{2,1,0:T(8,128)(2,1)}, u32[]{:S(2)}, u32[]{:S(2)}) collective-permute-start(bf16[2,256,1024]{2,1,0:T(8,128)(2,1)} %fusion.13), channel_id=1, source_target_pairs={{0,2},{1,3},{2,0},{3,1},{4,6},{5,7},{6,4},{7,5},{8,10},{9,11},{10,... | collective-permute-start | bytes 3145736 | tf_op jit(solution)/shard_map/ppermute | solution.py:498
  246.2 13.6 %collective-permute-start.33 = (bf16[256,1024]{1,0:T(8,128)(2,1)S(1)}, bf16[256,1024]{1,0:T(8,128)(2,1)S(1)}, u32[]{:S(2)}, u32[]{:S(2)}) collective-permute-start(bf16[256,1024]{1,0:T(8,128)(2,1)S(1)} %get-tuple-element.84.refs_1_.refs_0_), channel_id=1, source_target_pairs={{0,2},{1,3},{2,0},{3,1},{4,6},{5,7},{6,4},{7,5},{8,10},{9,11},{10,... | collective-permute-start | bytes 1572872 | tf_op jit(solution)/shard_map/ppermute | solution.py:498
  247.7 15.4 %collective-permute-start.34 = (bf16[256,1024]{1,0:T(8,128)(2,1)S(1)}, bf16[256,1024]{1,0:T(8,128)(2,1)S(1)}, u32[]{:S(2)}, u32[]{:S(2)}) collective-permute-start(bf16[256,1024]{1,0:T(8,128)(2,1)S(1)} %get-tuple-element.84.refs_1_.refs_0_), channel_id=1, source_target_pairs={{0,1},{1,0},{2,3},{3,2},{4,5},{5,4},{6,7},{7,6},{8,9},{9,8},{10,11... | collective-permute-start | bytes 1572872 | tf_op jit(solution)/shard_map/ppermute | solution.py:498
  260.7 19.6 %collective-permute-start.27 = (bf16[2,128,1024]{2,1,0:T(8,128)(2,1)}, bf16[2,128,1024]{2,1,0:T(8,128)(2,1)S(1)}, u32[]{:S(2)}, u32[]{:S(2)}) collective-permute-start(bf16[2,128,1024]{2,1,0:T(8,128)(2,1)} %pad_maximum_fusion.5), channel_id=1, source_target_pairs={{0,4},{4,0},{1,5},{5,1},{2,6},{6,2},{3,7},{7,3},{8,12},{12,8},{9,1... | collective-permute-start | bytes 1572872 | tf_op jit(solution)/shard_map/ppermute | solution.py:498
  280.0 21.6 %collective-permute-start.36 = (bf16[512,1024]{1,0:T(8,128)(2,1)}, bf16[512,1024]{1,0:T(8,128)(2,1)S(1)}, u32[]{:S(2)}, u32[]{:S(2)}) collective-permute-start(bf16[512,1024]{1,0:T(8,128)(2,1)} %get-tuple-element.58), channel_id=1, source_target_pairs={{0,1},{1,0},{2,3},{3,2},{4,5},{5,4},{6,7},{7,6},{8,9},{9,8},{10,11... | collective-permute-start | bytes 3145736 | tf_op jit(solution)/shard_map/ppermute | solution.py:498
  286.5 9.4 %collective-permute-start.49 = (bf16[512,256]{1,0:T(8,128)(2,1)}, bf16[512,256]{1,0:T(8,128)(2,1)S(1)}, u32[]{:S(2)}, u32[]{:S(2)}) collective-permute-start(bf16[512,256]{1,0:T(8,128)(2,1)} %get-tuple-element.68), channel_id=1, source_target_pairs={{0,4},{4,0},{1,5},{5,1},{2,6},{6,2},{3,7},{7,3},{8,12},{12,8},{9,1... | collective-permute-start | bytes 786440 | tf_op jit(solution)/shard_map/ppermute | solution.py:498
  294.3 19.8 %collective-permute-start.45 = (bf16[512,768]{1,0:T(8,128)(2,1)}, bf16[512,768]{1,0:T(8,128)(2,1)}, u32[]{:S(2)}, u32[]{:S(2)}) collective-permute-start(bf16[512,768]{1,0:T(8,128)(2,1)} %get-tuple-element.62), channel_id=1, source_target_pairs={{0,4},{4,0},{1,5},{5,1},{2,6},{6,2},{3,7},{7,3},{8,12},{12,8},{9,1... | collective-permute-start | bytes 2359304 | tf_op jit(solution)/shard_map/ppermute | solution.py:498
  296.6 7.9 %collective-permute-start.50 = (bf16[128,256]{1,0:T(8,128)(2,1)}, bf16[128,256]{1,0:T(8,128)(2,1)S(1)}, u32[]{:S(2)}, u32[]{:S(2)}) collective-permute-start(bf16[128,256]{1,0:T(8,128)(2,1)} %get-tuple-element.121), channel_id=1, source_target_pairs={{0,8},{8,0},{16,24},{24,16},{1,9},{9,1},{17,25},{25,17},{2,10},{10... | collective-permute-start | bytes 196616 | tf_op jit(solution)/shard_map/ppermute | solution.py:498
  297.4 8.1 %collective-permute-start.52 = (bf16[128,256]{1,0:T(8,128)(2,1)}, bf16[128,256]{1,0:T(8,128)(2,1)}, u32[]{:S(2)}, u32[]{:S(2)}) collective-permute-start(bf16[128,256]{1,0:T(8,128)(2,1)} %get-tuple-element.122), channel_id=1, source_target_pairs={{0,24},{8,16},{16,8},{24,0},{1,25},{9,17},{17,9},{25,1},{2,26},{10... | collective-permute-start | bytes 196616 | tf_op jit(solution)/shard_map/ppermute | solution.py:498
  301.6 5.7 %collective-permute-start.51 = (bf16[128,256]{1,0:T(8,128)(2,1)}, bf16[128,256]{1,0:T(8,128)(2,1)}, u32[]{:S(2)}, u32[]{:S(2)}) collective-permute-start(bf16[128,256]{1,0:T(8,128)(2,1)} %get-tuple-element.123), channel_id=1, source_target_pairs={{0,16},{8,24},{16,0},{24,8},{1,17},{9,25},{17,1},{25,9},{2,18},{10... | collective-permute-start | bytes 196616 | tf_op jit(solution)/shard_map/ppermute | solution.py:498
  302.8 17.5 %collective-permute-start.37 = (bf16[256,1024]{1,0:T(8,128)(2,1)}, bf16[256,1024]{1,0:T(8,128)(2,1)S(1)}, u32[]{:S(2)}, u32[]{:S(2)}) collective-permute-start(bf16[256,1024]{1,0:T(8,128)(2,1)} %slice.304), channel_id=1, source_target_pairs={{0,2},{1,3},{2,0},{3,1},{4,6},{5,7},{6,4},{7,5},{8,10},{9,11},{10,... | collective-permute-start | bytes 1572872 | tf_op jit(solution)/shard_map/ppermute | solution.py:498
  315.6 6.0 %collective-permute-start.46 = (bf16[128,768]{1,0:T(8,128)(2,1)S(1)}, bf16[128,768]{1,0:T(8,128)(2,1)S(1)}, u32[]{:S(2)}, u32[]{:S(2)}) collective-permute-start(bf16[128,768]{1,0:T(8,128)(2,1)S(1)} %get-tuple-element.99), channel_id=1, source_target_pairs={{0,8},{8,0},{16,24},{24,16},{1,9},{9,1},{17,25},{25,17},{2,10},{10... | collective-permute-start | bytes 589832 | tf_op jit(solution)/shard_map/ppermute | solution.py:498
  316.4 14.0 %collective-permute-start.48 = (bf16[128,768]{1,0:T(8,128)(2,1)S(1)}, bf16[128,768]{1,0:T(8,128)(2,1)S(1)}, u32[]{:S(2)}, u32[]{:S(2)}) collective-permute-start(bf16[128,768]{1,0:T(8,128)(2,1)S(1)} %get-tuple-element.100), channel_id=1, source_target_pairs={{0,24},{8,16},{16,8},{24,0},{1,25},{9,17},{17,9},{25,1},{2,26},{10... | collective-permute-start | bytes 589832 | tf_op jit(solution)/shard_map/ppermute | solution.py:498
  320.3 15.5 %collective-permute-start.47 = (bf16[128,768]{1,0:T(8,128)(2,1)S(1)}, bf16[128,768]{1,0:T(8,128)(2,1)S(1)}, u32[]{:S(2)}, u32[]{:S(2)}) collective-permute-start(bf16[128,768]{1,0:T(8,128)(2,1)S(1)} %get-tuple-element.101), channel_id=1, source_target_pairs={{0,16},{8,24},{16,0},{24,8},{1,17},{9,25},{17,1},{25,9},{2,18},{10... | collective-permute-start | bytes 589832 | tf_op jit(solution)/shard_map/ppermute | solution.py:498
  320.9 16.0 %collective-permute-start.39 = (f32[4,1024]{1,0:T(4,128)S(1)}, f32[4,1024]{1,0:T(4,128)S(1)}, u32[]{:S(2)}, u32[]{:S(2)}) collective-permute-start(f32[4,1024]{1,0:T(4,128)S(1)} %pad_maximum_fusion.11), channel_id=1, source_target_pairs={{0,1},{1,0},{2,3},{3,2},{4,5},{5,4},{6,7},{7,6},{8,9},{9,8},{10,11... | collective-permute-start | bytes 49160 | tf_op jit(solution)/shard_map/ppermute | solution.py:498
  344.5 7.2 %collective-permute-start.44 = (f32[4,1024]{1,0:T(4,128)S(1)}, f32[4,1024]{1,0:T(4,128)S(1)}, u32[]{:S(2)}, u32[]{:S(2)}) collective-permute-start(f32[4,1024]{1,0:T(4,128)S(1)} %add.259), channel_id=1, source_target_pairs={{0,24},{8,16},{16,8},{24,0},{1,25},{9,17},{17,9},{25,1},{2,26},{10... | collective-permute-start | bytes 49160 | tf_op jit(solution)/shard_map/ppermute | solution.py:498
  351.0 8.8 %collective-permute-start.38 = (bf16[128,1024]{1,0:T(8,128)(2,1)S(1)}, bf16[128,1024]{1,0:T(8,128)(2,1)S(1)}, u32[]{:S(2)}, u32[]{:S(2)}) collective-permute-start(bf16[128,1024]{1,0:T(8,128)(2,1)S(1)} %slice.213), channel_id=1, source_target_pairs={{0,4},{4,0},{1,5},{5,1},{2,6},{6,2},{3,7},{7,3},{8,12},{12,8},{9,1... | collective-permute-start | bytes 786440 | tf_op jit(solution)/shard_map/ppermute | solution.py:498
  353.5 10.5 %collective-permute-start.53 = (bf16[128,1536]{1,0:T(8,128)(2,1)S(1)}, bf16[128,1536]{1,0:T(8,128)(2,1)S(1)}, u32[]{:S(2)}, u32[]{:S(2)}) collective-permute-start(bf16[128,1536]{1,0:T(8,128)(2,1)S(1)} %dynamic-slice_bitcast_fusion), channel_id=1, source_target_pairs={{0,4},{4,0},{1,5},{5,1},{2,6},{6,2},{3,7},{7,3},{8,12},{12,8},{9,1... | collective-permute-start | bytes 1179656 | tf_op jit(solution)/shard_map/ppermute | solution.py:498
  (62 other events, 663.2 us)
Sparse Core Ops, SparseCore 0:
  54.1 62.6 all-gather.1
  229.3 59.1 reduce-scatter.1

commit v4 on v3

--- a/solution.py
+++ b/solution.py
@@ -46,8 +46,8 @@
     rows, refs = refs[:row_parts], refs[row_parts:]
     weights, refs = refs[:weight_parts], refs[weight_parts:]
     cosine, sine, seg_row, seg_wide, feature, coef = refs[:6]
-    q_aug, k_aug, v_out, mixed_out, lse_out, keep_out, send_out = refs[6:13]
-    full, out_full, mixed_wide, v_turn = refs[13:]
+    q_aug, k_aug, v_out, mixed_out, lse_out, keep_out, rest_out, send_own, send_rest = refs[6:15]
+    full, out_full, mixed_wide, v_turn = refs[15:]
     pairs = heads // 2
     proj = heads * HEAD
     length = q_aug.shape[1]
@@ -124,39 +124,51 @@
     half = row_parts // 2
     for p in range(row_parts):
         back = nt_dot(mixed_out[p * part : (p + 1) * part, :], out_full[...])
-        if p < half:
-            keep_out[p * part : (p + 1) * part, :] = back
+        if p == 0:
+            keep_out[...] = back
+        elif p < half:
+            rest_out[(p - 1) * part : p * part, :] = back
         else:
-            send_out[(p - half) * part : (p - half + 1) * part, :] = back.astype(BF16)
+            if p == half:
+                send_own[...] = back.astype(BF16)
+            else:
+                send_rest[(p - half - 1) * part : (p - half) * part, :] = back.astype(BF16)
 
 
 def vmem():
     return pl.BlockSpec(memory_space=pltpu.VMEM)
 
 
+def anywhere():
+    return pl.BlockSpec(memory_space=pl.ANY)
+
+
 def smem():
     return pl.BlockSpec(memory_space=pltpu.SMEM)
 
 
-def attention_forward(tables, rows, weights, cosine, sine, seg_row, seg_wide, feature, coef, heads):
+def attention_forward(tables, rows, weights, cosine, sine, seg_row, seg_wide, feature, coef, heads, behind=()):
     proj = heads * HEAD
     length = cosine.shape[0]
-    width = rows[0].shape[1]
+    part, width = rows[0].shape
     shapes = (
         jax.ShapeDtypeStruct((heads, length, LANES), BF16),
         jax.ShapeDtypeStruct((heads, length, LANES), BF16),
         jax.ShapeDtypeStruct((heads // 2, length, LANES), BF16),
         jax.ShapeDtypeStruct((length, proj), BF16),
         jax.ShapeDtypeStruct((heads, length // QUERIES, QUERIES), F32),
-        jax.ShapeDtypeStruct((length // 2, width), F32),
-        jax.ShapeDtypeStruct((length // 2, width), BF16),
+        jax.ShapeDtypeStruct((part, width), F32),
+        jax.ShapeDtypeStruct((length // 2 - part, width), F32),
+        jax.ShapeDtypeStruct((part, width), BF16),
+        jax.ShapeDtypeStruct((length // 2 - part, width), BF16),
     )
     count = len(rows) + len(weights) + 6
+    operands = (tables, *rows, *weights, cosine, sine, seg_row, seg_wide, feature, coef)
     return pl.pallas_call(
-        functools.partial(fwd_kernel, len(rows), len(weights), heads),
+        without(functools.partial(fwd_kernel, len(rows), len(weights), heads), len(operands), len(behind)),
         out_shape=shapes,
-        in_specs=[smem()] + [vmem()] * count,
-        out_specs=[vmem()] * 7,
+        in_specs=[smem()] + [vmem()] * count + [anywhere()] * len(behind),
+        out_specs=[vmem()] * 9,
         scratch_shapes=[
             pltpu.VMEM((width, 3 * proj), BF16),
             pltpu.VMEM((width, proj), BF16),
@@ -168,7 +180,7 @@
             flops=2 * length * width * 3 * proj, bytes_accessed=8 << 20, transcendentals=length * length * heads // 2
         ),
         name="attn_fwd",
-    )(tables, *rows, *weights, cosine, sine, seg_row, seg_wide, feature, coef)
+    )(*operands, *behind)
 
 
 def bwd_kernel(row_parts, weight_parts, heads, *refs):
@@ -176,8 +188,8 @@
     rows, refs = refs[:row_parts], refs[row_parts:]
     weights, refs = refs[:weight_parts], refs[weight_parts:]
     q_aug, k_aug, v_in, lse, cosine, sine, seg_row, seg_wide, hot_rows = refs[:9]
-    keep_out, send_out, d_qkv_out, bias_out = refs[9:13]
-    full, out_full, d_out, k_turn, dq_acc, dk_acc, dv_acc = refs[13:]
+    keep_out, rest_out, send_own, send_rest, d_qkv_out, bias_out = refs[9:15]
+    full, out_full, d_out, k_turn, dq_acc, dk_acc, dv_acc = refs[15:]
     pairs = heads // 2
     proj = heads * HEAD
     length = q_aug.shape[1]
@@ -261,28 +273,36 @@
         part_rows = d_qkv_out[p * part : (p + 1) * part, :]
         back = nt_dot(part_rows, full[...])
         half = row_parts // 2
-        if p < half:
-            keep_out[p * part : (p + 1) * part, :] = back
+        if p == 0:
+            keep_out[...] = back
+        elif p < half:
+            rest_out[(p - 1) * part : p * part, :] = back
         else:
-            send_out[(p - half) * part : (p - half + 1) * part, :] = back.astype(BF16)
-
-
-def attention_backward(tables, rows, weights, q_aug, k_aug, v_in, lse, cosine, sine, seg_row, seg_wide, hot_rows, heads):
+            if p == half:
+                send_own[...] = back.astype(BF16)
+            else:
+                send_rest[(p - half - 1) * part : (p - half) * part, :] = back.astype(BF16)
+
+
+def attention_backward(tables, rows, weights, q_aug, k_aug, v_in, lse, cosine, sine, seg_row, seg_wide, hot_rows, heads, behind=()):
     proj = heads * HEAD
     length = cosine.shape[0]
-    width = rows[0].shape[1]
+    part, width = rows[0].shape
     shapes = (
-        jax.ShapeDtypeStruct((length // 2, width), F32),
-        jax.ShapeDtypeStruct((length // 2, width), BF16),
+        jax.ShapeDtypeStruct((part, width), F32),
+        jax.ShapeDtypeStruct((length // 2 - part, width), F32),
+        jax.ShapeDtypeStruct((part, width), BF16),
+        jax.ShapeDtypeStruct((length // 2 - part, width), BF16),
         jax.ShapeDtypeStruct((length, 3 * proj), BF16),
         jax.ShapeDtypeStruct((heads, 16, QUERIES), F32),
     )
     count = len(rows) + len(weights) + 9
+    operands = (tables, *rows, *weights, q_aug, k_aug, v_in, lse, cosine, sine, seg_row, seg_wide, hot_rows)
     return pl.pallas_call(
-        functools.partial(bwd_kernel, len(rows), len(weights), heads),
+        without(functools.partial(bwd_kernel, len(rows), len(weights), heads), len(operands), len(behind)),
         out_shape=shapes,
-        in_specs=[smem()] + [vmem()] * count,
-        out_specs=[vmem()] * 4,
+        in_specs=[smem()] + [vmem()] * count + [anywhere()] * len(behind),
+        out_specs=[vmem()] * 6,
         scratch_shapes=[
             pltpu.VMEM((width, 3 * proj), BF16),
             pltpu.VMEM((width, proj), BF16),
@@ -297,7 +317,7 @@
             flops=2 * length * width * 4 * proj, bytes_accessed=12 << 20, transcendentals=length * length * heads // 2
         ),
         name="attn_bwd",
-    )(tables, *rows, *weights, q_aug, k_aug, v_in, lse, cosine, sine, seg_row, seg_wide, hot_rows)
+    )(*operands, *behind)
 
 
 def attention_tables(segments, variates, times, variate_bias, order, places):
@@ -337,17 +357,28 @@
     return tables, cosine, sine, seg_row, seg_wide, feature, coef, hot_rows
 
 
-def ffn_kernel(row_parts, seq, *refs):
+def ffn_kernel(row_parts, flipped, which, *refs):
     rows, refs = refs[:row_parts], refs[row_parts:]
-    grads, refs = refs[:row_parts], refs[row_parts:]
-    weight, act_out, d_both_out, keep_out, send_out = refs
+    near, refs = refs[:row_parts], refs[row_parts:]
+    far, refs = refs[:row_parts], refs[row_parts:]
+    weight, act_out, d_both_out, keep_out, rest_out, send_own, send_rest, grads, sems = refs
     part = rows[0].shape[0]
+    share = part // 2
     cols = act_out.shape[1]
     half = row_parts // 2
+    copies = []
+    for p in range(row_parts):
+        pair = (far[p], near[p]) if flipped else (near[p], far[p])
+        for k in range(2):
+            copy = pltpu.make_async_copy(pair[k].at[which[0]], grads.at[p, pl.ds(k * share, share)], sems.at[p, k])
+            copy.start()
+            copies.append(copy)
     for p in list(range(half, row_parts)) + list(range(half)):
         at = slice(p * part, (p + 1) * part)
         both = nn_dot(rows[p][...], weight[:, : 2 * cols])
-        d_act = nn_dot(grads[p][seq * part : (seq + 1) * part, :], weight[:, 2 * cols :])
+        copies[2 * p].wait()
+        copies[2 * p + 1].wait()
+        d_act = nn_dot(grads[p], weight[:, 2 * cols :])
         gate, up = both[:, :cols], both[:, cols:]
         sig = 1.0 / (1.0 + jnp.exp(-gate))
         silu = gate * sig
@@ -355,52 +386,67 @@
         d_both_out[at, :cols] = (d_act * up * (sig + silu * (1.0 - sig))).astype(BF16)
         d_both_out[at, cols:] = (d_act * silu).astype(BF16)
         back = nt_dot(d_both_out[at, :], weight[:, : 2 * cols])
-        if p < half:
-            keep_out[at, :] = back
+        if p == 0:
+            keep_out[...] = back
+        elif p < half:
+            rest_out[(p - 1) * part : p * part, :] = back
         else:
-            send_out[(p - half) * part : (p - half + 1) * part, :] = back.astype(BF16)
-
-
-def ffn_middle(seq, rows, grads, weight):
+            if p == half:
+                send_own[...] = back.astype(BF16)
+            else:
+                send_rest[(p - half - 1) * part : (p - half) * part, :] = back.astype(BF16)
+
+
+def ffn_middle(flipped, which, rows, near, far, weight, behind=()):
     part, width = rows[0].shape
-    length = part * len(rows)
+    count = len(rows)
+    length = part * count
     cols = weight.shape[1] // 3
+    operands = (which, *rows, *near, *far, weight)
     return pl.pallas_call(
-        functools.partial(ffn_kernel, len(rows), seq),
+        without(functools.partial(ffn_kernel, count, flipped), len(operands), len(behind)),
         out_shape=(
             jax.ShapeDtypeStruct((length, cols), BF16),
             jax.ShapeDtypeStruct((length, 2 * cols), BF16),
-            jax.ShapeDtypeStruct((length // 2, width), F32),
-            jax.ShapeDtypeStruct((length // 2, width), BF16),
+            jax.ShapeDtypeStruct((part, width), F32),
+            jax.ShapeDtypeStruct((length // 2 - part, width), F32),
+            jax.ShapeDtypeStruct((part, width), BF16),
+            jax.ShapeDtypeStruct((length // 2 - part, width), BF16),
         ),
-        in_specs=[vmem()] * (2 * len(rows) + 1),
-        out_specs=[vmem()] * 4,
+        in_specs=[smem()] + [vmem()] * count + [anywhere()] * (2 * count) + [vmem()] + [anywhere()] * len(behind),
+        out_specs=[vmem()] * 6,
+        scratch_shapes=[pltpu.VMEM((count, part, width), BF16), pltpu.SemaphoreType.DMA((count, 2))],
         compiler_params=pltpu.CompilerParams(vmem_limit_bytes=VMEM_LIMIT),
         cost_estimate=pl.CostEstimate(
             flops=10 * length * width * cols, bytes_accessed=16 << 20, transcendentals=length * cols
         ),
         name="ffn_middle",
-    )(*rows, *grads, weight)
-
-
-def ffn_grad_kernel(row_parts, *refs):
+    )(*operands, *behind)
+
+
+def ffn_grad_kernel(row_parts, which, *refs):
     own, refs = refs[:row_parts], refs[row_parts:]
     other, refs = refs[:row_parts], refs[row_parts:]
-    grads, refs = refs[:row_parts], refs[row_parts:]
+    near, refs = refs[:row_parts], refs[row_parts:]
+    far, refs = refs[:row_parts], refs[row_parts:]
     act_own, act_other, d_own, d_other, out, left = refs
     part, width = own[0].shape
+    share = part // 2
     length = part * row_parts
     cols = act_own.shape[1]
+    ix = which[0]
     for what in range(2):
         for seq in range(2):
             for p in range(row_parts):
+                at = seq * length + p * part
                 for c in range(width // LANES):
                     lanes = slice(c * LANES, (c + 1) * LANES)
                     if what == 0:
-                        tile = grads[p][seq * part : (seq + 1) * part, lanes]
+                        now = ix if seq == 0 else 1 - ix
+                        pair = (near[p], far[p]) if seq == 0 else (far[p], near[p])
+                        tile = jnp.concatenate([ref[now, :, lanes] for ref in pair], axis=0)
                     else:
                         tile = (own, other)[seq][p][:, lanes]
-                    at = seq * length + p * part
                     left[lanes, at : at + part] = tile.astype(F32).T.astype(BF16)
         first, second = ((act_own, act_other), (d_own, d_other))[what]
         to = slice(2 * cols, 3 * cols) if what == 0 else slice(0, 2 * cols)
@@ -411,14 +457,15 @@
             out[at, to] = total.astype(BF16)
 
 
-def ffn_partials(own, other, grads, act_own, act_other, d_own, d_other):
+def ffn_partials(which, own, other, near, far, act_own, act_other, d_own, d_other, behind=()):
     part, width = own[0].shape
     length = part * len(own)
     cols = act_own.shape[1]
+    operands = (which, *own, *other, *near, *far, act_own, act_other, d_own, d_other)
     return pl.pallas_call(
-        functools.partial(ffn_grad_kernel, len(own)),
+        without(functools.partial(ffn_grad_kernel, len(own)), len(operands), len(behind)),
         out_shape=jax.ShapeDtypeStruct((width, 3 * cols), BF16),
-        in_specs=[vmem()] * (3 * len(own) + 4),
+        in_specs=[smem()] + [vmem()] * (4 * len(own) + 4) + [anywhere()] * len(behind),
         out_specs=vmem(),
         scratch_shapes=[pltpu.VMEM((width, 2 * length), BF16)],
         compiler_params=pltpu.CompilerParams(vmem_limit_bytes=VMEM_LIMIT),
@@ -426,33 +473,219 @@
             flops=12 * length * width * cols, bytes_accessed=17 << 20, transcendentals=0
         ),
         name="ffn_partials",
-    )(*own, *other, *grads, act_own, act_other, d_own, d_other)
-
-
-def ffn_out_kernel(act_own, act_other, weight, keep_out, send_out):
+    )(*operands, *behind)
+
+
+def ffn_out_kernel(act_own, act_other, weight, *outs):
     length, cols = act_own.shape
+    part = outs[0].shape[0]
     half = length // 2
     down = weight[:, 2 * cols :]
     for seq, act in enumerate((act_own, act_other)):
-        at = slice(seq * half, (seq + 1) * half)
-        keep_out[at, :] = nt_dot(act[:half, :], down)
-        send_out[at, :] = nt_dot(act[half:, :], down).astype(BF16)
-
-
-def ffn_result(act_own, act_other, weight):
+        both = nt_dot(act[:half, :], down)
+        outs[4 * seq][...] = both[:part]
+        outs[4 * seq + 1][...] = both[part:]
+        both = nt_dot(act[half:, :], down).astype(BF16)
+        outs[4 * seq + 2][...] = both[:part]
+        outs[4 * seq + 3][...] = both[part:]
+
+
+def ffn_result(act_own, act_other, weight, part, behind=()):
     length, cols = act_own.shape
     width = weight.shape[0]
+    shapes = (
+        jax.ShapeDtypeStruct((part, width), F32),
+        jax.ShapeDtypeStruct((length // 2 - part, width), F32),
+        jax.ShapeDtypeStruct((part, width), BF16),
+        jax.ShapeDtypeStruct((length // 2 - part, width), BF16),
+    )
+    operands = (act_own, act_other, weight)
     return pl.pallas_call(
-        ffn_out_kernel,
-        out_shape=(jax.ShapeDtypeStruct((length, width), F32), jax.ShapeDtypeStruct((length, width), BF16)),
-        in_specs=[vmem()] * 3,
-        out_specs=[vmem()] * 2,
+        without(ffn_out_kernel, len(operands), len(behind)),
+        out_shape=shapes * 2,
+        in_specs=[vmem()] * 3 + [anywhere()] * len(behind),
+        out_specs=[vmem()] * 8,
         compiler_params=pltpu.CompilerParams(vmem_limit_bytes=VMEM_LIMIT),
         cost_estimate=pl.CostEstimate(
             flops=4 * length * width * cols, bytes_accessed=12 << 20, transcendentals=0
         ),
         name="ffn_result",
-    )(act_own, act_other, weight)
+    )(*operands, *behind)
+
+
+def without(kernel, start, count):
+    return lambda *refs: kernel(*refs[:start], *refs[start + count :])
+
+
+def rows_call(kernel, name, shapes, *operands, scalars=(), behind=()):
+    single = not isinstance(shapes, (list, tuple))
+    count = len(scalars) + len(operands)
+    return pl.pallas_call(
+        without(kernel, count, len(behind)),
+        out_shape=shapes,
+        in_specs=[smem()] * len(scalars) + [vmem()] * len(operands) + [anywhere()] * len(behind),
+        out_specs=vmem() if single else [vmem()] * len(shapes),
+        compiler_params=pltpu.CompilerParams(vmem_limit_bytes=VMEM_LIMIT),
+        cost_estimate=pl.CostEstimate(
+            flops=16 * operands[0].size, bytes_accessed=sum(o.size * o.dtype.itemsize for o in operands), transcendentals=0
+        ),
+        name=name,
+    )(*scalars, *operands, *behind)
+
+
+def pack_kernel(*refs):
+    out, start = refs[-1], 0
+    for ref in refs[:-1]:
+        stop = start + ref.shape[1]
+        out[:, start:stop] = ref[...]
+        start = stop
+
+
+def split_kernel(which, gate, up, down, mine, theirs):
+    cols = gate.shape[1] // 2
+    for k, ref in enumerate((gate, up, down)):
+        for own, out in ((0, mine), (1, theirs)):
+
+            @pl.when(which[0] == 0)
+            def _(ref=ref, out=out, k=k, own=own):
+                out[:, k * cols : (k + 1) * cols] = ref[:, own * cols : (own + 1) * cols]
+
+            @pl.when(which[0] == 1)
+            def _(ref=ref, out=out, k=k, own=own):
+                out[:, k * cols : (k + 1) * cols] = ref[:, (1 - own) * cols : (2 - own) * cols]
+
+
+def stack_kernel(which, mine, theirs, out):
+    block = mine.shape[0]
+    first = pl.multiple_of(which[0] * block, block)
+    second = pl.multiple_of((1 - which[0]) * block, block)
+    out[pl.ds(first, block), :] = mine[...]
+    out[pl.ds(second, block), :] = theirs[...]
+
+
+def pair_kernel(*refs):
+    blocks = (len(refs) - 1) // 2
+    keeps, other, outs = refs[:blocks], refs[blocks], refs[blocks + 1 :]
+    rows = keeps[0].shape[0]
+    for k in range(blocks):
+        total = keeps[k][...].astype(F32) + other[k * rows : (k + 1) * rows, :].astype(F32)
+        outs[k][...] = total.astype(outs[k].dtype)
+
+
+def finish_kernel(count, own, *refs):
+    total = own[...]
+    for ref in refs[:-count]:
+        total = total + ref[...].astype(F32)
+    start = 0
+    for out in refs[-count:]:
+        stop = start + out.shape[1]
+        out[...] = total[:, start:stop]
+        start = stop
+
+
+def pair_sums(partials, other):
+    shape = partials[0].shape
+    blocks = len(partials) - 1
+    shapes = [jax.ShapeDtypeStruct(shape, F32 if k == 0 else BF16) for k in range(blocks)]
+    return rows_call(pair_kernel, "pair_sums", shapes, *partials[:-1], other)
+
+
+def weight_sums(own, arrived, pieces):
+    outs = [jax.ShapeDtypeStruct((own.shape[0], own.shape[1] // pieces), F32)] * pieces
+    return rows_call(functools.partial(finish_kernel, pieces), "weight_sums", outs, own, *arrived)
+
+
+def ffn_finish_kernel(which, grads, far, *outs):
+    cols = far.shape[1] // 3
+    rows = far.shape[0]
+    mine = grads[pl.ds(pl.multiple_of(which[0] * rows, rows), rows), :].astype(F32)
+    theirs = far[...].astype(F32)
+    for own in range(2):
+
+        @pl.when(which[0] == own)
+        def _(own=own):
+            for k, out in enumerate(outs):
+                out[:, own * cols : (own + 1) * cols] = mine[:, k * cols : (k + 1) * cols]
+                out[:, (1 - own) * cols : (2 - own) * cols] = theirs[:, k * cols : (k + 1) * cols]
+
+
+def out_kernel(hidden, keep, twin, keep_next, twin_next, *refs):
+    count = (len(refs) - 2) // 2
+    mine = rows_sum(keep, twin, refs[:count]) + hidden[...]
+    theirs = rows_sum(keep_next, twin_next, refs[count : 2 * count])
+    held, sent = refs[-2:]
+    share = held.shape[1]
+    held[0] = mine[:share]
+    held[1] = theirs[share:]
+    sent[0] = theirs[:share].astype(BF16)
+    sent[1] = mine[share:].astype(BF16)
+
+
+def out_finish_kernel(which, held, arrived, out):
+    for own in range(2):
+        out[pl.ds(which[0] if own == 0 else 1 - which[0], 1)] = (held[own] + arrived[own].astype(F32)).astype(BF16)[None]
+
+
+def inverse_rms(values):
+    return lax.rsqrt(jnp.mean(values * values, axis=-1, keepdims=True) + EPS)
+
+
+def both_halves(first, second):
+    return jnp.concatenate([first[...], second[...]], axis=0).astype(F32)
+
+
+def rows_sum(keep, twin, arrived):
+    total = keep[...] + twin[...].astype(F32)
+    for ref in arrived:
+        total = total + ref[...].astype(F32)
+    return total
+
+
+def norm_kernel(near, far, gain, out):
+    values = both_halves(near, far)
+    out[...] = (values * inverse_rms(values) * gain[...].astype(F32)).astype(BF16)
+
+
+def rest_kernel(rest, twin, out):
+    out[...] = (rest[...] + twin[...].astype(F32)).astype(BF16)
+
+
+def sum_kernel(keep, twin, *refs):
+    refs[-1][...] = rows_sum(keep, twin, refs[:-1]).astype(BF16)
+
+
+def middle_kernel(near, far, gain, keep, twin, *refs):
+    arrived, (hidden, out) = refs[:-2], refs[-2:]
+    values = both_halves(near, far) + rows_sum(keep, twin, arrived)
+    hidden[...] = values
+    out[...] = (values * inverse_rms(values) * gain[...].astype(F32)).astype(BF16)
+
+
+def pull_norm(values, gain, grad):
+    inv = inverse_rms(values)
+    scaled = grad * gain
+    normed = values * inv
+    d_values = inv * (scaled - normed * jnp.mean(scaled * normed, axis=-1, keepdims=True))
+    return d_values, jnp.sum(grad * normed, axis=0, keepdims=True)
+
+
+def back_two_kernel(hidden, near, far, gain, across, keep, twin, *refs):
+    arrived, (d_hidden, low, d_gain) = refs[:-3], refs[-3:]
+    grad = rows_sum(keep, twin, arrived) + across[...].astype(F32)
+    d_values, d_gain[...] = pull_norm(hidden[...], gain[...].astype(F32), grad)
+    total = both_halves(near, far) + d_values
+    d_hidden[...] = total
+    low[...] = total.astype(BF16)
+
+
+def back_one_kernel(near, far, gain, d_hidden, keep, twin, *refs):
+    arrived, (first, second, d_gain) = refs[:-3], refs[-3:]
+    grad = rows_sum(keep, twin, arrived)
+    d_values, d_gain[...] = pull_norm(both_halves(near, far), gain[...].astype(F32), grad)
+    total = (d_hidden[...] + d_values).astype(BF16)
+    share = first.shape[0]
+    first[...] = total[:share]
+    second[...] = total[share:]
 
 
 def grad_kernel(row_parts, blocks, tables, *refs):
@@ -510,26 +743,6 @@
     return values
 
 
-def gather_weight(block):
-    nz = lax.axis_size("fsdp")
-    mine = [block] + [hop(block, "fsdp", k) for k in range(1, nz)]
-    return mine + [hop(piece, "ctx", 1) for piece in mine]
-
-
-def scatter_weight(partials):
-    keeps, send = partials[:-1], partials[-1]
-    rows = keeps[0].shape[0]
-    other = hop(send, "ctx", 1)
-    out = None
-    for k, keep in enumerate(keeps):
-        total = keep.astype(F32) + other[k * rows : (k + 1) * rows].astype(F32)
-        if k == 0:
-            out = total
-        else:
-            out = out + hop(total.astype(BF16), "fsdp", k).astype(F32)
-    return out
-
-
 def gather_chips(block):
     nt = lax.axis_size("tp")
     return [block] + [hop(block, "tp", 2 * k) for k in range(1, nt // 2)]
@@ -543,15 +756,22 @@
     return with_twins(gather_chips(block))
 
 
-def scatter_rows(keep, send):
-    nt = lax.axis_size("tp")
-    rows = 2 * keep.shape[0] // nt
-    other = hop(send, "tp", 1)
-    total = keep + other.astype(F32)
-    out = total[:rows]
-    for k in range(1, nt // 2):
-        out = out + hop(total[k * rows : (k + 1) * rows].astype(BF16), "tp", 2 * k).astype(F32)
-    return out
+def region(ready, run):
+    shapes = jax.eval_shape(run)
+    return lax.cond(ready, run, lambda: jax.tree.map(lambda a: jnp.zeros(a.shape, a.dtype), shapes))
+
+
+def chips_low(rest, twin, *behind):
+    return rows_call(
+        rest_kernel, "rest_rows", jax.ShapeDtypeStruct(rest.shape, BF16), rest, twin, behind=behind
+    )
+
+
+def chips_hop(low, nt):
+    if nt == 4:
+        return [hop(low, "tp", 2)]
+    rows = low.shape[0] // (nt // 2 - 1)
+    return [hop(low[(k - 1) * rows : k * rows], "tp", 2 * k) for k in range(1, nt // 2)]
 
 
 def total_over(values):
@@ -561,18 +781,6 @@
     values = values + across
     values = sum([hop(values, "tp", 2 * k) for k in range(1, nt // 2)], values)
     return sum([hop(values, "fsdp", k) for k in range(1, nz)], values)
-
-
-def inverse_rms(values):
-    return lax.rsqrt(jnp.mean(values * values, axis=-1, keepdims=True) + EPS)
-
-
-def norm_back(values, inv, gain, grad):
-    scaled = grad * gain
-    normed = values * inv
-    d_gain = jnp.sum(grad * normed, axis=0, keepdims=True)
-    d_values = inv * (scaled - normed * jnp.mean(scaled * normed, axis=-1, keepdims=True))
-    return d_values, d_gain
 
 
 def shards(
@@ -606,92 +814,209 @@
     def swap(mine, theirs):
         return jnp.where(ix == 0, mine, theirs), jnp.where(ix == 0, theirs, mine)
 
-    order = jnp.arange(nx * nt).reshape(nx, nt // 2, 2)
-    order = swap_blocks(swap_blocks(swap_blocks(order, 0, ix, nx), 1, it // 2, nt // 2), 2, it % 2, 2)
-    order = order.transpose(2, 1, 0).reshape(nx * nt)
-    places = jnp.arange(nz * nx).reshape(nz, nx)
-    places = swap_blocks(swap_blocks(places, 0, iz, nz), 1, ix, nx).transpose(1, 0).reshape(nz * nx)
-    tables, cosine, sine, seg_row, seg_wide, feature, coef, hot_rows = attention_tables(
-        pick(segment_ids, ix), pick(variate_ids, ix), pick(time_ids, ix), variate_bias, order, places
-    )
-    gain_one = attn_gain.astype(F32)[None]
-    gain_two = ffn_gain.astype(F32)[None]
-
-    inputs = jnp.concatenate([pick(layer_in, ix), hop(pick(layer_in, 1 - ix), "ctx", 1)], axis=0).astype(F32)
-    inv_one = inverse_rms(inputs)
-    rows_one = gather_rows((inputs * inv_one * gain_one).astype(BF16))
-    attn_w = gather_weight(jnp.concatenate([query_weight, key_weight, value_weight, out_weight], axis=1))
-
+    gain_one, gain_two = attn_gain[None], ffn_gain[None]
+    part = nx * share
+    low_rows = jax.ShapeDtypeStruct((part, width), BF16)
+    wide_rows = jax.ShapeDtypeStruct((part, width), F32)
+    gain_row = jax.ShapeDtypeStruct((1, width), F32)
+    half_rows = jax.ShapeDtypeStruct((share, width), BF16)
+    which = ix.astype(jnp.int32).reshape(1)
+    ready = ix >= 0
     cols = gate_weight.shape[1] // 2
-    pieces = [w.reshape(w.shape[0], 2, cols) for w in (gate_weight, up_weight, down_weight)]
-    mine = jnp.concatenate([lax.dynamic_index_in_dim(w, ix, 1, keepdims=False) for w in pieces], axis=1)
-    theirs = jnp.concatenate([lax.dynamic_index_in_dim(w, 1 - ix, 1, keepdims=False) for w in pieces], axis=1)
-    ffn_w = jnp.concatenate(swap(mine, hop(theirs, "ctx", 1)), axis=0)
+    near, grad_own = pick(layer_in, ix), out_grad
+    attn_shape = jax.ShapeDtypeStruct((query_weight.shape[0], 4 * proj), BF16)
+    ffn_shape = jax.ShapeDtypeStruct((gate_weight.shape[0], 3 * cols), BF16)
+    attn_own = rows_call(
+        pack_kernel, "pack_weights", attn_shape, query_weight, key_weight, value_weight, out_weight
+    )
+    mine, theirs = rows_call(
+        split_kernel, "split_weights", (ffn_shape, ffn_shape), gate_weight, up_weight, down_weight, scalars=(which,)
+    )
+
+    def twin(block):
+        return hop(block, "tp", 1)
+
+    def across(block):
+        return hop(block, "ctx", 1)
+
+    def first_transfers():
+        far = across(pick(layer_in, 1 - ix))
+        attn_z = [hop(attn_own, "fsdp", k) for k in range(1, nz)]
+        attn_x = across(attn_own)
+        ffn_x = across(theirs)
+        grad_y = gather_chips(grad_own)[1:]
+        order = jnp.arange(nx * nt).reshape(nx, nt // 2, 2)
+        order = swap_blocks(swap_blocks(swap_blocks(order, 0, ix, nx), 1, it // 2, nt // 2), 2, it % 2, 2)
+        order = order.transpose(2, 1, 0).reshape(nx * nt)
+        places = jnp.arange(nz * nx).reshape(nz, nx)
+        places = swap_blocks(swap_blocks(places, 0, iz, nz), 1, ix, nx).transpose(1, 0).reshape(nz * nx)
+        tables = attention_tables(
+            pick(segment_ids, ix), pick(variate_ids, ix), pick(time_ids, ix), variate_bias, order, places
+        )
+        return far, attn_z, attn_x, ffn_x, grad_y, tables
+
+    far, attn_z, attn_x, ffn_x, grad_y, made = region(ready, first_transfers)
+    tables, cosine, sine, seg_row, seg_wide, feature, coef, hot_rows = made
+    ffn_w = rows_call(
+        stack_kernel, "stack_weights", jax.ShapeDtypeStruct((2 * ffn_shape.shape[0], 3 * cols), BF16), mine, ffn_x,
+        scalars=(which,),
+    )
     ffn_w = lax.all_gather(ffn_w, "fsdp", axis=0, tiled=True)
 
-    other_grad = hop(out_grad, "ctx", 1)
-    grads = jnp.concatenate([pick(out_grad, ix), pick(other_grad, ix)], axis=0)
-    grads_next = jnp.concatenate([pick(other_grad, 1 - ix), pick(out_grad, 1 - ix)], axis=0)
-    grad_rows = gather_rows(jnp.concatenate([grads, grads_next], axis=0))
-
-    q_aug, k_aug, v_rows, mixed, lse, keep, send = attention_forward(
-        tables, rows_one, attn_w, cosine, sine, seg_row, seg_wide, feature, coef, heads
-    )
-    hidden = inputs + scatter_rows(keep, send)
-    inv_two = inverse_rms(hidden)
-    chips_two = gather_chips((hidden * inv_two * gain_two).astype(BF16))
-    rows_two = with_twins(chips_two)
-    rows_next = with_twins([hop(block, "ctx", 1) for block in chips_two])
-    act, d_both, keep, send = ffn_middle(0, rows_two, grad_rows, ffn_w)
-    d_normed_two = scatter_rows(keep, send)
-    act_next, d_both_next, keep, send = ffn_middle(1, rows_next, grad_rows, ffn_w)
-    d_normed_two = d_normed_two + hop(scatter_rows(keep, send).astype(BF16), "ctx", 1).astype(F32)
-
-    ffn_grad = ffn_partials(rows_two, rows_next, grad_rows, act, act_next, d_both, d_both_next)
+    def gather_one():
+        rows = rows_call(norm_kernel, "norm_rows", low_rows, near, far, gain_one)
+        return gather_rows(rows), [across(piece) for piece in attn_z]
+
+    rows_one, rest_x = region(ready, gather_one)
+    attn_w = [attn_own] + attn_z + [attn_x] + rest_x
+
+    def attend():
+        return across(grad_own), attention_forward(
+            tables, rows_one, attn_w, cosine, sine, seg_row, seg_wide, feature, coef, heads
+        )
+
+    grad_far, (q_aug, k_aug, v_rows, mixed, lse, keep, rest, send, send_rest) = region(ready, attend)
+
+    def scatter_attn():
+        low = chips_low(rest, twin(send_rest))
+        return chips_hop(low, nt), twin(send), [across(piece) for piece in grad_y]
+
+    chips, twins, grad_far_y = region(ready, scatter_attn)
+    grad_near, grad_far = [grad_own] + grad_y, [grad_far] + grad_far_y
+    hidden, rows_two = rows_call(
+        middle_kernel, "middle_rows", (wide_rows, low_rows), near, far, gain_two, keep, twins, *chips
+    )
+
+    def gather_two():
+        return gather_chips(rows_two), across(rows_two), with_twins(grad_near), with_twins(grad_far), twin(rows_two)
+
+    chips_two, next_own, grad_near, grad_far, rows_twin = region(ready, gather_two)
+
+    def ffn_own():
+        rows = chips_two + [rows_twin] + [twin(block) for block in chips_two[1:]]
+        return [across(block) for block in chips_two[1:]], rows, ffn_middle(
+            False, which, rows, grad_near, grad_far, ffn_w
+        )
+
+    next_y, rows_two, (act, d_both, keep, rest, send, send_rest) = region(ready, ffn_own)
+
+    def ffn_next():
+        low = chips_low(rest, twin(send_rest))
+        rows = with_twins([next_own] + next_y)
+        return chips_hop(low, nt), twin(send), rows, ffn_middle(True, 1 - which, rows, grad_near, grad_far, ffn_w)
+
+    chips, twins, rows_next, made = region(ready, ffn_next)
+    act_next, d_both_next, keep_next, rest_next, send_next, send_rest = made
+    low_next = chips_low(rest_next, twin(send_rest))
+
+    def scatter_next():
+        parts = ffn_result(act, act_next, ffn_w, part)
+        return chips_hop(low_next, nt), twin(send_next), parts, [twin(parts[k]) for k in (2, 3, 6, 7)]
+
+    chips_next, twins_next, ffn_parts, out_twins = region(ready, scatter_next)
+    low_across = rows_call(sum_kernel, "sum_rows", low_rows, keep_next, twins_next, *chips_next)
+    low_out = chips_low(ffn_parts[1], out_twins[1])
+
+    def cross_next():
+        return across(low_across), chips_hop(low_out, nt), ffn_partials(
+            which, rows_two, rows_next, grad_near, grad_far, act, act_next, d_both, d_both_next
+        )
+
+    arrived, out_chips, ffn_grad = region(ready, cross_next)
     ffn_grad = lax.psum_scatter(ffn_grad, "fsdp", scatter_dimension=0, tiled=True)
-    ffn_grad = ffn_grad.reshape(nx, ffn_grad.shape[0] // nx, ffn_grad.shape[1])
-    low, high = swap(pick(ffn_grad, ix), hop(pick(ffn_grad, 1 - ix), "ctx", 1))
-    gate_grad, up_grad, down_grad = [
-        jnp.concatenate([low[:, k * cols : (k + 1) * cols], high[:, k * cols : (k + 1) * cols]], axis=1).astype(F32)
-        for k in range(3)
-    ]
-
-    keep, send = ffn_result(act, act_next, ffn_w)
-    other = hop(send, "tp", 1)
-    total = (keep + other.astype(F32)).reshape(2, nt // 2, nx * share, width)
-    ffn = total[:, 0]
-    for k in range(1, nt // 2):
-        ffn = ffn + hop(total[:, k].astype(BF16), "tp", 2 * k).astype(F32)
-    mine, theirs = (ffn[0] + hidden).reshape(2, share, width), ffn[1].reshape(2, share, width)
-    sent = hop(jnp.stack([mine[1], theirs[0]]).astype(BF16), "ctx", 1).astype(F32)
-    layer_out = jnp.stack(swap(mine[0] + sent[1], theirs[1] + sent[0])).astype(BF16)
-
-    d_hidden_norm, d_gain_two = norm_back(hidden, inv_two, gain_two, d_normed_two)
-    d_hidden = grads.astype(F32) + d_hidden_norm
-    branch_rows = gather_rows(d_hidden.astype(BF16))
-    keep, send, d_qkv, bias_parts = attention_backward(
-        tables, branch_rows, attn_w, q_aug, k_aug, v_rows, lse, cosine, sine, seg_row, seg_wide, hot_rows, heads
-    )
-    d_normed_one = scatter_rows(keep, send)
-    out_weight_grad = scatter_weight(weight_partials(tables, branch_rows, mixed, nz))
-    qkv_grad = scatter_weight(weight_partials(tables, rows_one, d_qkv, nz))
-
-    d_input_norm, d_gain_one = norm_back(inputs, inv_one, gain_one, d_normed_one)
-    d_inputs = (d_hidden + d_input_norm).astype(BF16)
-    in_grad = jnp.stack(swap(d_inputs[:share], hop(d_inputs[share:], "ctx", 1)))
-    sums = jnp.sum(bias_parts, axis=2)
-    bias_sums = jnp.stack([jnp.sum(sums[:, :8], axis=1), jnp.sum(sums[:, 8:], axis=1)])
+    d_hidden, low, d_gain_two = rows_call(
+        back_two_kernel,
+        "back_two",
+        (wide_rows, low_rows, gain_row),
+        hidden,
+        pick(grad_near[0], ix),
+        pick(grad_far[0], ix),
+        gain_two,
+        arrived,
+        keep,
+        twins,
+        *chips,
+    )
+
+    def gather_back():
+        rows = gather_rows(low)
+        return rows, chips_low(ffn_parts[5], out_twins[3])
+
+    branch_rows, low_out = region(ready, gather_back)
+    out_grads = weight_partials(tables, branch_rows, mixed, nz)
+
+    def attend_back():
+        return chips_hop(low_out, nt), across(out_grads[-1]), attention_backward(
+            tables, branch_rows, attn_w, q_aug, k_aug, v_rows, lse, cosine, sine, seg_row, seg_wide, hot_rows, heads
+        )
+
+    out_chips_next, out_other, made = region(ready, attend_back)
+    keep, rest, send, send_rest, d_qkv, bias_parts = made
+
+    def scatter_one():
+        low = chips_low(rest, twin(send_rest))
+        grads = weight_partials(tables, rows_one, d_qkv, nz)
+        sums = pair_sums(out_grads, out_other)
+        arrived = [hop(piece, "fsdp", k) for k, piece in enumerate(sums) if k > 0]
+        return chips_hop(low, nt), twin(send), grads, across(grads[-1]), sums[0], arrived
+
+    chips, twins, qkv_grads, qkv_other, out_sum, out_arrived = region(ready, scatter_one)
+    d_near, d_far, d_gain_one = rows_call(
+        back_one_kernel,
+        "back_one",
+        (half_rows, half_rows, gain_row),
+        near,
+        far,
+        gain_one,
+        d_hidden,
+        keep,
+        twins,
+        *chips,
+    )
+    qkv_sums = pair_sums(qkv_grads, qkv_other)
+    bias_sums = jnp.sum(bias_parts, axis=2)
+    bias_sums = jnp.stack([jnp.sum(bias_sums[:, :8], axis=1), jnp.sum(bias_sums[:, 8:], axis=1)])
     spread = lax.dynamic_update_slice(jnp.zeros((2, width), F32), bias_sums, (0, it * heads))
-    totals = total_over(jnp.concatenate([d_gain_one, d_gain_two, spread], axis=0))
+    gains = jnp.concatenate([d_gain_one, d_gain_two, spread], axis=0)
+
+    def last_transfers():
+        arrived = [hop(piece, "fsdp", k) for k, piece in enumerate(qkv_sums) if k > 0]
+        ffn_half = ffn_grad.shape[0] // 2
+        ffn_far = across(lax.dynamic_slice_in_dim(ffn_grad, (1 - ix) * ffn_half, ffn_half, 0))
+        held, sent = rows_call(
+            out_kernel,
+            "out_rows",
+            (jax.ShapeDtypeStruct(layer_in.shape, F32), jax.ShapeDtypeStruct(layer_in.shape, BF16)),
+            hidden,
+            ffn_parts[0],
+            out_twins[0],
+            ffn_parts[4],
+            out_twins[2],
+            *out_chips,
+            *out_chips_next,
+        )
+        (out_weight_grad,) = weight_sums(out_sum, out_arrived, 1)
+        return arrived, ffn_far, across(d_far), held, across(sent), total_over(gains), out_weight_grad
+
+    arrived, ffn_far, d_cross, held, out_cross, totals, out_weight_grad = region(ready, last_transfers)
+    query_grad, key_grad, value_grad = weight_sums(qkv_sums[0], arrived, 3)
+    in_grad = jnp.stack(swap(d_near, d_cross))
+    layer_out = rows_call(
+        out_finish_kernel, "layer_out", jax.ShapeDtypeStruct(layer_in.shape, BF16), held, out_cross, scalars=(which,)
+    )
+    gate_grad, up_grad, down_grad = rows_call(
+        ffn_finish_kernel, "ffn_sums", [jax.ShapeDtypeStruct(gate_weight.shape, F32)] * 3, ffn_grad, ffn_far,
+        scalars=(which,),
+    )
     bias_grad = lax.dynamic_slice(totals, (2, it * heads), (2, heads))
     return (
         layer_out,
         in_grad,
         totals[0],
         totals[1],
-        qkv_grad[:, :proj],
-        qkv_grad[:, proj : 2 * proj],
-        qkv_grad[:, 2 * proj :],
+        query_grad,
+        key_grad,
+        value_grad,
         out_weight_grad,
         bias_grad,
         gate_grad,

time: 380 us -> 352 us (0.926)
  waiting for transfers between devices: 154 us -> 111 us
  Pallas kernels: 82.5 us -> 125 us
  other arithmetic: 37.5 us -> 6.89 us
  local copies, waits for them, and re-layouts: 27.6 us -> 32.3 us
    ppermute x54 -> x65, waiting for transfers between devices: 154 us -> 111 us  [hop(): return lax.ppermute(values, axis, [(i, i ^ flip) for i in range(size)])]
    pallas_call x6 -> x27, Pallas kernels: 73.3 us -> 116 us  [the longest x21 46.1 us: rows_call(): pl.pallas_call(without(kernel, count, len(behind)), out_shape=shapes, in_...]
    cond x0 -> x36, local copies, waits for them, and re-layouts: none -> 11.3 us
    convert_element_type x13 -> x1, other arithmetic: 10.8 us -> 0.73 us  [attention_tables(): angles = times.astype(F32)[:, None] * frequency]
    add x8 -> x0, other arithmetic: 8.86 us -> none  [the longest x4 2.84 us: scatter_rows(): total = keep + other.astype(F32)]
    unnamed x117 -> x78, local copies, waits for them, and re-layouts: 9.33 us -> 5.1 us
    another operation x1 -> x5, local copies, waits for them, and re-layouts: 0.09 us -> 4.11 us  [swap_blocks(): cut = values.reshape(split)]
    ppermute x54 -> x65, starting transfers between devices: 57 us -> 55.7 us  [hop(): return lax.ppermute(values, axis, [(i, i ^ flip) for i in range(size)])]
  transfers between devices with their start and end apart: 56 -> 67, of which waited for: 28 -> 31; matrix products, arithmetic and copies ran while one was open for 14% -> 8% of each run, Pallas kernels for 22% -> 29%
where the time goes in v4:
time: 352 us; the launch traced here: 346 us
  Pallas kernels  125 us (36%)
  waiting for transfers between devices  111 us (32%)
  starting transfers between devices  55.8 us (16%)
  local copies, waits for them, and re-layouts  32.3 us (9%)
  between operations  14.8 us (4%)
  other arithmetic  6.89 us (2%)
    ppermute x65, waiting for transfers between devices, hop(): return lax.ppermute(values, axis, [(i, i ^ flip) for i in range(size)])  111 us
    ppermute x65, starting transfers between devices, hop(): return lax.ppermute(values, axis, [(i, i ^ flip) for i in range(size)])  55.7 us
    pallas_call x21, Pallas kernels, rows_call(): pl.pallas_call(without(kernel, count, len(behind)), out_shape=shapes, in_...  46.1 us
    pallas_call x2, Pallas kernels, ffn_middle(): pl.pallas_call(without(functools.partial(ffn_kernel, count, flipped), len...  23.2 us
    pallas_call x1, Pallas kernels, attention_backward(): pl.pallas_call(without(functools.partial(bwd_kernel, len(rows), len(weigh...  16.9 us
    pallas_call x1, Pallas kernels, attention_forward(): pl.pallas_call(without(functools.partial(fwd_kernel, len(rows), len(weigh...  12.8 us
    cond x36, local copies, waits for them, and re-layouts  11.3 us
    pallas_call x1, Pallas kernels, ffn_partials(): pl.pallas_call(without(functools.partial(ffn_grad_kernel, len(own)), len(...  11.1 us
  transfers between devices with their start and end apart: 67, of which 31 were waited for; matrix products, arithmetic and copies ran while one was open for 8% of the time, Pallas kernels for 29%

profile of v4, /device:TPU:0, one launch (start us, length us, event | category | flops | bytes accessed | tf_op | source)
XLA Modules:
  0.0 345.7 jit_solution(2729017129307525539)
XLA Ops:
  10.2 28.6 %conditional.13 = (bf16[128,1024]{1,0:T(8,128)(2,1)}, bf16[128,1024]{1,0:T(8,128)(2,1)}, bf16[128,1024]{1,0:T(8,128)(2,1)}, bf16[128,1024]{1,0:T(8,128)(2,1)}, b...) conditional(s32[]{:T(128)} %convert_element_type.39, () %tuple.118, ...), branch_computations={%region_0.1_spmd, %region_1.4_spmd} | conditional | flops 1342132 | bytes 12817355 | solution.py:761
  10.2 3.1 collective-permute-start.46
  13.3 2.6 collective-permute-start.47
  29.4 6.4 %collective-permute-done.48 = bf16[128,1024]{1,0:T(8,128)(2,1)} collective-permute-done((bf16[128,1024]{1,0:T(8,128)(2,1)S(1)}, bf16[128,1024]{1,0:T(8,128)(2,1)}, u32[]{:S(2)}, u32[]{:S(2)}) %collective-permute-start.48) | collective-permute-done | bytes 262176 | tf_op jit(solution)/shard_map/cond/branch_1_fun/ppermute | solution.py:731
  35.8 2.8 collective-permute-done.49
  38.8 2.8 stack_weights.1
  42.3 34.8 %conditional.14 = (bf16[256,1024]{1,0:T(8,128)(2,1)}, bf16[256,1024]{1,0:T(8,128)(2,1)}, bf16[256,1024]{1,0:T(8,128)(2,1)}, bf16[256,1024]{1,0:T(8,128)(2,1)}, b...) conditional(s32[]{:T(128)} %convert_element_type.39, () %tuple.121, ...), branch_computations={%region_4.5_spmd, %region_5.6_spmd} | conditional | flops 2097152 | bytes 9963816 | solution.py:761
  45.8 11.0 %collective-permute-done = bf16[256,1024]{1,0:T(8,128)(2,1)} collective-permute-done((bf16[256,1024]{1,0:T(8,128)(2,1)}, bf16[256,1024]{1,0:T(8,128)(2,1)}, u32[]{:S(2)}, u32[]{:S(2)}) %collective-permute-start) | collective-permute-done | bytes 524320 | tf_op jit(solution)/shard_map/cond/branch_1_fun/ppermute | solution.py:731
  60.3 5.9 %collective-permute-done.3 = bf16[128,1024]{1,0:T(8,128)(2,1)} collective-permute-done((bf16[128,1024]{1,0:T(8,128)(2,1)}, bf16[128,1024]{1,0:T(8,128)(2,1)}, u32[]{:S(2)}, u32[]{:S(2)}) %collective-permute-start.3) | collective-permute-done | bytes 262176 | tf_op jit(solution)/shard_map/cond/branch_1_fun/ppermute | solution.py:731
  66.2 5.6 %collective-permute-done.4 = bf16[128,1024]{1,0:T(8,128)(2,1)} collective-permute-done((bf16[128,1024]{1,0:T(8,128)(2,1)}, bf16[128,1024]{1,0:T(8,128)(2,1)}, u32[]{:S(2)}, u32[]{:S(2)}) %collective-permute-start.4) | collective-permute-done | bytes 262176 | tf_op jit(solution)/shard_map/cond/branch_1_fun/ppermute | solution.py:731
  71.9 5.2 %collective-permute-done.5 = bf16[128,1024]{1,0:T(8,128)(2,1)} collective-permute-done((bf16[128,1024]{1,0:T(8,128)(2,1)}, bf16[128,1024]{1,0:T(8,128)(2,1)}, u32[]{:S(2)}, u32[]{:S(2)}) %collective-permute-start.5) | collective-permute-done | bytes 262176 | tf_op jit(solution)/shard_map/cond/branch_1_fun/ppermute | solution.py:731
  77.1 16.5 %conditional.15 = (bf16[2,128,1024]{2,1,0:T(8,128)(2,1)}, bf16[4,1024,128]{2,1,0:T(8,128)(2,1)}, bf16[4,1024,128]{2,1,0:T(8,128)(2,1)}, bf16[2,1024,128]{2,1,0:T...) conditional(s32[]{:T(128)} %convert_element_type.39, () %tuple.120, ...), branch_computations={%region_6.7_spmd, %region_7.8_spmd} | conditional | flops 1610612736 | bytes 14680240 | solution.py:761
  80.8 12.8 %attn_fwd.1 = (bf16[4,1024,128]{2,1,0:T(8,128)(2,1)}, bf16[4,1024,128]{2,1,0:T(8,128)(2,1)}, bf16[2,1024,128]{2,1,0:T(8,128)(2,1)}, bf16[1024,256]{1,0:T(8,128)(...) custom-call(s32[4,8]{1,0:T(4,128)S(1)} %get-tuple-element.344.refs_0, ...), custom_call_target="tpu_custom_call" | custom-call | flops 1610612736 | bytes 8388608 | tf_op jit(solution)/shard_map/cond/branch_1_fun/attn_fwd/pallas_call | solution.py:167
  93.6 19.6 %conditional.16 = (bf16[256,1024]{1,0:T(8,128)(2,1)}, bf16[256,1024]{1,0:T(8,128)(2,1)}, bf16[2,128,1024]{2,1,0:T(8,128)(2,1)}) conditional(s32[]{:T(128)} %convert_element_type.39, () %tuple.124, (bf16[256,1024]{1,0:T(8,128)(2,1)}, f32[256,1024]{1,0:T(8,128)}, bf16[256,1024]{1,0:T(8,128)(2,1)}, bf16[2,128,1024]{2,1,0:T(8,128)(2,1)}) %tuple.125), branch_computations={%region_8.9_spmd, %region_9.10_spmd} | conditional | flops 4194304 | bytes 12058836 | solution.py:761
  96.6 2.2 rest_rows.6
  100.4 7.9 %collective-permute-done.10 = bf16[2,128,1024]{2,1,0:T(8,128)(2,1)} collective-permute-done((bf16[2,128,1024]{2,1,0:T(8,128)(2,1)}, bf16[2,128,1024]{2,1,0:T(8,128)(2,1)}, u32[]{:S(2)}, u32[]{:S(2)}) %collective-permute-start.10) | collective-permute-done | bytes 524320 | tf_op jit(solution)/shard_map/cond/branch_1_fun/ppermute | solution.py:731
  108.3 4.8 %collective-permute-done.8 = bf16[256,1024]{1,0:T(8,128)(2,1)} collective-permute-done((bf16[256,1024]{1,0:T(8,128)(2,1)}, bf16[256,1024]{1,0:T(8,128)(2,1)}, u32[]{:S(2)}, u32[]{:S(2)}) %collective-permute-start.8) | collective-permute-done | bytes 524320 | tf_op jit(solution)/shard_map/cond/branch_1_fun/ppermute | solution.py:731
  113.2 2.6 middle_rows.1
  115.8 17.7 %conditional.17 = (bf16[256,1024]{1,0:T(8,128)(2,1)S(1)}, bf16[256,1024]{1,0:T(8,128)(2,1)}, bf16[256,1024]{1,0:T(8,128)(2,1)}, bf16[2,128,1024]{2,1,0:T(8,128)(...) conditional(s32[]{:T(128)} %convert_element_type.39, () %tuple.126, ...), branch_computations={%region_10.11_spmd, %region_11.12_spmd} | conditional | bytes 19923320 | solution.py:761
  118.4 10.6 %collective-permute-done.11 = bf16[256,1024]{1,0:T(8,128)(2,1)} collective-permute-done((bf16[256,1024]{1,0:T(8,128)(2,1)S(1)}, bf16[256,1024]{1,0:T(8,128)(2,1)}, u32[]{:S(2)}, u32[]{:S(2)}) %collective-permute-start.11) | collective-permute-done | bytes 524320 | tf_op jit(solution)/shard_map/cond/branch_1_fun/ppermute | solution.py:731
  134.3 15.2 %conditional.18 = (bf16[256,1024]{1,0:T(8,128)(2,1)}, bf16[256,1024]{1,0:T(8,128)(2,1)S(1)}, bf16[256,1024]{1,0:T(8,128)(2,1)S(1)}, bf16[256,1024]{1,0:T(8,128)(...) conditional(s32[]{:T(128)} %convert_element_type.39, () %tuple.130, ...), branch_computations={%region_12.13_spmd, %region_13.14_spmd} | conditional | flops 5368709120 | bytes 25166020 | solution.py:761
  137.6 12.0 %ffn_middle.2 = (bf16[1024,512]{1,0:T(8,128)(2,1)}, bf16[1024,1024]{1,0:T(8,128)(2,1)}, f32[256,1024]{1,0:T(8,128)}, f32[256,1024]{1,0:T(8,128)S(1)}, bf16[256,1...) custom-call(s32[1]{0:T(128)} %get-tuple-element.384.refs_0_, bf16[256,1024]{1,0:T(8,128)(2,1)S(1)} %get-tuple-element.1060.refs_1_, ...), custom_call_target="tpu_custom_call" | custom-call | flops 5368709120 | bytes 16777216 | tf_op jit(solution)/shard_map/cond/branch_1_fun/ffn_middle/pallas_call | solution.py:406
  150.7 19.0 %conditional.19 = (bf16[256,1024]{1,0:T(8,128)(2,1)}, bf16[256,1024]{1,0:T(8,128)(2,1)}, bf16[256,1024]{1,0:T(8,128)(2,1)S(1)}, bf16[256,1024]{1,0:T(8,128)(2,1)...) conditional(s32[]{:T(128)} %convert_element_type.39, () %tuple.129, ...), branch_computations={%region_14.15_spmd, %region_15.16_spmd} | conditional | flops 5372903424 | bytes 41419200 | solution.py:761
  158.0 11.2 %ffn_middle.3 = (bf16[1024,512]{1,0:T(8,128)(2,1)S(1)}, bf16[1024,1024]{1,0:T(8,128)(2,1)}, f32[256,1024]{1,0:T(8,128)S(1)}, f32[256,1024]{1,0:T(8,128)S(1)}, bf...) custom-call(s32[1]{0:T(128)S(6)} %sub.79.refs_0_, bf16[256,1024]{1,0:T(8,128)(2,1)} %get-tuple-element.1084.refs_1_, ...), custom_call_target="tpu_custom_call" | custom-call | flops 5368709120 | bytes 16777216 | tf_op jit(solution)/shard_map/cond/branch_1_fun/ffn_middle/pallas_call | solution.py:406
  173.6 20.8 %conditional.20 = (bf16[256,1024]{1,0:T(8,128)(2,1)}, bf16[256,1024]{1,0:T(8,128)(2,1)}, f32[256,1024]{1,0:T(8,128)}, f32[256,1024]{1,0:T(8,128)S(1)}, f32[256,1...) conditional(s32[]{:T(128)} %convert_element_type.39, () %tuple.133, ...), branch_computations={%region_16.17_spmd, %region_17.18_spmd} | conditional | flops 2147483648 | bytes 25166144 | solution.py:761
  173.7 5.7 %ffn_result.1 = (f32[256,1024]{1,0:T(8,128)}, f32[256,1024]{1,0:T(8,128)S(1)}, bf16[256,1024]{1,0:T(8,128)(2,1)}, bf16[256,1024]{1,0:T(8,128)(2,1)}, f32[256,102...) custom-call(bf16[1024,512]{1,0:T(8,128)(2,1)S(1)} %get-tuple-element.423.refs_0_, ...), custom_call_target="tpu_custom_call" | custom-call | flops 2147483648 | bytes 12582912 | tf_op jit(solution)/shard_map/cond/branch_1_fun/ffn_result/pallas_call | solution.py:503
  183.9 10.6 %collective-permute-done.25 = bf16[256,1024]{1,0:T(8,128)(2,1)} collective-permute-done((bf16[256,1024]{1,0:T(8,128)(2,1)S(1)}, bf16[256,1024]{1,0:T(8,128)(2,1)}, u32[]{:S(2)}, u32[]{:S(2)}) %collective-permute-start.25) | collective-permute-done | bytes 524320 | tf_op jit(solution)/shard_map/cond/branch_1_fun/ppermute | solution.py:731
  198.7 14.7 %conditional.21 = (bf16[256,1024]{1,0:T(8,128)(2,1)}, bf16[256,1024]{1,0:T(8,128)(2,1)}, bf16[1024,1536]{1,0:T(8,128)(2,1)S(1)}) conditional(s32[]{:T(128)} %convert_element_type.39, () %tuple.128, (bf16[256,1024]{1,0:T(8,128)(2,1)}, bf16[256,1024]{1,0:T(8,128)(2,1)}, s32[1]{0:T(128)}, bf16[256,1024]{1,0:T(8,128)(2,1)}, ...), branch_computations={%region_18.19_spmd, %region_19.20_spmd} | conditional | flops 6442450944 | bytes 26214532 | solution.py:761
  201.4 11.1 %ffn_partials.1 = bf16[1024,1536]{1,0:T(8,128)(2,1)S(1)} custom-call(s32[1]{0:T(128)} %get-tuple-element.436.refs_0_, bf16[256,1024]{1,0:T(8,128)(2,1)} %get-tuple-element.437.refs_1_, bf16[256,1024]{1,0:T(8,128)(2,1)} %get-tuple-element.438.refs_2_, bf16[256,1024]{1,0:T(8,128)(2,1)} %get-tuple-element.439.refs_3_, ...), custom_call_target="tpu_custom_call" | custom-call | flops 6442450944 | bytes 17825792 | tf_op jit(solution)/shard_map/cond/branch_1_fun/ffn_partials/pallas_call | solution.py:465
  217.0 3.9 %back_two.1 = (f32[256,1024]{1,0:T(8,128)}, bf16[256,1024]{1,0:T(8,128)(2,1)S(1)}, f32[1,1024]{1,0:T(1,128)}) custom-call(f32[256,1024]{1,0:T(8,128)} %get-tuple-element.715.refs_0_, bf16[128,1024]{1,0:T(8,128)(2,1)} %get-tuple-element.953.refs_1_, bf16[128,1024]{1,0:T(8,128)(2,1)} %get-tuple-element.952.refs_2_, ...), custom_call_target="tpu_custom_call" | custom-call | flops 4194304 | bytes 4196352 | tf_op jit(solution)/shard_map/back_two/pallas_call | solution.py:523
  221.0 14.3 %conditional.22 = (bf16[256,1024]{1,0:T(8,128)(2,1)S(1)}, bf16[256,1024]{1,0:T(8,128)(2,1)}, bf16[256,1024]{1,0:T(8,128)(2,1)}, bf16[256,1024]{1,0:T(8,128)(2,1)}, bf16[256,1024]{1,0:T(8,128)(2,1)}) conditional(s32[]{:T(128)} %convert_element_type.39, () %tuple.117, (bf16[256,1024]{1,0:T(8,128)(2,1)S(1)}, f32[256,1024]{1,0:T(8,128)S(1)}, ...), branch_computations={%region_20.21_spmd, %region_21.22_spmd} | conditional | flops 4194304 | bytes 8913056 | solution.py:761
  222.1 10.9 %collective-permute-done.33 = bf16[256,1024]{1,0:T(8,128)(2,1)} collective-permute-done((bf16[256,1024]{1,0:T(8,128)(2,1)S(1)}, bf16[256,1024]{1,0:T(8,128)(2,1)}, u32[]{:S(2)}, u32[]{:S(2)}) %collective-permute-start.33) | collective-permute-done | bytes 524320 | tf_op jit(solution)/shard_map/cond/branch_1_fun/ppermute | solution.py:731
  235.3 3.7 %weight_partials.3 = (bf16[128,256]{1,0:T(8,128)(2,1)S(1)}, bf16[128,256]{1,0:T(8,128)(2,1)S(1)}, bf16[128,256]{1,0:T(8,128)(2,1)S(1)}, bf16[128,256]{1,0:T(8,128)(2,1)}, bf16[512,256]{1,0:T(8,128)(2,1)}) custom-call(s32[4,8]{1,0:T(4,128)S(1)} %get-tuple-element.690.tables, bf16[256,1024]{1,0:T(8,128)(2,1)S(1)} %get-tuple-element.765.refs_0_, ...), custom_call_target="tpu_custom_call" | custom-call | flops 536870912 | bytes 8388608 | tf_op jit(solution)/shard_map/weight_partials/pallas_call | solution.py:714
  239.0 20.6 %conditional.23 = (bf16[256,1024]{1,0:T(8,128)(2,1)}, bf16[512,256]{1,0:T(8,128)(2,1)}, f32[256,1024]{1,0:T(8,128)}, f32[256,1024]{1,0:T(8,128)}, bf16[256,1024]...) conditional(s32[]{:T(128)} %convert_element_type.39, () %tuple.116, ...), branch_computations={%region_22.23_spmd, %region_23.24_spmd} | conditional | flops 2147483648 | bytes 17825936 | solution.py:761
  242.8 16.9 %attn_bwd.1 = (f32[256,1024]{1,0:T(8,128)}, f32[256,1024]{1,0:T(8,128)}, bf16[256,1024]{1,0:T(8,128)(2,1)}, bf16[256,1024]{1,0:T(8,128)(2,1)}, bf16[1024,768]{1,0:T(8,128)(2,1)}, /*index=5*/f32[4,16,256]{2,1,0:T(8,128)S(1)}) custom-call(s32[4,8]{1,0:T(4,128)S(1)} %get-tuple-element.462.refs_0_, bf16[256,1024]{1,0:T(8,128)(2,1)S(1)} %get-tuple-element.463.refs_1_, ...), custom_call_target="tpu_custom_call" | custom-call | flops 2147483648 | bytes 12582912 | tf_op jit(solution)/shard_map/cond/branch_1_fun/attn_bwd/pallas_call | solution.py:301
  259.8 25.8 %conditional.24 = (bf16[256,1024]{1,0:T(8,128)(2,1)}, bf16[256,1024]{1,0:T(8,128)(2,1)}, bf16[128,768]{1,0:T(8,128)(2,1)S(1)}, bf16[128,768]{1,0:T(8,128)(2,1)S(...) conditional(s32[]{:T(128)} %convert_element_type.39, () %tuple.115, ...), branch_computations={%region_24.25_spmd, %region_25.26_spmd} | conditional | flops 1615331328 | bytes 23069096 | solution.py:761
  259.9 5.4 %weight_partials.2 = (bf16[128,768]{1,0:T(8,128)(2,1)S(1)}, bf16[128,768]{1,0:T(8,128)(2,1)S(1)}, bf16[128,768]{1,0:T(8,128)(2,1)S(1)}, bf16[128,768]{1,0:T(8,128)(2,1)S(1)}, bf16[512,768]{1,0:T(8,128)(2,1)}) custom-call(s32[4,8]{1,0:T(4,128)S(1)} %get-tuple-element.493.tables, bf16[256,1024]{1,0:T(8,128)(2,1)} %get-tuple-element.494.refs_0_, ...), custom_call_target="tpu_custom_call" | custom-call | flops 1610612736 | bytes 8388608 | tf_op jit(solution)/shard_map/cond/branch_1_fun/weight_partials/pallas_call | solution.py:714
  267.8 2.2 rest_rows.9
  279.7 4.0 %collective-permute-done.44 = bf16[128,256]{1,0:T(8,128)(2,1)} collective-permute-done((bf16[128,256]{1,0:T(8,128)(2,1)}, bf16[128,256]{1,0:T(8,128)(2,1)}, u32[]{:S(2)}, u32[]{:S(2)}) %collective-permute-start.44) | collective-permute-done | bytes 65568 | tf_op jit(solution)/shard_map/cond/branch_1_fun/ppermute | solution.py:731
  288.7 3.4 back_one.1
  292.9 36.1 %conditional.25 = (bf16[128,768]{1,0:T(8,128)(2,1)}, bf16[128,768]{1,0:T(8,128)(2,1)}, bf16[128,768]{1,0:T(8,128)(2,1)}, bf16[128,1536]{1,0:T(8,128)(2,1)}, bf16...) conditional(s32[]{:T(128)} %convert_element_type.39, () %tuple.114, ...), branch_computations={%region_30.31_spmd, %region_31.32_spmd} | conditional | flops 4743173 | bytes 14090886 | solution.py:761
  295.7 2.2 collective-permute-done.59
  298.9 2.8 out_rows.1
  313.4 2.3 collective-permute-start.53
  316.3 4.7 %collective-permute-done.52 = bf16[128,768]{1,0:T(8,128)(2,1)} collective-permute-done((bf16[128,768]{1,0:T(8,128)(2,1)}, bf16[128,768]{1,0:T(8,128)(2,1)}, u32[]{:S(2)}, u32[]{:S(2)}) %collective-permute-start.52) | collective-permute-done | bytes 196640 | tf_op jit(solution)/shard_map/cond/branch_1_fun/ppermute | solution.py:731
  325.8 3.1 collective-permute-done.54
  332.1 2.2 layer_out.1
  336.4 2.3 ffn_sums.1
  (312 shorter events, 123.4 us)
Async XLA Ops:
  7.2 126.4 %all-gather.2.cloned.1.call-start = ((), (), s32[]{:S(2)}) async-start(), calls=%async_computation.1 | async-start | bytes 3932160 | tf_op jit(solution)/shard_map/all_gather | solution.py:864
  10.2 17.2 %collective-permute-start.46 = (bf16[128,1024]{1,0:T(8,128)(2,1)S(1)}, bf16[128,1024]{1,0:T(8,128)(2,1)}, u32[]{:S(2)}, u32[]{:S(2)}) collective-permute-start(bf16[128,1024]{1,0:T(8,128)(2,1)S(1)} %get-tuple-element.328), channel_id=1, source_target_pairs={{0,8},{8,0},{16,24},{24,16},{1,9},{9,1},{17,25},{25,17},{2,10},{10... | collective-permute-start | bytes 786440 | tf_op jit(solution)/shard_map/cond/branch_1_fun/ppermute | solution.py:731
  13.3 16.1 %collective-permute-start.47 = (bf16[128,1024]{1,0:T(8,128)(2,1)S(1)}, bf16[128,1024]{1,0:T(8,128)(2,1)}, u32[]{:S(2)}, u32[]{:S(2)}) collective-permute-start(bf16[128,1024]{1,0:T(8,128)(2,1)S(1)} %get-tuple-element.328), channel_id=1, source_target_pairs={{0,16},{8,24},{16,0},{24,8},{1,17},{9,25},{17,1},{25,9},{2,18},{10... | collective-permute-start | bytes 786440 | tf_op jit(solution)/shard_map/cond/branch_1_fun/ppermute | solution.py:731
  16.8 10.2 %collective-permute-start.45 = (bf16[128,1024]{1,0:T(8,128)(2,1)S(1)}, bf16[128,1024]{1,0:T(8,128)(2,1)}, u32[]{:S(2)}, u32[]{:S(2)}) collective-permute-start(bf16[128,1024]{1,0:T(8,128)(2,1)S(1)} %dynamic-slice_bitcast_fusion), channel_id=1, source_target_pairs={{0,4},{4,0},{1,5},{5,1},{2,6},{6,2},{3,7},{7,3},{8,12},{12,8},{9,1... | collective-permute-start | bytes 786440 | tf_op jit(solution)/shard_map/cond/branch_1_fun/ppermute | solution.py:731
  18.4 20.2 %collective-permute-start.51 = (bf16[2,128,1024]{2,1,0:T(8,128)(2,1)}, bf16[2,128,1024]{2,1,0:T(8,128)(2,1)}, u32[]{:S(2)}, u32[]{:S(2)}) collective-permute-start(bf16[2,128,1024]{2,1,0:T(8,128)(2,1)} %get-tuple-element.330), channel_id=1, source_target_pairs={{0,2},{1,3},{2,0},{3,1},{4,6},{5,7},{6,4},{7,5},{8,10},{9,11},{10,... | collective-permute-start | bytes 1572872 | tf_op jit(solution)/shard_map/cond/branch_1_fun/ppermute | solution.py:731
  19.9 18.6 %collective-permute-start.50 = (bf16[128,1536]{1,0:T(8,128)(2,1)S(1)}, bf16[128,1536]{1,0:T(8,128)(2,1)}, u32[]{:S(2)}, u32[]{:S(2)}) collective-permute-start(bf16[128,1536]{1,0:T(8,128)(2,1)S(1)} %get-tuple-element.329), channel_id=1, source_target_pairs={{0,4},{4,0},{1,5},{5,1},{2,6},{6,2},{3,7},{7,3},{8,12},{12,8},{9,1... | collective-permute-start | bytes 1179656 | tf_op jit(solution)/shard_map/cond/branch_1_fun/ppermute | solution.py:731
  27.0 8.7 %collective-permute-start.48 = (bf16[128,1024]{1,0:T(8,128)(2,1)S(1)}, bf16[128,1024]{1,0:T(8,128)(2,1)}, u32[]{:S(2)}, u32[]{:S(2)}) collective-permute-start(bf16[128,1024]{1,0:T(8,128)(2,1)S(1)} %get-tuple-element.328), channel_id=1, source_target_pairs={{0,24},{8,16},{16,8},{24,0},{1,25},{9,17},{17,9},{25,1},{2,26},{10... | collective-permute-start | bytes 786440 | tf_op jit(solution)/shard_map/cond/branch_1_fun/ppermute | solution.py:731
  27.3 11.2 %collective-permute-start.49 = (bf16[128,1024]{1,0:T(8,128)(2,1)S(1)}, bf16[128,1024]{1,0:T(8,128)(2,1)}, u32[]{:S(2)}, u32[]{:S(2)}) collective-permute-start(bf16[128,1024]{1,0:T(8,128)(2,1)S(1)} %get-tuple-element.328), channel_id=1, source_target_pairs={{0,4},{4,0},{1,5},{5,1},{2,6},{6,2},{3,7},{7,3},{8,12},{12,8},{9,1... | collective-permute-start | bytes 786440 | tf_op jit(solution)/shard_map/cond/branch_1_fun/ppermute | solution.py:731
  41.6 251.2 %reduce-scatter.2.cloned.1.call-start = ((), (), s32[]{:S(2)}) async-start(), calls=%async_computation.2 | async-start | bytes 3932160 | tf_op jit(solution)/shard_map/reduce_scatter | solution.py:926
  44.3 12.5 %collective-permute-start = (bf16[256,1024]{1,0:T(8,128)(2,1)}, bf16[256,1024]{1,0:T(8,128)(2,1)}, u32[]{:S(2)}, u32[]{:S(2)}) collective-permute-start(bf16[256,1024]{1,0:T(8,128)(2,1)} %norm_rows.1), channel_id=1, source_target_pairs={{0,2},{1,3},{2,0},{3,1},{4,6},{5,7},{6,4},{7,5},{8,10},{9,11},{10,... | collective-permute-start | bytes 1572872 | tf_op jit(solution)/shard_map/cond/branch_1_fun/ppermute | solution.py:731
  45.8 31.2 %collective-permute-start.1 = (bf16[256,1024]{1,0:T(8,128)(2,1)}, bf16[256,1024]{1,0:T(8,128)(2,1)}, u32[]{:S(2)}, u32[]{:S(2)}) collective-permute-start(bf16[256,1024]{1,0:T(8,128)(2,1)} %norm_rows.1), channel_id=1, source_target_pairs={{0,1},{1,0},{2,3},{3,2},{4,5},{5,4},{6,7},{7,6},{8,9},{9,8},{10,11... | collective-permute-start | bytes 1572872 | tf_op jit(solution)/shard_map/cond/branch_1_fun/ppermute | solution.py:731
  56.8 20.3 %collective-permute-start.2 = (bf16[256,1024]{1,0:T(8,128)(2,1)}, bf16[256,1024]{1,0:T(8,128)(2,1)}, u32[]{:S(2)}, u32[]{:S(2)}) collective-permute-start(bf16[256,1024]{1,0:T(8,128)(2,1)} %collective-permute-done), channel_id=1, source_target_pairs={{0,1},{1,0},{2,3},{3,2},{4,5},{5,4},{6,7},{7,6},{8,9},{9,8},{10,11... | collective-permute-start | bytes 1572872 | tf_op jit(solution)/shard_map/cond/branch_1_fun/ppermute | solution.py:731
  56.8 9.4 %collective-permute-start.3 = (bf16[128,1024]{1,0:T(8,128)(2,1)}, bf16[128,1024]{1,0:T(8,128)(2,1)}, u32[]{:S(2)}, u32[]{:S(2)}) collective-permute-start(bf16[128,1024]{1,0:T(8,128)(2,1)} %get-tuple-element.340), channel_id=1, source_target_pairs={{0,4},{4,0},{1,5},{5,1},{2,6},{6,2},{3,7},{7,3},{8,12},{12,8},{9,1... | collective-permute-start | bytes 786440 | tf_op jit(solution)/shard_map/cond/branch_1_fun/ppermute | solution.py:731
  58.3 13.6 %collective-permute-start.4 = (bf16[128,1024]{1,0:T(8,128)(2,1)}, bf16[128,1024]{1,0:T(8,128)(2,1)}, u32[]{:S(2)}, u32[]{:S(2)}) collective-permute-start(bf16[128,1024]{1,0:T(8,128)(2,1)} %get-tuple-element.341), channel_id=1, source_target_pairs={{0,4},{4,0},{1,5},{5,1},{2,6},{6,2},{3,7},{7,3},{8,12},{12,8},{9,1... | collective-permute-start | bytes 786440 | tf_op jit(solution)/shard_map/cond/branch_1_fun/ppermute | solution.py:731
  58.8 18.2 %collective-permute-start.5 = (bf16[128,1024]{1,0:T(8,128)(2,1)}, bf16[128,1024]{1,0:T(8,128)(2,1)}, u32[]{:S(2)}, u32[]{:S(2)}) collective-permute-start(bf16[128,1024]{1,0:T(8,128)(2,1)} %get-tuple-element.342), channel_id=1, source_target_pairs={{0,4},{4,0},{1,5},{5,1},{2,6},{6,2},{3,7},{7,3},{8,12},{12,8},{9,1... | collective-permute-start | bytes 786440 | tf_op jit(solution)/shard_map/cond/branch_1_fun/ppermute | solution.py:731
  77.2 16.4 %collective-permute-start.6 = (bf16[2,128,1024]{2,1,0:T(8,128)(2,1)}, bf16[2,128,1024]{2,1,0:T(8,128)(2,1)}, u32[]{:S(2)}, u32[]{:S(2)}) collective-permute-start(bf16[2,128,1024]{2,1,0:T(8,128)(2,1)} %get-tuple-element.343), channel_id=1, source_target_pairs={{0,4},{4,0},{1,5},{5,1},{2,6},{6,2},{3,7},{7,3},{8,12},{12,8},{9,1... | collective-permute-start | bytes 1572872 | tf_op jit(solution)/shard_map/cond/branch_1_fun/ppermute | solution.py:731
  93.7 14.7 %collective-permute-start.10 = (bf16[2,128,1024]{2,1,0:T(8,128)(2,1)}, bf16[2,128,1024]{2,1,0:T(8,128)(2,1)}, u32[]{:S(2)}, u32[]{:S(2)}) collective-permute-start(bf16[2,128,1024]{2,1,0:T(8,128)(2,1)} %get-tuple-element.375), channel_id=1, source_target_pairs={{0,4},{4,0},{1,5},{5,1},{2,6},{6,2},{3,7},{7,3},{8,12},{12,8},{9,1... | collective-permute-start | bytes 1572872 | tf_op jit(solution)/shard_map/cond/branch_1_fun/ppermute | solution.py:731
  94.3 14.0 %collective-permute-start.9 = (bf16[256,1024]{1,0:T(8,128)(2,1)}, bf16[256,1024]{1,0:T(8,128)(2,1)}, u32[]{:S(2)}, u32[]{:S(2)}) collective-permute-start(bf16[256,1024]{1,0:T(8,128)(2,1)} %get-tuple-element.374), channel_id=1, source_target_pairs={{0,1},{1,0},{2,3},{3,2},{4,5},{5,4},{6,7},{7,6},{8,9},{9,8},{10,11... | collective-permute-start | bytes 1572872 | tf_op jit(solution)/shard_map/cond/branch_1_fun/ppermute | solution.py:731
  98.9 14.3 %collective-permute-start.8 = (bf16[256,1024]{1,0:T(8,128)(2,1)}, bf16[256,1024]{1,0:T(8,128)(2,1)}, u32[]{:S(2)}, u32[]{:S(2)}) collective-permute-start(bf16[256,1024]{1,0:T(8,128)(2,1)} %rest_rows.6), channel_id=1, source_target_pairs={{0,2},{1,3},{2,0},{3,1},{4,6},{5,7},{6,4},{7,5},{8,10},{9,11},{10,... | collective-permute-start | bytes 1572872 | tf_op jit(solution)/shard_map/cond/branch_1_fun/ppermute | solution.py:731
  115.8 13.2 %collective-permute-start.11 = (bf16[256,1024]{1,0:T(8,128)(2,1)S(1)}, bf16[256,1024]{1,0:T(8,128)(2,1)}, u32[]{:S(2)}, u32[]{:S(2)}) collective-permute-start(bf16[256,1024]{1,0:T(8,128)(2,1)S(1)} %get-tuple-element.1036), channel_id=1, source_target_pairs={{0,2},{1,3},{2,0},{3,1},{4,6},{5,7},{6,4},{7,5},{8,10},{9,11},{10,... | collective-permute-start | bytes 1572872 | tf_op jit(solution)/shard_map/cond/branch_1_fun/ppermute | solution.py:731
  117.3 13.0 %collective-permute-start.12 = (bf16[256,1024]{1,0:T(8,128)(2,1)S(1)}, bf16[256,1024]{1,0:T(8,128)(2,1)}, u32[]{:S(2)}, u32[]{:S(2)}) collective-permute-start(bf16[256,1024]{1,0:T(8,128)(2,1)S(1)} %get-tuple-element.1036), channel_id=1, source_target_pairs={{0,4},{4,0},{1,5},{5,1},{2,6},{6,2},{3,7},{7,3},{8,12},{12,8},{9,1... | collective-permute-start | bytes 1572872 | tf_op jit(solution)/shard_map/cond/branch_1_fun/ppermute | solution.py:731
  117.9 15.6 %collective-permute-start.17 = (bf16[256,1024]{1,0:T(8,128)(2,1)S(1)}, bf16[256,1024]{1,0:T(8,128)(2,1)}, u32[]{:S(2)}, u32[]{:S(2)}) collective-permute-start(bf16[256,1024]{1,0:T(8,128)(2,1)S(1)} %get-tuple-element.1036), channel_id=1, source_target_pairs={{0,1},{1,0},{2,3},{3,2},{4,5},{5,4},{6,7},{7,6},{8,9},{9,8},{10,11... | collective-permute-start | bytes 1572872 | tf_op jit(solution)/shard_map/cond/branch_1_fun/ppermute | solution.py:731
  117.9 15.6 %collective-permute-start.13 = (bf16[2,128,1024]{2,1,0:T(8,128)(2,1)S(1)}, bf16[2,128,1024]{2,1,0:T(8,128)(2,1)}, u32[]{:S(2)}, u32[]{:S(2)}) collective-permute-start(bf16[2,128,1024]{2,1,0:T(8,128)(2,1)S(1)} %get-tuple-element.1039), channel_id=1, source_target_pairs={{0,1},{1,0},{2,3},{3,2},{4,5},{5,4},{6,7},{7,6},{8,9},{9,8},{10,11... | collective-permute-start | bytes 1572872 | tf_op jit(solution)/shard_map/cond/branch_1_fun/ppermute | solution.py:731
  118.4 15.1 %collective-permute-start.14 = (bf16[2,128,1024]{2,1,0:T(8,128)(2,1)}, bf16[2,128,1024]{2,1,0:T(8,128)(2,1)}, u32[]{:S(2)}, u32[]{:S(2)}) collective-permute-start(bf16[2,128,1024]{2,1,0:T(8,128)(2,1)} %get-tuple-element.1040), channel_id=1, source_target_pairs={{0,1},{1,0},{2,3},{3,2},{4,5},{5,4},{6,7},{7,6},{8,9},{9,8},{10,11... | collective-permute-start | bytes 1572872 | tf_op jit(solution)/shard_map/cond/branch_1_fun/ppermute | solution.py:731
  134.8 14.7 %collective-permute-start.18 = (bf16[256,1024]{1,0:T(8,128)(2,1)}, bf16[256,1024]{1,0:T(8,128)(2,1)}, u32[]{:S(2)}, u32[]{:S(2)}) collective-permute-start(bf16[256,1024]{1,0:T(8,128)(2,1)} %get-tuple-element.1061.refs_2_), channel_id=1, source_target_pairs={{0,4},{4,0},{1,5},{5,1},{2,6},{6,2},{3,7},{7,3},{8,12},{12,8},{9,1... | collective-permute-start | bytes 1572872 | tf_op jit(solution)/shard_map/cond/branch_1_fun/ppermute | solution.py:731
  150.7 7.3 %collective-permute-start.23 = (bf16[256,1024]{1,0:T(8,128)(2,1)}, bf16[256,1024]{1,0:T(8,128)(2,1)}, u32[]{:S(2)}, u32[]{:S(2)}) collective-permute-start(bf16[256,1024]{1,0:T(8,128)(2,1)} %get-tuple-element.1084.refs_1_), channel_id=1, source_target_pairs={{0,1},{1,0},{2,3},{3,2},{4,5},{5,4},{6,7},{7,6},{8,9},{9,8},{10,11... | collective-permute-start | bytes 1572872 | tf_op jit(solution)/shard_map/cond/branch_1_fun/ppermute | solution.py:731
  151.3 17.9 %collective-permute-start.22 = (bf16[256,1024]{1,0:T(8,128)(2,1)}, bf16[256,1024]{1,0:T(8,128)(2,1)}, u32[]{:S(2)}, u32[]{:S(2)}) collective-permute-start(bf16[256,1024]{1,0:T(8,128)(2,1)} %get-tuple-element.402), channel_id=1, source_target_pairs={{0,1},{1,0},{2,3},{3,2},{4,5},{5,4},{6,7},{7,6},{8,9},{9,8},{10,11... | collective-permute-start | bytes 1572872 | tf_op jit(solution)/shard_map/cond/branch_1_fun/ppermute | solution.py:731
  155.4 14.3 %collective-permute-start.21 = (bf16[256,1024]{1,0:T(8,128)(2,1)}, bf16[256,1024]{1,0:T(8,128)(2,1)}, u32[]{:S(2)}, u32[]{:S(2)}) collective-permute-start(bf16[256,1024]{1,0:T(8,128)(2,1)} %rest_rows.7), channel_id=1, source_target_pairs={{0,2},{1,3},{2,0},{3,1},{4,6},{5,7},{6,4},{7,5},{8,10},{9,11},{10,... | collective-permute-start | bytes 1572872 | tf_op jit(solution)/shard_map/cond/branch_1_fun/ppermute | solution.py:731
  180.4 14.1 %collective-permute-start.25 = (bf16[256,1024]{1,0:T(8,128)(2,1)S(1)}, bf16[256,1024]{1,0:T(8,128)(2,1)}, u32[]{:S(2)}, u32[]{:S(2)}) collective-permute-start(bf16[256,1024]{1,0:T(8,128)(2,1)S(1)} %get-tuple-element.421), channel_id=1, source_target_pairs={{0,2},{1,3},{2,0},{3,1},{4,6},{5,7},{6,4},{7,5},{8,10},{9,11},{10,... | collective-permute-start | bytes 1572872 | tf_op jit(solution)/shard_map/cond/branch_1_fun/ppermute | solution.py:731
  181.6 12.8 %collective-permute-start.26 = (bf16[256,1024]{1,0:T(8,128)(2,1)S(1)}, bf16[256,1024]{1,0:T(8,128)(2,1)}, u32[]{:S(2)}, u32[]{:S(2)}) collective-permute-start(bf16[256,1024]{1,0:T(8,128)(2,1)S(1)} %get-tuple-element.422), channel_id=1, source_target_pairs={{0,1},{1,0},{2,3},{3,2},{4,5},{5,4},{6,7},{7,6},{8,9},{9,8},{10,11... | collective-permute-start | bytes 1572872 | tf_op jit(solution)/shard_map/cond/branch_1_fun/ppermute | solution.py:731
  198.7 13.7 %collective-permute-start.31 = (bf16[256,1024]{1,0:T(8,128)(2,1)}, bf16[256,1024]{1,0:T(8,128)(2,1)}, u32[]{:S(2)}, u32[]{:S(2)}) collective-permute-start(bf16[256,1024]{1,0:T(8,128)(2,1)} %get-tuple-element.434), channel_id=1, source_target_pairs={{0,4},{4,0},{1,5},{5,1},{2,6},{6,2},{3,7},{7,3},{8,12},{12,8},{9,1... | collective-permute-start | bytes 1572872 | tf_op jit(solution)/shard_map/cond/branch_1_fun/ppermute | solution.py:731
  200.2 13.2 %collective-permute-start.32 = (bf16[256,1024]{1,0:T(8,128)(2,1)}, bf16[256,1024]{1,0:T(8,128)(2,1)}, u32[]{:S(2)}, u32[]{:S(2)}) collective-permute-start(bf16[256,1024]{1,0:T(8,128)(2,1)} %get-tuple-element.435), channel_id=1, source_target_pairs={{0,2},{1,3},{2,0},{3,1},{4,6},{5,7},{6,4},{7,5},{8,10},{9,11},{10,... | collective-permute-start | bytes 1572872 | tf_op jit(solution)/shard_map/cond/branch_1_fun/ppermute | solution.py:731
  221.0 12.0 %collective-permute-start.33 = (bf16[256,1024]{1,0:T(8,128)(2,1)S(1)}, bf16[256,1024]{1,0:T(8,128)(2,1)}, u32[]{:S(2)}, u32[]{:S(2)}) collective-permute-start(bf16[256,1024]{1,0:T(8,128)(2,1)S(1)} %get-tuple-element.1125), channel_id=1, source_target_pairs={{0,2},{1,3},{2,0},{3,1},{4,6},{5,7},{6,4},{7,5},{8,10},{9,11},{10,... | collective-permute-start | bytes 1572872 | tf_op jit(solution)/shard_map/cond/branch_1_fun/ppermute | solution.py:731
  222.1 12.9 %collective-permute-start.34 = (bf16[256,1024]{1,0:T(8,128)(2,1)S(1)}, bf16[256,1024]{1,0:T(8,128)(2,1)}, u32[]{:S(2)}, u32[]{:S(2)}) collective-permute-start(bf16[256,1024]{1,0:T(8,128)(2,1)S(1)} %get-tuple-element.1125), channel_id=1, source_target_pairs={{0,1},{1,0},{2,3},{3,2},{4,5},{5,4},{6,7},{7,6},{8,9},{9,8},{10,11... | collective-permute-start | bytes 1572872 | tf_op jit(solution)/shard_map/cond/branch_1_fun/ppermute | solution.py:731
  239.0 20.6 %collective-permute-start.36 = (bf16[256,1024]{1,0:T(8,128)(2,1)}, bf16[256,1024]{1,0:T(8,128)(2,1)}, u32[]{:S(2)}, u32[]{:S(2)}) collective-permute-start(bf16[256,1024]{1,0:T(8,128)(2,1)} %get-tuple-element.460), channel_id=1, source_target_pairs={{0,2},{1,3},{2,0},{3,1},{4,6},{5,7},{6,4},{7,5},{8,10},{9,11},{10,... | collective-permute-start | bytes 1572872 | tf_op jit(solution)/shard_map/cond/branch_1_fun/ppermute | solution.py:731
  240.2 19.5 %collective-permute-start.37 = (bf16[512,256]{1,0:T(8,128)(2,1)}, bf16[512,256]{1,0:T(8,128)(2,1)}, u32[]{:S(2)}, u32[]{:S(2)}) collective-permute-start(bf16[512,256]{1,0:T(8,128)(2,1)} %get-tuple-element.461), channel_id=1, source_target_pairs={{0,4},{4,0},{1,5},{5,1},{2,6},{6,2},{3,7},{7,3},{8,12},{12,8},{9,1... | collective-permute-start | bytes 786440 | tf_op jit(solution)/shard_map/cond/branch_1_fun/ppermute | solution.py:731
  259.8 7.3 %collective-permute-start.38 = (bf16[256,1024]{1,0:T(8,128)(2,1)}, bf16[256,1024]{1,0:T(8,128)(2,1)S(1)}, u32[]{:S(2)}, u32[]{:S(2)}) collective-permute-start(bf16[256,1024]{1,0:T(8,128)(2,1)} %get-tuple-element.491), channel_id=1, source_target_pairs={{0,1},{1,0},{2,3},{3,2},{4,5},{5,4},{6,7},{7,6},{8,9},{9,8},{10,11... | collective-permute-start | bytes 1572872 | tf_op jit(solution)/shard_map/cond/branch_1_fun/ppermute | solution.py:731
  265.2 20.3 %collective-permute-start.41 = (bf16[512,768]{1,0:T(8,128)(2,1)}, bf16[512,768]{1,0:T(8,128)(2,1)}, u32[]{:S(2)}, u32[]{:S(2)}) collective-permute-start(bf16[512,768]{1,0:T(8,128)(2,1)} %get-tuple-element.503), channel_id=1, source_target_pairs={{0,4},{4,0},{1,5},{5,1},{2,6},{6,2},{3,7},{7,3},{8,12},{12,8},{9,1... | collective-permute-start | bytes 2359304 | tf_op jit(solution)/shard_map/cond/branch_1_fun/ppermute | solution.py:731
  266.8 16.9 %collective-permute-start.40 = (bf16[256,1024]{1,0:T(8,128)(2,1)}, bf16[256,1024]{1,0:T(8,128)(2,1)}, u32[]{:S(2)}, u32[]{:S(2)}) collective-permute-start(bf16[256,1024]{1,0:T(8,128)(2,1)} %get-tuple-element.492), channel_id=1, source_target_pairs={{0,1},{1,0},{2,3},{3,2},{4,5},{5,4},{6,7},{7,6},{8,9},{9,8},{10,11... | collective-permute-start | bytes 1572872 | tf_op jit(solution)/shard_map/cond/branch_1_fun/ppermute | solution.py:731
  270.1 15.5 %collective-permute-start.39 = (bf16[256,1024]{1,0:T(8,128)(2,1)}, bf16[256,1024]{1,0:T(8,128)(2,1)}, u32[]{:S(2)}, u32[]{:S(2)}) collective-permute-start(bf16[256,1024]{1,0:T(8,128)(2,1)} %rest_rows.9), channel_id=1, source_target_pairs={{0,2},{1,3},{2,0},{3,1},{4,6},{5,7},{6,4},{7,5},{8,10},{9,11},{10,... | collective-permute-start | bytes 1572872 | tf_op jit(solution)/shard_map/cond/branch_1_fun/ppermute | solution.py:731
  301.7 27.2 %collective-permute-start.57 = (bf16[2,128,1024]{2,1,0:T(8,128)(2,1)}, bf16[2,128,1024]{2,1,0:T(8,128)(2,1)}, u32[]{:S(2)}, u32[]{:S(2)}) collective-permute-start(bf16[2,128,1024]{2,1,0:T(8,128)(2,1)} %get-tuple-element.527), channel_id=1, source_target_pairs={{0,4},{4,0},{1,5},{5,1},{2,6},{6,2},{3,7},{7,3},{8,12},{12,8},{9,1... | collective-permute-start | bytes 1572872 | tf_op jit(solution)/shard_map/cond/branch_1_fun/ppermute | solution.py:731
  304.0 7.5 %collective-permute-start.61 = (f32[4,1024]{1,0:T(4,128)S(1)}, f32[4,1024]{1,0:T(4,128)S(1)}, u32[]{:S(2)}, u32[]{:S(2)}) collective-permute-start(f32[4,1024]{1,0:T(4,128)S(1)} %add.107), channel_id=1, source_target_pairs={{0,8},{8,0},{16,24},{24,16},{1,9},{9,1},{17,25},{25,17},{2,10},{10... | collective-permute-start | bytes 49160 | tf_op jit(solution)/shard_map/cond/branch_1_fun/ppermute | solution.py:731
  305.2 8.0 %collective-permute-start.62 = (f32[4,1024]{1,0:T(4,128)S(1)}, f32[4,1024]{1,0:T(4,128)S(1)}, u32[]{:S(2)}, u32[]{:S(2)}) collective-permute-start(f32[4,1024]{1,0:T(4,128)S(1)} %add.107), channel_id=1, source_target_pairs={{0,16},{8,24},{16,0},{24,8},{1,17},{9,25},{17,1},{25,9},{2,18},{10... | collective-permute-start | bytes 49160 | tf_op jit(solution)/shard_map/cond/branch_1_fun/ppermute | solution.py:731
  309.4 19.5 %collective-permute-start.55 = (bf16[128,1536]{1,0:T(8,128)(2,1)S(1)}, bf16[128,1536]{1,0:T(8,128)(2,1)}, u32[]{:S(2)}, u32[]{:S(2)}) collective-permute-start(bf16[128,1536]{1,0:T(8,128)(2,1)S(1)} %constant_dynamic-slice_fusion), channel_id=1, source_target_pairs={{0,4},{4,0},{1,5},{5,1},{2,6},{6,2},{3,7},{7,3},{8,12},{12,8},{9,1... | collective-permute-start | bytes 1179656 | tf_op jit(solution)/shard_map/cond/branch_1_fun/ppermute | solution.py:731
  311.5 17.4 %collective-permute-start.56 = (bf16[128,1024]{1,0:T(8,128)(2,1)}, bf16[128,1024]{1,0:T(8,128)(2,1)}, u32[]{:S(2)}, u32[]{:S(2)}) collective-permute-start(bf16[128,1024]{1,0:T(8,128)(2,1)} %get-tuple-element.518), channel_id=1, source_target_pairs={{0,4},{4,0},{1,5},{5,1},{2,6},{6,2},{3,7},{7,3},{8,12},{12,8},{9,1... | collective-permute-start | bytes 786440 | tf_op jit(solution)/shard_map/cond/branch_1_fun/ppermute | solution.py:731
  313.1 7.9 %collective-permute-start.52 = (bf16[128,768]{1,0:T(8,128)(2,1)}, bf16[128,768]{1,0:T(8,128)(2,1)}, u32[]{:S(2)}, u32[]{:S(2)}) collective-permute-start(bf16[128,768]{1,0:T(8,128)(2,1)} %get-tuple-element.513), channel_id=1, source_target_pairs={{0,8},{8,0},{16,24},{24,16},{1,9},{9,1},{17,25},{25,17},{2,10},{10... | collective-permute-start | bytes 589832 | tf_op jit(solution)/shard_map/cond/branch_1_fun/ppermute | solution.py:731
  313.4 12.4 %collective-permute-start.53 = (bf16[128,768]{1,0:T(8,128)(2,1)}, bf16[128,768]{1,0:T(8,128)(2,1)}, u32[]{:S(2)}, u32[]{:S(2)}) collective-permute-start(bf16[128,768]{1,0:T(8,128)(2,1)} %get-tuple-element.514), channel_id=1, source_target_pairs={{0,16},{8,24},{16,0},{24,8},{1,17},{9,25},{17,1},{25,9},{2,18},{10... | collective-permute-start | bytes 589832 | tf_op jit(solution)/shard_map/cond/branch_1_fun/ppermute | solution.py:731
  321.0 7.9 %collective-permute-start.54 = (bf16[128,768]{1,0:T(8,128)(2,1)}, bf16[128,768]{1,0:T(8,128)(2,1)}, u32[]{:S(2)}, u32[]{:S(2)}) collective-permute-start(bf16[128,768]{1,0:T(8,128)(2,1)} %get-tuple-element.515), channel_id=1, source_target_pairs={{0,24},{8,16},{16,8},{24,0},{1,25},{9,17},{17,9},{25,1},{2,26},{10... | collective-permute-start | bytes 589832 | tf_op jit(solution)/shard_map/cond/branch_1_fun/ppermute | solution.py:731
  (70 other events, 481.2 us)
Sparse Core Ops, SparseCore 0:
  41.8 63.1 all-gather.1
  215.3 59.1 reduce-scatter.1
